TPU v7x, 32 devices: a whole 2x2x4 slice. The times are simulated.
32 devices in a mesh: dp: 4 (over x, core), ctx: 8 (over z, y).
Axes of the slice: x: 2, y: 2, z: 4, core: 2. Of those that a mesh axis runs over, the one named last changes fastest.
Arguments:
- hidden_in: bfloat16 [8192, 1024], P(('dp', 'ctx')), may hold values from -6 to 6
- segment_ids: int32 [4, 1, 2048], P('dp'), may hold values from 0 to 15, as said below
- query_weight: float32 [2, 1024, 1024], P(None, 'ctx'), may hold values from -0.1875 to 0.1875
- query_bias: float32 [2, 1024], P(None, 'ctx'), may hold values from -3 to 3
- key_weight: float32 [2, 1024, 1024], P(None, 'ctx'), may hold values from -0.1875 to 0.1875
- value_weight: float32 [2, 1024, 1024], P(None, 'ctx'), may hold values from -0.1875 to 0.1875
- value_bias: float32 [2, 1024], P(None, 'ctx'), may hold values from -3 to 3
- output_weight: float32 [2, 1024, 1024], P(None, 'ctx'), may hold values from -0.5 to 0.5
- output_bias: float32 [2, 1024], P(None, 'ctx'), may hold values from -3 to 3
- first_gain: float32 [2, 1024], P(None, 'ctx'), may hold values from 0.5 to 1.5
- first_shift: float32 [2, 1024], P(None, 'ctx'), may hold values from -2 to 2
- inner_weight: float32 [2, 1024, 4096], P(None, 'ctx'), may hold values from -0.1875 to 0.1875
- inner_bias: float32 [2, 4096], P(None, 'ctx'), may hold values from -3 to 3
- outer_weight: float32 [2, 4096, 1024], P(None, 'ctx'), may hold values from -0.09375 to 0.09375
- outer_bias: float32 [2, 1024], P(None, 'ctx'), may hold values from -2 to 2
- second_gain: float32 [2, 1024], P(None, 'ctx'), may hold values from 0.5 to 1.5
- second_shift: float32 [2, 1024], P(None, 'ctx'), may hold values from -2 to 2
- cotangent: bfloat16 [8192, 1024], P(('dp', 'ctx')), may hold values from -6 to 6
Outputs:
- output: bfloat16 [8192, 1024], P(('dp', 'ctx'))
- input_gradient: bfloat16 [8192, 1024], P(('dp', 'ctx'))
- query_weight_gradient: float32 [2, 1024, 1024], P(None, 'ctx')
- query_bias_gradient: float32 [2, 1024], P(None, 'ctx')
- key_weight_gradient: float32 [2, 1024, 1024], P(None, 'ctx')
- value_weight_gradient: float32 [2, 1024, 1024], P(None, 'ctx')
- value_bias_gradient: float32 [2, 1024], P(None, 'ctx')
- output_weight_gradient: float32 [2, 1024, 1024], P(None, 'ctx')
- output_bias_gradient: float32 [2, 1024], P(None, 'ctx')
- first_gain_gradient: float32 [2, 1024], P(None, 'ctx')
- first_shift_gradient: float32 [2, 1024], P(None, 'ctx')
- inner_weight_gradient: float32 [2, 1024, 4096], P(None, 'ctx')
- inner_bias_gradient: float32 [2, 4096], P(None, 'ctx')
- outer_weight_gradient: float32 [2, 4096, 1024], P(None, 'ctx')
- outer_bias_gradient: float32 [2, 1024], P(None, 'ctx')
- second_gain_gradient: float32 [2, 1024], P(None, 'ctx')
- second_shift_gradient: float32 [2, 1024], P(None, 'ctx')
Inputs may be any that keep to these rules, and one draw needn't show every extreme that they name: `segment_ids`: within each sequence of 2048 tokens (a row of the last dimension) the numbers never fall, every number 0 .. 15 is used, and each document has 1 to 512 tokens, one exactly 512.
All inputs are finite; a program needn't handle non-finite values.
Results may differ from a plain program's by a relative error of at most 0.025.
Values may be sent and summed in bfloat16 or wider, within the bound.
No kernel may reach another device: no remote copies, remote signals or barrier semaphores. Data moves between devices by JAX's collectives and lax.ppermute only.
A program may use at most 256 MiB of HBM per device.

v0:
```python
import jax
import jax.numpy as jnp
from jax import lax
from jax.sharding import PartitionSpec as P

HD = 64
LAYERS = 2
SEQ = 2048
REACH = 2
WIN = 1280


heads_paired = 2


def from_behind(shard, axis, by):
    peers = lax.axis_size(axis)
    pairs = [(i, i + by) for i in range(peers) if 0 <= i + by < peers]
    return lax.ppermute(shard, axis, pairs)


def normalize(operand, norm_gain, norm_shift):
    centered = operand - jnp.mean(operand, axis=-1, keepdims=True)
    spread = jnp.mean(centered * centered, axis=-1, keepdims=True)
    return centered * lax.rsqrt(spread + 1e-05) * norm_gain + norm_shift


def gelu_exact(operand):
    return jax.nn.gelu(operand, approximate=False)


def project(left, right):
    return jnp.dot(left, right, preferred_element_type=jnp.float32)


def contract_rows(left, right):
    return lax.dot_general(
        left, right, (((0,), (0,)), ((), ())), preferred_element_type=jnp.float32
    )


def against(left, right):
    return lax.dot_general(
        left, right, (((1,), (1,)), ((), ())), preferred_element_type=jnp.float32
    )


def column_sums(operand):
    return jnp.sum(operand.astype(jnp.float32), axis=0)


def keep_order(operand):
    return operand


def document_mask(segment_ids, tokens):
    group_ids = segment_ids.reshape(-1)
    device_place = lax.axis_index("ctx") * tokens
    margin_rows = REACH * tokens
    padded = jnp.pad(group_ids, (margin_rows, margin_rows), constant_values=-1)
    key_ids = lax.dynamic_slice_in_dim(padded, device_place, WIN)
    query_ids = lax.dynamic_slice_in_dim(group_ids, device_place, tokens)
    key_places = device_place - margin_rows + jnp.arange(WIN, dtype=jnp.int32)
    query_places = device_place + jnp.arange(tokens, dtype=jnp.int32)
    same_sequence = query_places[:, None] // SEQ == key_places[None, :] // SEQ
    same_segment = query_ids[:, None] == key_ids[None, :]
    return same_sequence & same_segment & (key_ids[None, :] >= 0)


def widen_window(key_rows, value_rows):
    key_blocks = []
    value_blocks = []
    for block_index in range(2 * REACH + 1):
        offset = REACH - block_index
        if offset == 0:
            key_blocks.append(key_rows)
            value_blocks.append(value_rows)
        else:
            arrived = from_behind((key_rows, value_rows), "ctx", offset)
            key_blocks.append(arrived[0])
            value_blocks.append(arrived[1])
    return (jnp.concatenate(key_blocks, axis=0), jnp.concatenate(value_blocks, axis=0))


def give_back(key_partial, value_partial, tokens):
    key_total = key_partial[REACH * tokens : (REACH + 1) * tokens]
    value_total = value_partial[REACH * tokens : (REACH + 1) * tokens]
    for block_index in range(2 * REACH + 1):
        offset = REACH - block_index
        if offset != 0:
            row_start = block_index * tokens
            received = (
                from_behind(
                    key_partial[row_start : row_start + tokens].astype(jnp.bfloat16), "ctx", -offset
                ).astype(jnp.float32),
                from_behind(
                    value_partial[row_start : row_start + tokens].astype(jnp.bfloat16),
                    "ctx",
                    -offset,
                ).astype(jnp.float32),
            )
            key_total = key_total + received[0]
            value_total = value_total + received[1]
    return (key_total, value_total)


def pair_slices(queries, window_keys, window_values, pair_index):
    tokens = queries.shape[0]
    pair_lanes = heads_paired * HD
    column_start = pair_index * pair_lanes
    query_pair = lax.dynamic_slice_in_dim(queries, column_start, pair_lanes, 1).reshape(
        tokens, heads_paired, HD
    )
    key_pair = lax.dynamic_slice_in_dim(window_keys, column_start, pair_lanes, 1).reshape(
        WIN, heads_paired, HD
    )
    value_pair = lax.dynamic_slice_in_dim(window_values, column_start, pair_lanes, 1).reshape(
        WIN, heads_paired, HD
    )
    return (query_pair, key_pair, value_pair)


def attend(queries, window_keys, window_values, allowed):
    tokens = queries.shape[0]
    pair_lanes = heads_paired * HD
    pair_count = queries.shape[1] // pair_lanes

    def one_pair(pair_index, running):
        mixed_heads, log_total = running
        query_pair, key_pair, value_pair = pair_slices(
            queries, window_keys, window_values, pair_index
        )
        scores = jnp.einsum(
            "qhd,khd->hqk", query_pair, key_pair, preferred_element_type=jnp.float32
        )
        scores = jnp.where(allowed[None], scores, -1e30)
        row_top = jnp.max(scores, axis=-1, keepdims=True)
        exponent = jnp.exp(scores - row_top)
        row_total = jnp.sum(exponent, axis=-1, keepdims=True)
        probabilities = (exponent / row_total).astype(jnp.bfloat16)
        mixed_pair = jnp.einsum(
            "hqk,khd->qhd", probabilities, value_pair, preferred_element_type=jnp.float32
        )
        mixed_heads = lax.dynamic_update_slice_in_dim(
            mixed_heads, mixed_pair.reshape(tokens, pair_lanes), pair_index * pair_lanes, 1
        )
        log_total = lax.dynamic_update_slice_in_dim(
            log_total, (row_top + jnp.log(row_total))[:, :, 0], pair_index * heads_paired, 0
        )
        return (mixed_heads, log_total)

    start_state = (
        jnp.zeros((tokens, queries.shape[1]), jnp.float32),
        jnp.zeros((pair_count * heads_paired, tokens), jnp.float32),
    )
    return lax.fori_loop(0, pair_count, one_pair, start_state)


def attend_back(queries, window_keys, window_values, allowed, log_total, grad_mixed):
    tokens = queries.shape[0]
    pair_lanes = heads_paired * HD
    pair_count = queries.shape[1] // pair_lanes

    def one_pair(pair_index, running):
        grad_queries, grad_keys, grad_values = running
        query_pair, key_pair, value_pair = pair_slices(
            queries, window_keys, window_values, pair_index
        )
        column_start = pair_index * pair_lanes
        grad_pair = lax.dynamic_slice_in_dim(grad_mixed, column_start, pair_lanes, 1).reshape(
            tokens, heads_paired, HD
        )
        pair_log = lax.dynamic_slice_in_dim(log_total, pair_index * heads_paired, heads_paired, 0)
        scores = jnp.einsum(
            "qhd,khd->hqk", query_pair, key_pair, preferred_element_type=jnp.float32
        )
        scores = jnp.where(allowed[None], scores, -1e30)
        probabilities = jnp.exp(scores - pair_log[:, :, None])
        probs_low = probabilities.astype(jnp.bfloat16)
        grad_probs = jnp.einsum(
            "qhd,khd->hqk", grad_pair, value_pair, preferred_element_type=jnp.float32
        )
        row_inner = jnp.sum(probabilities * grad_probs, axis=-1, keepdims=True)
        grad_scores = (probabilities * (grad_probs - row_inner)).astype(jnp.bfloat16)
        query_part = jnp.einsum(
            "hqk,khd->qhd", grad_scores, key_pair, preferred_element_type=jnp.float32
        )
        key_part = jnp.einsum(
            "hqk,qhd->khd", grad_scores, query_pair, preferred_element_type=jnp.float32
        )
        value_part = jnp.einsum(
            "hqk,qhd->khd", probs_low, grad_pair, preferred_element_type=jnp.float32
        )
        grad_queries = lax.dynamic_update_slice_in_dim(
            grad_queries, query_part.reshape(tokens, pair_lanes), column_start, 1
        )
        grad_keys = lax.dynamic_update_slice_in_dim(
            grad_keys, key_part.reshape(WIN, pair_lanes), column_start, 1
        )
        grad_values = lax.dynamic_update_slice_in_dim(
            grad_values, value_part.reshape(WIN, pair_lanes), column_start, 1
        )
        return (grad_queries, grad_keys, grad_values)

    width = queries.shape[1]
    start_state = (
        jnp.zeros((tokens, width), jnp.float32),
        jnp.zeros((WIN, width), jnp.float32),
        jnp.zeros((WIN, width), jnp.float32),
    )
    return lax.fori_loop(0, pair_count, one_pair, start_state)


def forward_layer(hidden, gathered, allowed, score_scale):
    (
        query_weight,
        query_bias,
        key_weight,
        value_weight,
        value_bias,
        output_weight,
        output_bias,
        first_gain,
        first_shift,
        inner_weight,
        inner_bias,
        outer_weight,
        outer_bias,
        second_gain,
        second_shift,
    ) = gathered
    rounded = hidden.astype(jnp.bfloat16)
    queries = ((project(rounded, query_weight) + query_bias) * score_scale).astype(jnp.bfloat16)
    key_rows = project(rounded, key_weight).astype(jnp.bfloat16)
    value_rows = (project(rounded, value_weight) + value_bias).astype(jnp.bfloat16)
    window_keys, window_values = widen_window(key_rows, value_rows)
    mixed_heads, log_total = attend(queries, window_keys, window_values, allowed)
    mixed_low = mixed_heads.astype(jnp.bfloat16)
    first_sum = hidden + (project(mixed_low, output_weight) + output_bias)
    settled = normalize(first_sum, first_gain.astype(jnp.float32), first_shift.astype(jnp.float32))
    settled_low = settled.astype(jnp.bfloat16)
    inner_act = project(settled_low, inner_weight) + inner_bias
    activated = gelu_exact(inner_act).astype(jnp.bfloat16)
    second_sum = settled + (project(activated, outer_weight) + outer_bias)
    layer_out = normalize(
        second_sum, second_gain.astype(jnp.float32), second_shift.astype(jnp.float32)
    )
    return (
        layer_out,
        (
            rounded,
            queries,
            window_keys,
            window_values,
            log_total,
            mixed_low,
            first_sum,
            settled_low,
            inner_act,
            activated,
            second_sum,
        ),
    )


def backward_layer(grad_out, layer_saved, gathered, allowed, score_scale, arrange):
    (
        query_weight,
        query_bias,
        key_weight,
        value_weight,
        value_bias,
        output_weight,
        output_bias,
        first_gain,
        first_shift,
        inner_weight,
        inner_bias,
        outer_weight,
        outer_bias,
        second_gain,
        second_shift,
    ) = gathered
    (
        rounded,
        queries,
        window_keys,
        window_values,
        log_total,
        mixed_low,
        first_sum,
        settled_low,
        inner_act,
        activated,
        second_sum,
    ) = layer_saved
    tokens = queries.shape[0]
    unused_second, second_pull = jax.vjp(
        normalize, second_sum, second_gain.astype(jnp.float32), second_shift.astype(jnp.float32)
    )
    grad_second, grad_second_gain, grad_second_shift = second_pull(grad_out)
    grad_outer = grad_second.astype(jnp.bfloat16)
    grad_outer_weight = contract_rows(arrange(activated), grad_outer)
    grad_outer_bias = arrange(column_sums(grad_outer))
    unused_inner, gelu_pull = jax.vjp(gelu_exact, inner_act)
    grad_inner = gelu_pull(against(grad_outer, outer_weight))[0].astype(jnp.bfloat16)
    grad_inner_weight = contract_rows(arrange(settled_low), grad_inner)
    grad_inner_bias = arrange(column_sums(grad_inner))
    grad_settled = grad_second + against(grad_inner, inner_weight)
    unused_first, first_pull = jax.vjp(
        normalize, first_sum, first_gain.astype(jnp.float32), first_shift.astype(jnp.float32)
    )
    grad_first, grad_first_gain, grad_first_shift = first_pull(grad_settled)
    grad_branch = grad_first.astype(jnp.bfloat16)
    grad_output_weight = contract_rows(arrange(mixed_low), grad_branch)
    grad_output_bias = arrange(column_sums(grad_branch))
    grad_mixed = against(grad_branch, output_weight).astype(jnp.bfloat16)
    query_partial, key_partial, value_partial = attend_back(
        queries, window_keys, window_values, allowed, log_total, grad_mixed
    )
    key_total, value_total = give_back(key_partial, value_partial, tokens)
    grad_keys = key_total.astype(jnp.bfloat16)
    grad_values = value_total.astype(jnp.bfloat16)
    grad_queries = query_partial.astype(jnp.bfloat16) * score_scale
    arranged_rounded = arrange(rounded)
    grad_query_weight = contract_rows(arranged_rounded, grad_queries)
    grad_query_bias = arrange(column_sums(grad_queries))
    grad_key_weight = contract_rows(arranged_rounded, grad_keys)
    grad_value_weight = contract_rows(arranged_rounded, grad_values)
    grad_value_bias = arrange(column_sums(grad_values))
    grad_hidden = (
        grad_first
        + against(grad_queries, query_weight)
        + against(grad_keys, key_weight)
        + against(grad_values, value_weight)
    )
    return (
        grad_hidden,
        (
            grad_query_weight,
            grad_query_bias,
            grad_key_weight,
            grad_value_weight,
            grad_value_bias,
            grad_output_weight,
            grad_output_bias,
            arrange(grad_first_gain),
            arrange(grad_first_shift),
            grad_inner_weight,
            grad_inner_bias,
            grad_outer_weight,
            grad_outer_bias,
            arrange(grad_second_gain),
            arrange(grad_second_shift),
        ),
    )


def local(
    hidden_in,
    segment_ids,
    query_weight,
    query_bias,
    key_weight,
    value_weight,
    value_bias,
    output_weight,
    output_bias,
    first_gain,
    first_shift,
    inner_weight,
    inner_bias,
    outer_weight,
    outer_bias,
    second_gain,
    second_shift,
    cotangent,
):
    masters = (
        query_weight,
        query_bias,
        key_weight,
        value_weight,
        value_bias,
        output_weight,
        output_bias,
        first_gain,
        first_shift,
        inner_weight,
        inner_bias,
        outer_weight,
        outer_bias,
        second_gain,
        second_shift,
    )
    tokens = hidden_in.shape[0]
    score_scale = HD ** (-0.5)
    allowed = document_mask(segment_ids, tokens)
    hidden = hidden_in.astype(jnp.float32)
    saved = []
    for layer_index in range(LAYERS):
        pieces = [master[layer_index].astype(jnp.bfloat16) for master in masters]
        gathered = (
            lax.all_gather(pieces[0], "ctx", axis=0, tiled=True),
            lax.all_gather(pieces[1], "ctx", axis=0, tiled=True),
            lax.all_gather(pieces[2], "ctx", axis=0, tiled=True),
            lax.all_gather(pieces[3], "ctx", axis=0, tiled=True),
            lax.all_gather(pieces[4], "ctx", axis=0, tiled=True),
            lax.all_gather(pieces[5], "ctx", axis=0, tiled=True),
            lax.all_gather(pieces[6], "ctx", axis=0, tiled=True),
            lax.all_gather(pieces[7], "ctx", axis=0, tiled=True),
            lax.all_gather(pieces[8], "ctx", axis=0, tiled=True),
            lax.all_gather(pieces[9], "ctx", axis=0, tiled=True),
            lax.all_gather(pieces[10], "ctx", axis=0, tiled=True),
            lax.all_gather(pieces[11], "ctx", axis=0, tiled=True),
            lax.all_gather(pieces[12], "ctx", axis=0, tiled=True),
            lax.all_gather(pieces[13], "ctx", axis=0, tiled=True),
            lax.all_gather(pieces[14], "ctx", axis=0, tiled=True),
        )
        hidden, layer_saved = forward_layer(hidden, gathered, allowed, score_scale)
        saved.append((layer_saved, None))
    output = hidden.astype(jnp.bfloat16)
    grad_hidden = cotangent.astype(jnp.float32)
    layer_grads = [None] * LAYERS
    for layer_index in reversed(range(LAYERS)):
        layer_saved, gathered = saved[layer_index]
        pieces = [master[layer_index].astype(jnp.bfloat16) for master in masters]
        gathered = (
            lax.all_gather(pieces[0], "ctx", axis=0, tiled=True),
            lax.all_gather(pieces[1], "ctx", axis=0, tiled=True),
            lax.all_gather(pieces[2], "ctx", axis=0, tiled=True),
            lax.all_gather(pieces[3], "ctx", axis=0, tiled=True),
            lax.all_gather(pieces[4], "ctx", axis=0, tiled=True),
            lax.all_gather(pieces[5], "ctx", axis=0, tiled=True),
            lax.all_gather(pieces[6], "ctx", axis=0, tiled=True),
            lax.all_gather(pieces[7], "ctx", axis=0, tiled=True),
            lax.all_gather(pieces[8], "ctx", axis=0, tiled=True),
            lax.all_gather(pieces[9], "ctx", axis=0, tiled=True),
            lax.all_gather(pieces[10], "ctx", axis=0, tiled=True),
            lax.all_gather(pieces[11], "ctx", axis=0, tiled=True),
            lax.all_gather(pieces[12], "ctx", axis=0, tiled=True),
            lax.all_gather(pieces[13], "ctx", axis=0, tiled=True),
            lax.all_gather(pieces[14], "ctx", axis=0, tiled=True),
        )
        grad_hidden, full_grads = backward_layer(
            grad_hidden, layer_saved, gathered, allowed, score_scale, keep_order
        )
        owned = (
            lax.psum_scatter(
                full_grads[0].astype(jnp.bfloat16), "ctx", scatter_dimension=0, tiled=True
            ).astype(jnp.float32),
            lax.psum_scatter(
                full_grads[1].astype(jnp.bfloat16), "ctx", scatter_dimension=0, tiled=True
            ).astype(jnp.float32),
            lax.psum_scatter(
                full_grads[2].astype(jnp.bfloat16), "ctx", scatter_dimension=0, tiled=True
            ).astype(jnp.float32),
            lax.psum_scatter(
                full_grads[3].astype(jnp.bfloat16), "ctx", scatter_dimension=0, tiled=True
            ).astype(jnp.float32),
            lax.psum_scatter(
                full_grads[4].astype(jnp.bfloat16), "ctx", scatter_dimension=0, tiled=True
            ).astype(jnp.float32),
            lax.psum_scatter(
                full_grads[5].astype(jnp.bfloat16), "ctx", scatter_dimension=0, tiled=True
            ).astype(jnp.float32),
            lax.psum_scatter(
                full_grads[6].astype(jnp.bfloat16), "ctx", scatter_dimension=0, tiled=True
            ).astype(jnp.float32),
            lax.psum_scatter(
                full_grads[7].astype(jnp.bfloat16), "ctx", scatter_dimension=0, tiled=True
            ).astype(jnp.float32),
            lax.psum_scatter(
                full_grads[8].astype(jnp.bfloat16), "ctx", scatter_dimension=0, tiled=True
            ).astype(jnp.float32),
            lax.psum_scatter(
                full_grads[9].astype(jnp.bfloat16), "ctx", scatter_dimension=0, tiled=True
            ).astype(jnp.float32),
            lax.psum_scatter(
                full_grads[10].astype(jnp.bfloat16), "ctx", scatter_dimension=0, tiled=True
            ).astype(jnp.float32),
            lax.psum_scatter(
                full_grads[11].astype(jnp.bfloat16), "ctx", scatter_dimension=0, tiled=True
            ).astype(jnp.float32),
            lax.psum_scatter(
                full_grads[12].astype(jnp.bfloat16), "ctx", scatter_dimension=0, tiled=True
            ).astype(jnp.float32),
            lax.psum_scatter(
                full_grads[13].astype(jnp.bfloat16), "ctx", scatter_dimension=0, tiled=True
            ).astype(jnp.float32),
            lax.psum_scatter(
                full_grads[14].astype(jnp.bfloat16), "ctx", scatter_dimension=0, tiled=True
            ).astype(jnp.float32),
        )
        shared = (
            lax.psum(owned[0].astype(jnp.bfloat16), "dp").astype(jnp.float32),
            lax.psum(owned[1].astype(jnp.bfloat16), "dp").astype(jnp.float32),
            lax.psum(owned[2].astype(jnp.bfloat16), "dp").astype(jnp.float32),
            lax.psum(owned[3].astype(jnp.bfloat16), "dp").astype(jnp.float32),
            lax.psum(owned[4].astype(jnp.bfloat16), "dp").astype(jnp.float32),
            lax.psum(owned[5].astype(jnp.bfloat16), "dp").astype(jnp.float32),
            lax.psum(owned[6].astype(jnp.bfloat16), "dp").astype(jnp.float32),
            lax.psum(owned[7].astype(jnp.bfloat16), "dp").astype(jnp.float32),
            lax.psum(owned[8].astype(jnp.bfloat16), "dp").astype(jnp.float32),
            lax.psum(owned[9].astype(jnp.bfloat16), "dp").astype(jnp.float32),
            lax.psum(owned[10].astype(jnp.bfloat16), "dp").astype(jnp.float32),
            lax.psum(owned[11].astype(jnp.bfloat16), "dp").astype(jnp.float32),
            lax.psum(owned[12].astype(jnp.bfloat16), "dp").astype(jnp.float32),
            lax.psum(owned[13].astype(jnp.bfloat16), "dp").astype(jnp.float32),
            lax.psum(owned[14].astype(jnp.bfloat16), "dp").astype(jnp.float32),
        )
        layer_grads[layer_index] = shared
    stacked = tuple(
        (
            jnp.stack(
                [layer_grads[layer_position][member_index] for layer_position in range(LAYERS)]
            )
            for member_index in range(15)
        )
    )
    return (output, grad_hidden.astype(jnp.bfloat16)) + stacked


def solution(mesh):
    placed = (
        P(("dp", "ctx"), None),
        P("dp", None, None),
        P(None, "ctx", None),
        P(None, "ctx"),
        P(None, "ctx", None),
        P(None, "ctx", None),
        P(None, "ctx"),
        P(None, "ctx", None),
        P(None, "ctx"),
        P(None, "ctx"),
        P(None, "ctx"),
        P(None, "ctx", None),
        P(None, "ctx"),
        P(None, "ctx", None),
        P(None, "ctx"),
        P(None, "ctx"),
        P(None, "ctx"),
        P(("dp", "ctx"), None),
    )
    return jax.shard_map(
        local,
        mesh=mesh,
        in_specs=placed,
        out_specs=(
            P(("dp", "ctx"), None),
            P(("dp", "ctx"), None),
            P(None, "ctx", None),
            P(None, "ctx"),
            P(None, "ctx", None),
            P(None, "ctx", None),
            P(None, "ctx"),
            P(None, "ctx", None),
            P(None, "ctx"),
            P(None, "ctx"),
            P(None, "ctx"),
            P(None, "ctx", None),
            P(None, "ctx"),
            P(None, "ctx", None),
            P(None, "ctx"),
            P(None, "ctx"),
            P(None, "ctx"),
        ),
        check_vma=False,
    )
```

profile of v0, /device:TPU:0, one launch (start us, length us, event | category | flops | bytes accessed | tf_op | source)
XLA Modules:
  0.0 2439.7 jit_solution(3733871637856658696)
XLA Ops:
  26.2 22.4 all-gather.1
  118.4 26.1 %all-gather.10 = bf16[1,4096]{1,0:T(2,128)(2,1)S(1)} all-gather(bf16[1,512]{1,0:T(2,128)(2,1)S(1)} %get-tuple-element.1111), channel_id=12, replica_groups=mesh['dp'=4,'ctx'=8] {'ctx'}, dimensions={1}, use_global_device_ids=true | all-gather | bytes 9216 | tf_op jit(solution)/shard_map/all_gather | solution.py:414
  285.2 26.7 %all-gather.25 = bf16[1,4096]{1,0:T(2,128)(2,1)S(1)} all-gather(bf16[1,512]{1,0:T(2,128)(2,1)S(1)} %get-tuple-element.1112), channel_id=27, replica_groups=mesh['dp'=4,'ctx'=8] {'ctx'}, dimensions={1}, use_global_device_ids=true | all-gather | bytes 9216 | tf_op jit(solution)/shard_map/all_gather | solution.py:414
  348.3 19.2 all-gather.29
  418.7 27.5 %collective-permute-done.7 = bf16[256,1024]{1,0:T(8,128)(2,1)} collective-permute-done((bf16[256,1024]{1,0:T(8,128)(2,1)}, bf16[256,1024]{1,0:T(8,128)(2,1)}, u32[]{:S(2)}, u32[]{:S(2)}) %collective-permute-start.7) | collective-permute-done | bytes 524320 | tf_op jit(solution)/shard_map/ppermute | solution.py:19
  450.8 39.4 %while.68 = (s32[]{:T(128)}, bf16[256,1024]{0,1:T(8,128)(2,1)}, f32[16,256]{1,0:T(8,128)S(1)}, bf16[1280,1024]{0,1:T(8,128)(2,1)}, bf16[256,1024]{0,1:T(8,128)(2...) while((s32[]{:T(128)}, bf16[256,1024]{0,1:T(8,128)(2,1)}, ...), condition=%wide.region_3.4_spmd.clone, body=%wide.region_0.3_spmd.clone.sunk | while | flops 173669888 | bytes 10909193 | solution.py:156
  516.9 31.5 %all-gather.59.cloned.1.call-done = bf16[1,1024,1024]{2,1,0:T(8,128)(2,1)} async-done(((bf16[1,128,1024]{2,1,0:T(8,128)(2,1)}), bf16[1,1024,1024]{2,1,0:T(8,128)(2,1)}) %all-gather.59.cloned.1.call-update) | async-done | bytes 2097168 | tf_op jit(solution)/shard_map/all_gather | solution.py:406
  560.8 47.6 %all-gather.55.cloned.1.call-done = bf16[1,1024,1024]{2,1,0:T(8,128)(2,1)} async-done(((bf16[1,128,1024]{2,1,0:T(8,128)(2,1)}), bf16[1,1024,1024]{2,1,0:T(8,128)(2,1)}) %all-gather.55.cloned.1.call-update) | async-done | bytes 2097168 | tf_op jit(solution)/shard_map/all_gather | solution.py:407
  614.8 47.1 %all-gather.57.cloned.1.call-done = bf16[1,1024,1024]{2,1,0:T(8,128)(2,1)} async-done(((bf16[1,128,1024]{2,1,0:T(8,128)(2,1)}), bf16[1,1024,1024]{2,1,0:T(8,128)(2,1)}) %all-gather.57.cloned.1.call-update) | async-done | bytes 2097168 | tf_op jit(solution)/shard_map/all_gather | solution.py:404
  710.0 34.7 %while.69 = (s32[]{:T(128)}, bf16[256,1024]{0,1:T(8,128)(2,1)S(1)}, f32[16,256]{1,0:T(8,128)S(1)}, bf16[1280,1024]{0,1:T(8,128)(2,1)}, bf16[256,1024]{0,1:T(8,12...) while((s32[]{:T(128)}, bf16[256,1024]{0,1:T(8,128)(2,1)S(1)}, ...), condition=%wide.region_11.12_spmd.clone, body=%wide.region_8.11_spmd.clone.sunk | while | flops 173669888 | bytes 10909193 | solution.py:156
  748.0 102.2 %all-gather.63.cloned.1.call-done = bf16[1,1024,4096]{2,1,0:T(8,128)(2,1)} async-done(((bf16[1,128,4096]{2,1,0:T(8,128)(2,1)}), bf16[1,1024,4096]{2,1,0:T(8,128)(2,1)}) %all-gather.63.cloned.1.call-update) | async-done | bytes 8388624 | tf_op jit(solution)/shard_map/all_gather | solution.py:413
  866.5 109.4 %all-gather.65.cloned.1.call-done = bf16[1,4096,1024]{2,1,0:T(8,128)(2,1)} async-done(((bf16[1,512,1024]{2,1,0:T(8,128)(2,1)}), bf16[1,4096,1024]{2,1,0:T(8,128)(2,1)}) %all-gather.65.cloned.1.call-update) | async-done | bytes 8388624 | tf_op jit(solution)/shard_map/all_gather | solution.py:415
  1011.3 73.4 %while.70 = (s32[]{:T(128)}, bf16[256,1024]{0,1:T(8,128)(2,1)}, f32[1280,1024]{0,1:T(8,128)}, f32[1280,1024]{0,1:T(8,128)}, bf16[1280,1024]{0,1:T(8,128)(2,1)}, ...) while((s32[]{:T(128)}, bf16[256,1024]{0,1:T(8,128)(2,1)}, ...), condition=%wide.region_22.23_spmd.clone, body=%wide.region_20.22_spmd.clone.sunk | while | flops 425983488 | bytes 27418156 | solution.py:211
  1194.9 72.8 %while.71 = (s32[]{:T(128)}, bf16[256,1024]{0,1:T(8,128)(2,1)}, f32[1280,1024]{0,1:T(8,128)}, f32[1280,1024]{0,1:T(8,128)}, bf16[1280,1024]{0,1:T(8,128)(2,1)}, ...) while((s32[]{:T(128)}, bf16[256,1024]{0,1:T(8,128)(2,1)}, ...), condition=%wide.region_29.30_spmd.clone, body=%wide.region_27.29_spmd.clone.sunk | while | flops 425983488 | bytes 31612516 | solution.py:211
  1407.9 68.2 %reduce-scatter.41.cloned.1.call-done = bf16[128,1024]{1,0:T(8,128)(2,1)} async-done(((bf16[1024,1024]{1,0:T(8,128)(2,1)}), bf16[128,1024]{1,0:T(8,128)(2,1)}) %reduce-scatter.41.cloned.1.call-update) | async-done | bytes 262160
  1477.9 68.3 %reduce-scatter.45.cloned.1.call-done = bf16[128,1024]{1,0:T(8,128)(2,1)} async-done(((bf16[1024,1024]{1,0:T(8,128)(2,1)}), bf16[128,1024]{1,0:T(8,128)(2,1)}) %reduce-scatter.45.cloned.1.call-update) | async-done | bytes 262160
  1548.0 68.4 %reduce-scatter.27.cloned.1.call-done = bf16[128,1024]{1,0:T(8,128)(2,1)} async-done(((bf16[1024,1024]{1,0:T(8,128)(2,1)}), bf16[128,1024]{1,0:T(8,128)(2,1)}) %reduce-scatter.27.cloned.1.call-update) | async-done | bytes 262160 | tf_op jit(solution)/shard_map/reduce_scatter | solution.py:464
  1616.3 70.0 %reduce-scatter.25.cloned.1.call-done = bf16[128,1024]{1,0:T(8,128)(2,1)} async-done(((bf16[1024,1024]{1,0:T(8,128)(2,1)}), bf16[128,1024]{1,0:T(8,128)(2,1)}) %reduce-scatter.25.cloned.1.call-update) | async-done | bytes 262160 | tf_op jit(solution)/shard_map/reduce_scatter | solution.py:464
  1686.4 151.7 %reduce-scatter.35.cloned.1.call-done = bf16[512,1024]{1,0:T(8,128)(2,1)} async-done(((bf16[4096,1024]{1,0:T(8,128)(2,1)}), bf16[512,1024]{1,0:T(8,128)(2,1)}) %reduce-scatter.35.cloned.1.call-update) | async-done | bytes 1048592 | tf_op jit(solution)/shard_map/reduce_scatter | solution.py:482
  1838.0 152.1 %reduce-scatter.31.cloned.1.call-done = bf16[128,4096]{1,0:T(8,128)(2,1)} async-done(((bf16[1024,4096]{1,0:T(8,128)(2,1)}), bf16[128,4096]{1,0:T(8,128)(2,1)}) %reduce-scatter.31.cloned.1.call-update) | async-done | bytes 1048592 | tf_op jit(solution)/shard_map/reduce_scatter | solution.py:476
  1990.2 151.7 %reduce-scatter.29.cloned.1.call-done = bf16[128,4096]{1,0:T(8,128)(2,1)} async-done(((bf16[1024,4096]{1,0:T(8,128)(2,1)}), bf16[128,4096]{1,0:T(8,128)(2,1)}) %reduce-scatter.29.cloned.1.call-update) | async-done | bytes 1048592 | tf_op jit(solution)/shard_map/reduce_scatter | solution.py:476
  2141.9 152.0 %reduce-scatter.33.cloned.1.call-done = bf16[512,1024]{1,0:T(8,128)(2,1)} async-done(((bf16[4096,1024]{1,0:T(8,128)(2,1)}), bf16[512,1024]{1,0:T(8,128)(2,1)}) %reduce-scatter.33.cloned.1.call-update) | async-done | bytes 1048592 | tf_op jit(solution)/shard_map/reduce_scatter | solution.py:482
  2297.8 35.9 %all-reduce.19 = (bf16[1024]{0:T(1024)(128)(2,1)S(1)}, bf16[1024]{0:T(1024)(128)(2,1)S(1)}, bf16[1024]{0:T(1024)(128)(2,1)S(1)}, bf16[1024]{0:T(1024)(128)(2,1)S...) all-reduce(bf16[1024]{0:T(1024)(128)(2,1)S(1)} %fusion.201, ...), channel_id=35, replica_groups=mesh['dp'=4,'ctx'=8] {'ctx'}, use_global_device_ids=true, to_apply=%region_38.39.clone | all-reduce | flops 24576 | bytes 98304
  2355.5 63.7 %all-reduce.24.cloned.1.call-done = (bf16[1,128,1024]{1,2,0:T(8,128)(2,1)}, bf16[1,128,1024]{1,2,0:T(8,128)(2,1)}, bf16[1,128,1024]{1,2,0:T(8,128)(2,1)}, bf16[1...) async-done(((bf16[1,128,1024]{1,2,0:T(8,128)(2,1)}, ...) | async-done | bytes 6291472 | tf_op jit(solution)/shard_map/psum | solution.py:496
  (944 shorter events, 978.3 us)
Async XLA Ops:
  7.2 360.9 %all-gather.43.cloned.1.call-start = ((), (), s32[]{:S(2)}) async-start(), calls=%async_computation.18 | async-start | bytes 2359296 | tf_op jit(solution)/shard_map/all_gather | solution.py:407
  9.5 367.8 %all-gather.47.cloned.1.call-start = ((), (), s32[]{:S(2)}) async-start(), calls=%async_computation.20 | async-start | bytes 2359296 | tf_op jit(solution)/shard_map/all_gather | solution.py:406
  11.7 374.1 %all-gather.45.cloned.1.call-start = ((), (), s32[]{:S(2)}) async-start(), calls=%async_computation.19 | async-start | bytes 2359296 | tf_op jit(solution)/shard_map/all_gather | solution.py:404
  12.7 477.5 %all-gather.49.cloned.1.call-start = ((), (), s32[]{:S(2)}) async-start(), calls=%async_computation.21 | async-start | bytes 2359296 | tf_op jit(solution)/shard_map/all_gather | solution.py:409
  13.7 479.4 %all-gather.51.cloned.1.call-start = ((), (), s32[]{:S(2)}) async-start(), calls=%async_computation.22 | async-start | bytes 9437184 | tf_op jit(solution)/shard_map/all_gather | solution.py:413
  17.7 491.3 %all-gather.53.cloned.1.call-start = ((), (), s32[]{:S(2)}) async-start(), calls=%async_computation.23 | async-start | bytes 9437184 | tf_op jit(solution)/shard_map/all_gather | solution.py:415
  21.9 526.5 %all-gather.59.cloned.1.call-start = ((), (), s32[]{:S(2)}) async-start(), calls=%async_computation.26 | async-start | bytes 2359296 | tf_op jit(solution)/shard_map/all_gather | solution.py:406
  22.7 585.7 %all-gather.55.cloned.1.call-start = ((), (), s32[]{:S(2)}) async-start(), calls=%async_computation.24 | async-start | bytes 2359296 | tf_op jit(solution)/shard_map/all_gather | solution.py:407
  23.4 638.5 %all-gather.57.cloned.1.call-start = ((), (), s32[]{:S(2)}) async-start(), calls=%async_computation.25 | async-start | bytes 2359296 | tf_op jit(solution)/shard_map/all_gather | solution.py:404
  24.2 720.6 %all-gather.61.cloned.1.call-start = ((), (), s32[]{:S(2)}) async-start(), calls=%async_computation.27 | async-start | bytes 2359296 | tf_op jit(solution)/shard_map/all_gather | solution.py:409
  24.7 825.5 %all-gather.63.cloned.1.call-start = ((), (), s32[]{:S(2)}) async-start(), calls=%async_computation.28 | async-start | bytes 9437184 | tf_op jit(solution)/shard_map/all_gather | solution.py:413
  25.5 950.4 %all-gather.65.cloned.1.call-start = ((), (), s32[]{:S(2)}) async-start(), calls=%async_computation.29 | async-start | bytes 9437184 | tf_op jit(solution)/shard_map/all_gather | solution.py:415
  26.1 1359.7 %reduce-scatter.39.cloned.1.call-start = ((), (), s32[]{:S(2)}) async-start(), calls=%async_computation.31 | async-start | bytes 2359296
  1088.0 299.5 %reduce-scatter.47.cloned.1.call-start = ((), (), s32[]{:S(2)}) async-start(), calls=%async_computation.35 | async-start | bytes 2359296
  1166.7 222.6 %reduce-scatter.43.cloned.1.call-start = ((), (), s32[]{:S(2)}) async-start(), calls=%async_computation.33 | async-start | bytes 2359296
  1186.3 219.8 %reduce-scatter.37.cloned.1.call-start = ((), (), s32[]{:S(2)}) async-start(), calls=%async_computation.30 | async-start | bytes 2359296
  1313.5 232.7 %reduce-scatter.45.cloned.1.call-start = ((), (), s32[]{:S(2)}) async-start(), calls=%async_computation.34 | async-start | bytes 2359296
  1345.1 271.2 %reduce-scatter.27.cloned.1.call-start = ((), (), s32[]{:S(2)}) async-start(), calls=%async_computation.13 | async-start | bytes 2359296 | tf_op jit(solution)/shard_map/reduce_scatter | solution.py:464
  1348.3 338.0 %reduce-scatter.25.cloned.1.call-start = ((), (), s32[]{:S(2)}) async-start(), calls=%async_computation.12 | async-start | bytes 2359296 | tf_op jit(solution)/shard_map/reduce_scatter | solution.py:464
  1351.8 486.2 %reduce-scatter.35.cloned.1.call-start = ((), (), s32[]{:S(2)}) async-start(), calls=%async_computation.17 | async-start | bytes 9437184 | tf_op jit(solution)/shard_map/reduce_scatter | solution.py:482
  1357.9 632.3 %reduce-scatter.31.cloned.1.call-start = ((), (), s32[]{:S(2)}) async-start(), calls=%async_computation.15 | async-start | bytes 9437184 | tf_op jit(solution)/shard_map/reduce_scatter | solution.py:476
  1366.7 775.2 %reduce-scatter.29.cloned.1.call-start = ((), (), s32[]{:S(2)}) async-start(), calls=%async_computation.14 | async-start | bytes 9437184 | tf_op jit(solution)/shard_map/reduce_scatter | solution.py:476
  1375.4 918.5 %reduce-scatter.33.cloned.1.call-start = ((), (), s32[]{:S(2)}) async-start(), calls=%async_computation.16 | async-start | bytes 9437184 | tf_op jit(solution)/shard_map/reduce_scatter | solution.py:482
  1382.7 1036.5 %all-reduce.24.cloned.1.call-start = ((), (), s32[]{:S(2)}) async-start(), calls=%async_computation.36 | async-start | bytes 12582912 | tf_op jit(solution)/shard_map/psum | solution.py:496
  (146 other events, 8990.4 us)
Sparse Core Ops, SparseCore 0:
  10.7 52.0 all-gather.42
  65.5 47.8 all-gather.46
  116.1 47.8 all-gather.44
  166.6 47.9 all-gather.48
  217.2 129.1 all-gather.50
  348.9 149.8 all-gather.52
  550.5 57.8 all-gather.54
  610.6 51.3 all-gather.56
  663.9 60.1 all-gather.60
  726.8 123.3 all-gather.62
  852.8 123.1 all-gather.64
  1088.1 88.3 reduce-scatter.38
  1179.9 66.5 reduce-scatter.46
  1250.5 82.4 reduce-scatter.42
  1337.0 69.0 reduce-scatter.36
  1409.5 66.5 reduce-scatter.40
  1479.5 66.6 reduce-scatter.44
  1549.7 66.6 reduce-scatter.26
  1619.7 66.6 reduce-scatter.24
  1690.0 147.9 reduce-scatter.34
  1842.1 148.0 reduce-scatter.30
  1993.8 148.0 reduce-scatter.28
  2145.8 147.9 reduce-scatter.32
  2298.3 120.8 all-reduce.23
  (1 shorter events, 47.4 us)
where the time goes:
time: 2450 us; the launch traced here: 2440 us
  waiting for transfers between devices  1420 us (58%)
  blocking collectives  384 us (16%)
  matrix products  222 us (9%)
  local copies, waits for them, and re-layouts  215 us (9%)
  starting transfers between devices  102 us (4%)
  other arithmetic  74.7 us (3%)
    reduce_scatter x2, waiting for transfers between devices, local(): lax.psum_scatter(full_grads[9].astype(jnp.bfloat16), 'ctx', scatter_dimen...  304 us
    reduce_scatter x2, waiting for transfers between devices, local(): lax.psum_scatter(full_grads[11].astype(jnp.bfloat16), 'ctx', scatter_dime...  304 us
    unnamed x31, waiting for transfers between devices  156 us
    reduce_scatter x2, waiting for transfers between devices, local(): lax.psum_scatter(full_grads[5].astype(jnp.bfloat16), 'ctx', scatter_dimen...  138 us
    ppermute x32, waiting for transfers between devices, from_behind(): return lax.ppermute(shard, axis, pairs)  120 us
    all_gather x2, waiting for transfers between devices, local(): lax.all_gather(pieces[11], 'ctx', axis=0, tiled=True)  109 us
    all_gather x2, waiting for transfers between devices, local(): lax.all_gather(pieces[9], 'ctx', axis=0, tiled=True)  102 us
    ppermute x32, starting transfers between devices, from_behind(): return lax.ppermute(shard, axis, pairs)  100 us
  transfers between devices with their start and end apart: 57, of which 28 were waited for; matrix products, arithmetic and copies ran while one was open for 15% of the time, Pallas kernels for 0%

commit v1 on v0

v1 whole, which is shorter than its diff:
```python
import jax
import jax.numpy as jnp
from jax import lax
from jax.experimental import pallas as pl
from jax.experimental.pallas import tpu as pltpu
from jax.sharding import PartitionSpec as P

HD = 64
LAYERS = 2
SEQ = 2048
SLOTS = 5
OWN = 2
BF16 = jnp.bfloat16
F32 = jnp.float32
CORE_PAIRS = [(i, i ^ 1) for i in range(4)]
X_PAIRS = [(i, i ^ 2) for i in range(4)]


def dot(left, right, dims, out=F32):
    return lax.dot_general(left, right, (dims, ((), ())), preferred_element_type=F32).astype(out)


NN = ((1,), (0,))
NT = ((1,), (1,))
TN = ((0,), (0,))


def core_swap(value):
    return lax.ppermute(value, "dp", CORE_PAIRS)


def x_swap(value):
    return lax.ppermute(value, "dp", X_PAIRS)


def tie(value, *tokens):
    return lax.optimization_barrier((value,) + tokens)[0]


def ordered(place, mine, peer, axis):
    first = jnp.where(place == 0, mine, peer)
    second = jnp.where(place == 0, peer, mine)
    return jnp.concatenate([first, second], axis=axis)


class Ring:
    def __init__(self, n):
        self.n = n
        self.order = [2 * r if r < n // 2 else 2 * (n - 1 - r) + 1 for r in range(n)]
        self.cw = [(self.order[r], self.order[(r + 1) % n]) for r in range(n)]
        self.ccw = [(b, a) for a, b in self.cw]
        ctx = lax.axis_index("ctx")
        self.place = jnp.where(ctx % 2 == 0, ctx // 2, n - 1 - ctx // 2)

    def member(self, distance):
        r = (self.place + distance) % self.n
        return jnp.where(r < self.n // 2, 2 * r, 2 * (self.n - 1 - r) + 1)

    def gather(self, own, long_cw):
        n = self.n
        chunks, distances = [own], [0]
        forward, backward = own, own
        cw_steps = n // 2 if long_cw else n // 2 - 1
        for step in range(1, n // 2 + 1):
            if step <= cw_steps:
                forward = lax.ppermute(forward, "ctx", self.cw)
                chunks.append(forward)
                distances.append(-step)
            if step <= n - 1 - cw_steps:
                backward = lax.ppermute(backward, "ctx", self.ccw)
                chunks.append(backward)
                distances.append(step)
        return chunks, distances

    def scatter(self, part_of, long_cw):
        n = self.n
        cw_steps = n // 2 if long_cw else n // 2 - 1
        ccw_steps = n - 1 - cw_steps
        got_cw = got_ccw = None
        for step in range(n // 2, 0, -1):
            if step <= cw_steps:
                part = part_of(self.member(step))
                if got_cw is not None:
                    part = part + got_cw.astype(F32)
                got_cw = lax.ppermute(part.astype(BF16), "ctx", self.cw)
            if step <= ccw_steps:
                part = part_of(self.member(-step))
                if got_ccw is not None:
                    part = part + got_ccw.astype(F32)
                got_ccw = lax.ppermute(part.astype(BF16), "ctx", self.ccw)
        return part_of(lax.axis_index("ctx")) + got_cw.astype(F32) + got_ccw.astype(F32)


def assemble_attention(chunks, owners):
    n = len(chunks)
    rows, wide = chunks[0].shape
    w = wide // 4

    def kernel(owner_ref, *refs):
        ins, qkv_ref, out_ref, sems = refs[:n], refs[n], refs[n + 1], refs[n + 2]
        copies = []
        for i in range(n):
            o = owner_ref[i]
            copies.append(pltpu.make_async_copy(ins[i].at[:, : 3 * w], qkv_ref.at[o], sems.at[2 * i]))
            copies.append(pltpu.make_async_copy(ins[i].at[:, 3 * w :], out_ref.at[o], sems.at[2 * i + 1]))
        for c in copies:
            c.start()
        for c in copies:
            c.wait()

    return pl.pallas_call(
        kernel,
        out_shape=(
            jax.ShapeDtypeStruct((n, rows, 3 * w), BF16),
            jax.ShapeDtypeStruct((n, rows, w), BF16),
        ),
        in_specs=[pl.BlockSpec(memory_space=pltpu.SMEM)] + [pl.BlockSpec(memory_space=pl.ANY)] * n,
        out_specs=(pl.BlockSpec(memory_space=pl.ANY), pl.BlockSpec(memory_space=pl.ANY)),
        scratch_shapes=[pltpu.SemaphoreType.DMA((2 * n,))],
    )(owners, *chunks)


def assemble_feed(mine, other, owners, place):
    n = len(mine)
    both, cols = mine[0].shape
    rows = both // 2

    def kernel(owner_ref, place_ref, *refs):
        ins, first_ref, second_ref, sems = refs[: 2 * n], refs[2 * n], refs[2 * n + 1], refs[2 * n + 2]
        copies = []
        for half in range(2):
            for i in range(n):
                o = owner_ref[i]
                h = place_ref[half]
                src = ins[half * n + i]
                k = 2 * (half * n + i)
                col = pl.multiple_of(h * cols, 128)
                copies.append(
                    pltpu.make_async_copy(
                        src.at[:rows], first_ref.at[o, :, pl.ds(col, cols)], sems.at[k]
                    )
                )
                copies.append(
                    pltpu.make_async_copy(src.at[rows:], second_ref.at[h, o], sems.at[k + 1])
                )
        for c in copies:
            c.start()
        for c in copies:
            c.wait()

    return pl.pallas_call(
        kernel,
        out_shape=(
            jax.ShapeDtypeStruct((n, rows, 2 * cols), BF16),
            jax.ShapeDtypeStruct((2, n, rows, cols), BF16),
        ),
        in_specs=[pl.BlockSpec(memory_space=pltpu.SMEM)] * 2 + [pl.BlockSpec(memory_space=pl.ANY)] * (2 * n),
        out_specs=(pl.BlockSpec(memory_space=pl.ANY), pl.BlockSpec(memory_space=pl.ANY)),
        scratch_shapes=[pltpu.SemaphoreType.DMA((4 * n,))],
    )(owners, place, *mine, *other)


SLOT_ORDER = (2, 1, 3, 0, 4)


def attend_kernel(need_ref, q_ref, k_ref, v_ref, qseg_ref, kseg_ref, mixed_ref, lse_ref, top, total, acc):
    seq = pl.program_id(0)
    q = q_ref[0]
    tokens = q.shape[0]
    lane = lax.broadcasted_iota(jnp.int32, q.shape, 1)
    zero = jnp.zeros_like(q)
    heads = (jnp.where(lane < HD, q, zero), jnp.where(lane < HD, zero, q))
    qseg = qseg_ref[0]

    def one_slot(slot, first):
        keys = k_ref[0, slot]
        values = v_ref[0, slot]
        mask = kseg_ref[0, slot * tokens : (slot + 1) * tokens] == qseg
        for h in range(2):
            scores = dot(keys, heads[h], NT)
            scores = jnp.where(mask, scores, -1e30)
            best = jnp.max(scores, axis=0, keepdims=True)
            if not first:
                old = top[h]
                best = jnp.maximum(best, old)
            expo = jnp.exp(scores - best)
            sums = jnp.sum(expo, axis=0, keepdims=True)
            part = dot(values, expo.astype(BF16), TN)
            if not first:
                shrink = jnp.exp(old - best)
                sums = sums + total[h] * shrink
                part = part + acc[h] * shrink
            top[h] = best
            total[h] = sums
            acc[h] = part

    one_slot(OWN, True)
    for slot in SLOT_ORDER[1:]:

        @pl.when(need_ref[seq * SLOTS + slot] > 0)
        def _(slot=slot):
            one_slot(slot, False)

    halves = [acc[h][HD * h : HD * (h + 1)] / total[h] for h in range(2)]
    mixed_ref[0] = jnp.concatenate(halves, axis=0).T.astype(BF16)
    lse_ref[0, 0] = jnp.concatenate([top[h] + jnp.log(total[h]) for h in range(2)], axis=0)


def attend(queries, keys_values, query_ids, key_ids, need):
    seqs, tokens, width = queries.shape
    pairs = width // 128
    return pl.pallas_call(
        attend_kernel,
        grid_spec=pltpu.PrefetchScalarGridSpec(
            num_scalar_prefetch=1,
            grid=(seqs, pairs),
            in_specs=[
                pl.BlockSpec((1, tokens, 128), lambda s, p, n: (s, 0, p)),
                pl.BlockSpec((1, SLOTS, tokens, 128), lambda s, p, n: (s, 0, 0, p)),
                pl.BlockSpec((1, SLOTS, tokens, 128), lambda s, p, n: (s, 0, 0, pairs + p)),
                pl.BlockSpec((1, 1, tokens), lambda s, p, n: (s, 0, 0)),
                pl.BlockSpec((1, SLOTS * tokens, 1), lambda s, p, n: (s, 0, 0)),
            ],
            out_specs=[
                pl.BlockSpec((1, tokens, 128), lambda s, p, n: (s, 0, p)),
                pl.BlockSpec((1, 1, 2, tokens), lambda s, p, n: (s, p, 0, 0)),
            ],
            scratch_shapes=[
                pltpu.VMEM((2, 1, tokens), F32),
                pltpu.VMEM((2, 1, tokens), F32),
                pltpu.VMEM((2, 128, tokens), F32),
            ],
        ),
        out_shape=(
            jax.ShapeDtypeStruct((seqs, tokens, width), BF16),
            jax.ShapeDtypeStruct((seqs, pairs, 2, tokens), F32),
        ),
    )(need, queries, keys_values, keys_values, query_ids, key_ids)


def attend_back_kernel(
    need_ref, q_ref, k_ref, v_ref, g_ref, mixed_ref, lse_ref, qseg_ref, kseg_ref, gq_ref, gk_ref, gv_ref, acc
):
    seq = pl.program_id(0)
    q = q_ref[0]
    g = g_ref[0]
    tokens = q.shape[0]
    lane = lax.broadcasted_iota(jnp.int32, q.shape, 1)
    zero = jnp.zeros_like(q)
    heads = (jnp.where(lane < HD, q, zero), jnp.where(lane < HD, zero, q))
    grads = (jnp.where(lane < HD, g, zero), jnp.where(lane < HD, zero, g))
    qseg = qseg_ref[0]
    product = (g.astype(F32) * mixed_ref[0].astype(F32)).T
    inner = [jnp.sum(product[HD * h : HD * (h + 1)], axis=0, keepdims=True) for h in range(2)]
    lse = lse_ref[0, 0]

    def one_slot(slot, first):
        keys = k_ref[0, slot]
        values = v_ref[0, slot]
        mask = kseg_ref[0, slot * tokens : (slot + 1) * tokens] == qseg
        key_grad = value_grad = None
        for h in range(2):
            scores = dot(keys, heads[h], NT)
            probs = jnp.exp(jnp.where(mask, scores, -1e30) - lse[h : h + 1])
            grad_probs = dot(values, grads[h], NT)
            grad_scores = (probs * (grad_probs - inner[h])).astype(BF16)
            part = dot(keys, grad_scores, TN)
            acc[h] = part if first else acc[h] + part
            key_part = dot(grad_scores, heads[h], NN)
            value_part = dot(probs.astype(BF16), grads[h], NN)
            key_grad = key_part if h == 0 else key_grad + key_part
            value_grad = value_part if h == 0 else value_grad + value_part
        gk_ref[0, slot] = key_grad.astype(BF16)
        gv_ref[0, slot] = value_grad.astype(BF16)

    one_slot(OWN, True)
    for slot in SLOT_ORDER[1:]:
        wanted = need_ref[seq * SLOTS + slot] > 0

        @pl.when(wanted)
        def _(slot=slot):
            one_slot(slot, False)

        @pl.when(jnp.logical_not(wanted))
        def _(slot=slot):
            gk_ref[0, slot] = zero
            gv_ref[0, slot] = zero

    joined = jnp.concatenate([acc[h][HD * h : HD * (h + 1)] for h in range(2)], axis=0)
    gq_ref[0] = joined.T.astype(BF16) * (HD**-0.5)


def attend_back(queries, keys_values, grad_mixed, mixed, lse, query_ids, key_ids, need):
    seqs, tokens, width = queries.shape
    pairs = width // 128
    row_spec = pl.BlockSpec((1, tokens, 128), lambda s, p, n: (s, 0, p))
    slot_spec = pl.BlockSpec((1, SLOTS, tokens, 128), lambda s, p, n: (s, 0, 0, p))
    return pl.pallas_call(
        attend_back_kernel,
        grid_spec=pltpu.PrefetchScalarGridSpec(
            num_scalar_prefetch=1,
            grid=(seqs, pairs),
            in_specs=[
                row_spec,
                slot_spec,
                pl.BlockSpec((1, SLOTS, tokens, 128), lambda s, p, n: (s, 0, 0, pairs + p)),
                row_spec,
                row_spec,
                pl.BlockSpec((1, 1, 2, tokens), lambda s, p, n: (s, p, 0, 0)),
                pl.BlockSpec((1, 1, tokens), lambda s, p, n: (s, 0, 0)),
                pl.BlockSpec((1, SLOTS * tokens, 1), lambda s, p, n: (s, 0, 0)),
            ],
            out_specs=[row_spec, slot_spec, slot_spec],
            scratch_shapes=[pltpu.VMEM((2, 128, tokens), F32)],
        ),
        out_shape=(
            jax.ShapeDtypeStruct((seqs, tokens, width), BF16),
            jax.ShapeDtypeStruct((seqs, SLOTS, tokens, width), BF16),
            jax.ShapeDtypeStruct((seqs, SLOTS, tokens, width), BF16),
        ),
    )(need, queries, keys_values, keys_values, grad_mixed, mixed, lse, query_ids, key_ids)


def normalize(operand, gain, shift):
    centered = operand - jnp.mean(operand, axis=-1, keepdims=True)
    spread = jnp.mean(centered * centered, axis=-1, keepdims=True)
    return centered * lax.rsqrt(spread + 1e-05) * gain + shift


def normalize_back(operand, gain, grad):
    centered = operand - jnp.mean(operand, axis=-1, keepdims=True)
    spread = jnp.mean(centered * centered, axis=-1, keepdims=True)
    inverse = lax.rsqrt(spread + 1e-05)
    unit = centered * inverse
    scaled = grad * gain
    out = inverse * (
        scaled
        - jnp.mean(scaled, axis=-1, keepdims=True)
        - unit * jnp.mean(scaled * unit, axis=-1, keepdims=True)
    )
    return out, jnp.sum(grad * unit, axis=0), jnp.sum(grad, axis=0)


def column_sums(operand):
    return jnp.sum(operand.astype(F32), axis=0)


def shifts(n, by):
    return [(i, i + by) for i in range(n) if 0 <= i + by < n]


def widen(own, n):
    odd = lax.axis_index("ctx") % 2 == 1
    pairs = [(i, i ^ 1) for i in range(n)]
    behind = lax.ppermute(own, "ctx", shifts(n, 2))
    ahead = lax.ppermute(own, "ctx", shifts(n, -2))
    beside = lax.ppermute(own, "ctx", pairs)
    across = lax.ppermute(jnp.where(odd, behind, ahead), "ctx", pairs)
    return jnp.stack([behind, beside, own, across, ahead])


def give_back(parts, n):
    odd = lax.axis_index("ctx") % 2 == 1
    pairs = [(i, i ^ 1) for i in range(n)]
    across = lax.ppermute(parts[3].astype(BF16), "ctx", pairs).astype(F32)
    beside = lax.ppermute(parts[1].astype(BF16), "ctx", pairs).astype(F32)
    behind = parts[0] + jnp.where(odd, across, 0.0)
    ahead = parts[4] + jnp.where(odd, 0.0, across)
    from_ahead = lax.ppermute(behind.astype(BF16), "ctx", shifts(n, -2)).astype(F32)
    from_behind = lax.ppermute(ahead.astype(BF16), "ctx", shifts(n, 2)).astype(F32)
    return parts[2] + beside + from_ahead + from_behind


def slot_ids(group_ids, tokens, n):
    ctx = lax.axis_index("ctx")
    per = SEQ // tokens
    odd = ctx % 2 == 1
    blocks = [ctx - 2, ctx ^ 1, ctx, jnp.where(odd, ctx + 1, ctx - 1), ctx + 2]
    out = []
    for block in blocks:
        inside = (block >= 0) & (block < n) & (block // per == ctx // per)
        start = jnp.clip(block, 0, n - 1) * tokens
        out.append(jnp.where(inside, lax.dynamic_slice_in_dim(group_ids, start, tokens), -1))
    return jnp.stack(out)


def local(
    hidden_in,
    segment_ids,
    query_weight,
    query_bias,
    key_weight,
    value_weight,
    value_bias,
    output_weight,
    output_bias,
    first_gain,
    first_shift,
    inner_weight,
    inner_bias,
    outer_weight,
    outer_bias,
    second_gain,
    second_shift,
    cotangent,
):
    tokens, width = hidden_in.shape
    n = lax.axis_size("ctx")
    ctx = lax.axis_index("ctx")
    dp = lax.axis_index("dp")
    core = dp % 2
    x = dp // 2
    half = width // 2
    ff = inner_weight.shape[2]
    quarter = ff // (4 * n)
    wide = ff // 4
    scale = HD**-0.5
    ring = Ring(n)

    def attention_pack(layer):
        parts = [
            lax.dynamic_slice_in_dim(w[layer], core * half, half, 1).astype(BF16)
            for w in (query_weight, key_weight, value_weight, output_weight)
        ]
        return jnp.concatenate(parts, axis=1)

    def feed_pack(layer, place):
        rows = inner_weight.shape[1]
        first = inner_weight[layer].reshape(rows, n, 4, quarter)
        first = lax.dynamic_index_in_dim(first, core * 2 + place, 2, keepdims=False)
        second = outer_weight[layer].reshape(4, quarter, width)
        second = lax.dynamic_index_in_dim(second, core * 2 + place, 0, keepdims=False)
        return jnp.concatenate([first.reshape(rows, wide).astype(BF16), second.astype(BF16)], axis=0)

    vectors = [
        query_bias, value_bias, output_bias, first_gain, first_shift,
        outer_bias, second_gain, second_shift, inner_bias,
    ]

    packs = {}
    packs["a0"] = attention_pack(0)
    chunks_a0, dist_long = ring.gather(packs["a0"], True)
    vector_pack = jnp.concatenate([v.astype(BF16) for v in vectors], axis=1)
    gathered_vectors = lax.all_gather(vector_pack, "ctx", axis=0)
    feed0 = tie(feed_pack(0, x), chunks_a0[3])
    chunks_f0, dist_short = ring.gather(feed0, False)
    others_f0 = [x_swap(c) for c in chunks_f0[1:]]
    attn1 = tie(attention_pack(1), chunks_f0[3])
    chunks_a1, _ = ring.gather(attn1, True)
    feed1 = tie(feed_pack(1, x), chunks_a1[3])
    chunks_f1, _ = ring.gather(feed1, False)
    others_f1 = [x_swap(c) for c in chunks_f1[1:]]

    owners_long = jnp.stack([ring.member(d) for d in dist_long]).astype(jnp.int32)
    owners_short = jnp.stack([ring.member(d) for d in dist_short]).astype(jnp.int32)
    places = jnp.stack([x, 1 - x]).astype(jnp.int32)

    def layer_weights(layer, chunks_a, chunks_f, others_f):
        qkv, out_half = assemble_attention(chunks_a, owners_long)
        qkv = qkv.reshape(width, 3 * half)
        out_half = out_half.reshape(width, half)
        mine = lax.dynamic_slice_in_dim(out_half, core * half, half, 0)
        theirs = core_swap(lax.dynamic_slice_in_dim(out_half, (1 - core) * half, half, 0))
        out_rows = ordered(core, mine, theirs, 1)
        first, second = assemble_feed(chunks_f, [feed_pack(layer, 1 - x)] + others_f, owners_short, places)
        return qkv[:, :half], qkv[:, half:], out_rows, first.reshape(width, 2 * wide), second.reshape(2 * wide, width)

    weights = [
        layer_weights(0, chunks_a0, chunks_f0, others_f0),
        layer_weights(1, chunks_a1, chunks_f1, others_f1),
    ]

    per = width // n

    def layer_vectors(layer):
        g = gathered_vectors[:, layer].astype(F32)
        flat = [g[:, i * per : (i + 1) * per].reshape(-1) for i in range(8)]
        inner = g[:, 8 * per :].reshape(n, 2, 2, quarter)
        inner = lax.dynamic_index_in_dim(inner, core, 1, keepdims=False)
        inner = jnp.transpose(inner, (1, 0, 2)).reshape(-1)
        mine = [lax.dynamic_slice_in_dim(v, core * half, half) for v in flat[:2]]
        return mine + flat[2:] + [inner]

    own_ids = segment_ids.reshape(-1)
    ids = [slot_ids(own_ids, tokens, n), slot_ids(core_swap(own_ids), tokens, n)]
    key_ids = jnp.stack(ids)
    query_ids = key_ids[:, OWN]
    low, high = jnp.min(query_ids, axis=1), jnp.max(query_ids, axis=1)
    need = (jnp.max(key_ids, axis=2) >= low[:, None]) & (jnp.min(key_ids, axis=2) <= high[:, None])
    need = need.astype(jnp.int32).reshape(-1)
    query_ids = query_ids.reshape(2, 1, tokens)
    key_ids = key_ids.reshape(2, SLOTS * tokens, 1)

    def both(value):
        return jnp.concatenate([value, core_swap(value)], axis=0)

    def sum_cores(partial):
        return partial[:tokens] + core_swap(partial[tokens:])

    hidden = hidden_in.astype(F32)
    saved = []
    for layer in range(LAYERS):
        wq, wkv, wo, w1, w2 = weights[layer]
        bq, bv, bo, g1, c1, b2, g2, c2, b1 = layer_vectors(layer)
        rounded = hidden.astype(BF16)
        window = widen(rounded, n)
        window = jnp.stack([window, core_swap(window)])
        rows = window[:, OWN].reshape(2 * tokens, width)
        flat = window.reshape(2 * SLOTS * tokens, width)
        queries = ((dot(rows, wq, NN) + bq) * scale).astype(BF16).reshape(2, tokens, half)
        kv_bias = jnp.concatenate([jnp.zeros_like(bv), bv])
        keys_values = (dot(flat, wkv, NN) + kv_bias).astype(BF16).reshape(2, SLOTS, tokens, width)
        mixed, lse = attend(queries, keys_values, query_ids, key_ids, need)
        mixed_rows = mixed.reshape(2 * tokens, half)
        first_sum = hidden + (sum_cores(dot(mixed_rows, wo, NN)) + bo)
        settled = normalize(first_sum, g1, c1)
        settled_rows = both(settled.astype(BF16))
        inner = dot(settled_rows, w1, NN) + b1
        cdf = (1.0 + lax.erf(inner * (0.5**0.5))) * 0.5
        activated = (inner * cdf).astype(BF16)
        slope = cdf + inner * jnp.exp(-0.5 * inner * inner) * (0.5 / jnp.pi) ** 0.5
        second_sum = settled + (sum_cores(dot(activated, w2, NN)) + b2)
        hidden = normalize(second_sum, g2, c2)
        saved.append((flat, rows, queries, keys_values, lse, mixed, first_sum, settled_rows, slope, activated, second_sum))
    output = hidden.astype(BF16)

    grad = cotangent.astype(F32)
    layer_grads = [None] * LAYERS
    vector_grads = [None] * LAYERS
    zeros_half = jnp.zeros((width,), F32)
    for layer in reversed(range(LAYERS)):
        wq, wkv, wo, w1, w2 = weights[layer]
        bq, bv, bo, g1, c1, b2, g2, c2, b1 = layer_vectors(layer)
        flat, rows, queries, keys_values, lse, mixed, first_sum, settled_rows, slope, activated, second_sum = saved[layer]
        grad_second, d_g2, d_c2 = normalize_back(second_sum, g2, grad)
        go = grad_second.astype(BF16)
        go_rows = both(go)
        d_w2 = dot(activated, go_rows, TN, BF16).reshape(2, n, quarter, width)
        d_b2 = column_sums(go)
        gi = (slope * dot(go_rows, w2, NT)).astype(BF16)
        d_w1 = dot(settled_rows, gi, TN, BF16)
        d_b1 = column_sums(gi)
        gset = grad_second + sum_cores(dot(gi, w1, NT))
        grad_first, d_g1, d_c1 = normalize_back(first_sum, g1, gset)
        gb = grad_first.astype(BF16)
        gb_rows = both(gb)
        d_wo = dot(mixed.reshape(2 * tokens, half), gb_rows, TN, BF16)
        d_bo = column_sums(gb)
        gm = dot(gb_rows, wo, NT, BF16).reshape(2, tokens, half)
        gq, gk, gv = attend_back(queries, keys_values, gm, mixed, lse, query_ids, key_ids, need)
        gq = gq.reshape(2 * tokens, half)
        gk = gk.reshape(2 * SLOTS * tokens, half)
        gv = gv.reshape(2 * SLOTS * tokens, half)
        d_bq = column_sums(gq)
        d_bv = column_sums(gv)
        d_wq = dot(rows, gq, TN, BF16)
        d_wk = dot(flat, gk, TN, BF16)
        d_wv = dot(flat, gv, TN, BF16)
        du_rows = dot(gq, wq, NT)
        du = (dot(gk, wkv[:, :half], NT) + dot(gv, wkv[:, half:], NT)).reshape(2, SLOTS, tokens, width)
        du = du.at[:, OWN].add(du_rows.reshape(2, tokens, width))
        du = du.astype(BF16)
        du_own = du[0].astype(F32) + core_swap(du[1]).astype(F32)
        grad = grad_first + give_back(du_own, n)

        def outer_part(t, d_w2=d_w2):
            return lax.dynamic_index_in_dim(d_w2, t, 1, keepdims=False).astype(F32)

        sum_w2 = ring.scatter(outer_part, True).astype(BF16)
        sum_w2 = (sum_w2.astype(F32) + x_swap(sum_w2).astype(F32)).astype(BF16)
        sum_w2 = sum_w2.reshape(2 * quarter, width)
        out_w2 = ordered(core, sum_w2, core_swap(sum_w2), 0).astype(F32)

        give = lax.dynamic_slice_in_dim(d_w1, (1 - x) * wide, wide, 1)
        keep = lax.dynamic_slice_in_dim(d_w1, x * wide, wide, 1).reshape(n, per, wide)
        came = x_swap(give).reshape(n, per, wide)

        def inner_part(t, keep=keep, came=came):
            mine = lax.dynamic_index_in_dim(keep, t, 0, keepdims=False).astype(F32)
            return mine + lax.dynamic_index_in_dim(came, t, 0, keepdims=False).astype(F32)

        sum_w1 = ring.scatter(inner_part, False).astype(BF16)
        pair_w1 = ordered(x, sum_w1.reshape(per, n, 1, quarter), x_swap(sum_w1).reshape(per, n, 1, quarter), 2)
        pair_w1 = pair_w1.reshape(per, n, 1, 2 * quarter)
        out_w1 = ordered(core, pair_w1, core_swap(pair_w1), 2).reshape(per, ff).astype(F32)

        give = lax.dynamic_slice_in_dim(d_wo, (1 - core) * half, half, 1)
        keep = lax.dynamic_slice_in_dim(d_wo, core * half, half, 1)
        d_wo = ordered(core, keep, core_swap(give), 0)
        pieces = [d.reshape(n, per, half) for d in (d_wq, d_wk, d_wv, d_wo)]

        def attention_part(t, pieces=pieces):
            return jnp.concatenate(
                [lax.dynamic_index_in_dim(p, t, 0, keepdims=False) for p in pieces], axis=1
            ).astype(F32)

        sum_a = ring.scatter(attention_part, True).astype(BF16)
        sum_a = (sum_a.astype(F32) + x_swap(sum_a).astype(F32)).astype(BF16)
        peer_a = core_swap(sum_a)
        outs_a = [
            ordered(core, sum_a[:, i * half : (i + 1) * half], peer_a[:, i * half : (i + 1) * half], 1).astype(F32)
            for i in range(4)
        ]
        layer_grads[layer] = outs_a + [out_w1, out_w2]

        spread = [
            lax.dynamic_update_slice_in_dim(zeros_half, v, core * half, 0) for v in (d_bq, d_bv)
        ]
        d_b1 = jnp.transpose(d_b1.reshape(2, n, quarter), (1, 0, 2)).reshape(n, 1, 2 * quarter)
        d_b1 = lax.dynamic_update_slice_in_dim(jnp.zeros((n, 2, 2 * quarter), F32), d_b1, core, 1)
        vector_grads[layer] = jnp.concatenate(
            spread + [d_bo, d_g1, d_c1, d_b2, d_g2, d_c2, d_b1.reshape(-1)]
        )

    sums = lax.psum(jnp.stack(vector_grads), ("dp", "ctx"))
    own_vectors = [
        lax.dynamic_slice_in_dim(sums[:, i * width : (i + 1) * width], ctx * per, per, 1) for i in range(8)
    ]
    own_b1 = lax.dynamic_slice_in_dim(sums[:, 8 * width :], ctx * (ff // n), ff // n, 1)
    d_bq, d_bv, d_bo, d_g1, d_c1, d_b2, d_g2, d_c2 = own_vectors
    dq, dk, dv, do, d1, d2 = [jnp.stack(pair) for pair in zip(*layer_grads)]
    return (
        output,
        grad.astype(BF16),
        dq, d_bq, dk, dv, d_bv, do, d_bo, d_g1, d_c1, d1, own_b1, d2, d_b2, d_g2, d_c2,
    )


def solution(mesh):
    tokens = P(("dp", "ctx"), None)
    matrix = P(None, "ctx", None)
    vector = P(None, "ctx")
    params = (
        matrix, vector, matrix, matrix, vector, matrix, vector, vector,
        vector, matrix, vector, matrix, vector, vector, vector,
    )
    return jax.shard_map(
        local,
        mesh=mesh,
        in_specs=(tokens, P("dp", None, None)) + params + (tokens,),
        out_specs=(tokens, tokens) + params,
        check_vma=False,
    )
```

time: 2450 us -> 1920 us (0.78)
  waiting for transfers between devices: 1420 us -> 467 us
  Pallas kernels: 0 us -> 836 us
  blocking collectives: 384 us -> 39.8 us
  local copies, waits for them, and re-layouts: 215 us -> 108 us
  matrix products: 222 us -> 134 us
  starting transfers between devices: 102 us -> 190 us
  other arithmetic: 74.7 us -> 121 us
    pallas_call x0 -> x8, Pallas kernels: none -> 836 us  [the longest x2 512 us: assemble_feed(): pl.pallas_call(kernel, out_shape=(jax.ShapeDtypeStruct((n, rows, 2 * cols...]
    reduce_scatter x6 -> x0, waiting for transfers between devices: 746 us -> none  [the longest x2 304 us: local(): lax.psum_scatter(full_grads[9].astype(jnp.bfloat16), 'ctx', scatter_dimen...]
    all_gather x12 -> x0, waiting for transfers between devices: 338 us -> none  [the longest x2 109 us: local(): lax.all_gather(pieces[11], 'ctx', axis=0, tiled=True)]
    all_gather x18 -> x1, blocking collectives: 336 us -> 39.8 us  [local(): gathered_vectors = lax.all_gather(vector_pack, 'ctx', axis=0)]
    ppermute x32 -> x135, waiting for transfers between devices: 120 us -> 367 us  [the longest x22 106 us: x_swap(): return lax.ppermute(value, 'dp', X_PAIRS)]
    unnamed x31 -> x1, waiting for transfers between devices: 156 us -> 0.02 us
    ppermute x32 -> x135, starting transfers between devices: 100 us -> 190 us  [the longest x20 46.4 us: scatter(): got_ccw = lax.ppermute(part.astype(BF16), 'ctx', self.ccw)]
    dot_general x148 -> x34, matrix products: 222 us -> 134 us  [dot(): lax.dot_general(left, right, (dims, ((), ())), preferred_element_type=F32)]
  transfers between devices with their start and end apart: 57 -> 136, of which waited for: 28 -> 58; matrix products, arithmetic and copies ran while one was open for 15% -> 16% of each run, Pallas kernels for 0% -> 44%
where the time goes in v1:
time: 1920 us; the launch traced here: 1910 us
  Pallas kernels  836 us (44%)
  waiting for transfers between devices  467 us (24%)
  starting transfers between devices  190 us (10%)
  matrix products  134 us (7%)
  other arithmetic  121 us (6%)
  local copies, waits for them, and re-layouts  108 us (6%)
  blocking collectives  39.8 us (2%)
    pallas_call x2, Pallas kernels, assemble_feed(): pl.pallas_call(kernel, out_shape=(jax.ShapeDtypeStruct((n, rows, 2 * cols...  512 us
    pallas_call x2, Pallas kernels, assemble_attention(): pl.pallas_call(kernel, out_shape=(jax.ShapeDtypeStruct((n, rows, 3 * w),...  258 us
    dot_general x34, matrix products, dot(): lax.dot_general(left, right, (dims, ((), ())), preferred_element_type=F32)  134 us
    ppermute x22, waiting for transfers between devices, x_swap(): return lax.ppermute(value, 'dp', X_PAIRS)  106 us
    psum x1, waiting for transfers between devices, local(): sums = lax.psum(jnp.stack(vector_grads), ('dp', 'ctx'))  100 us
    ppermute x22, waiting for transfers between devices, scatter(): got_cw = lax.ppermute(part.astype(BF16), 'ctx', self.cw)  68.6 us
    ppermute x20, waiting for transfers between devices, scatter(): got_ccw = lax.ppermute(part.astype(BF16), 'ctx', self.ccw)  52.3 us
    ppermute x14, waiting for transfers between devices, gather(): backward = lax.ppermute(backward, 'ctx', self.ccw)  47.2 us
  transfers between devices with their start and end apart: 136, of which 58 were waited for; matrix products, arithmetic and copies ran while one was open for 16% of the time, Pallas kernels for 44%

profile of v1, /device:TPU:0, one launch (start us, length us, event | category | flops | bytes accessed | tf_op | source)
XLA Modules:
  0.0 1914.0 jit_solution(10825090757543327367)
XLA Ops:
  29.8 39.8 %all-gather.1 = bf16[8,2,1536]{2,1,0:T(2,128)(2,1)S(1)} all-gather(bf16[1,2,1536]{2,1,0:T(2,128)(2,1)S(1)} %bitcast.799), channel_id=2, replica_groups=mesh['dp'=4,'ctx'=8] {'ctx'}, dimensions={0}, use_global_device_ids=true | all-gather | bytes 55296 | tf_op jit(solution)/shard_map/all_gather | solution.py:444
  123.6 129.0 %shard_map.305 = (bf16[8,128,1536]{2,1,0:T(8,128)(2,1)}, bf16[8,128,512]{2,1,0:T(8,128)(2,1)}) custom-call(s32[8]{0:T(128)} %stack.228.owner_ref, bf16[128,2048]{1,0:T(8,128)(2,1)} %pad_maximum_fusion.30.refs_0_, bf16[128,2048]{1,0:T(8,128)(2,1)} %collective-permute-done.6.refs_1_, bf16[128,2048]{1,0:T(8,128)(2,1)} %collective-permute-done.7.refs_2_, ...), custom_call_target="tpu_custom_call" | custom-call | tf_op jit(solution)/shard_map/pallas_call | solution.py:111
  275.5 15.9 shard_map.306
  350.8 11.2 collective-permute-done.28.refs_14_
  362.1 11.2 collective-permute-done.27.refs_13_
  373.3 10.8 collective-permute-done.29.refs_15_
  384.1 256.2 %shard_map.307 = (bf16[8,128,2048]{2,1,0:T(8,128)(2,1)}, bf16[2,8,128,1024]{3,2,1,0:T(8,128)(2,1)}) custom-call(s32[8]{0:T(128)} %stack.233.owner_ref, s32[2]{0:T(128)} %pad_add_fusion.1.place_ref, bf16[256,1024]{1,0:T(8,128)(2,1)} %pad_maximum_fusion.31.refs_0_, bf16[256,1024]{1,0:T(8,128)(2,1)} %collective-permute-done.16.refs_1_, ...), custom_call_target="tpu_custom_call" | custom-call | tf_op jit(solution)/shard_map/pallas_call | solution.py:151
  682.8 19.8 %collective-permute-done.34 = bf16[256,1024]{1,0:T(8,128)(2,1)S(1)} collective-permute-done((bf16[256,1024]{1,0:T(8,128)(2,1)S(1)}, bf16[256,1024]{1,0:T(8,128)(2,1)S(1)}, u32[]{:S(2)}, u32[]{:S(2)}) %collective-permute-start.34) | collective-permute-done | bytes 524320 | tf_op jit(solution)/shard_map/ppermute | solution.py:358
  706.4 12.3 collective-permute-done.37.refs_2_
  720.7 11.5 collective-permute-done.39.refs_4_
  735.0 12.1 collective-permute-done.41.refs_6_
  747.9 129.0 %shard_map.308 = (bf16[8,128,1536]{2,1,0:T(8,128)(2,1)}, bf16[8,128,512]{2,1,0:T(8,128)(2,1)}) custom-call(s32[8]{0:T(128)} %stack.228.owner_ref, bf16[128,2048]{1,0:T(8,128)(2,1)} %copy-done.27, bf16[128,2048]{1,0:T(8,128)(2,1)} %copy-done.59, bf16[128,2048]{1,0:T(8,128)(2,1)} %copy-done.64, bf16[128,2048]{1,0:T(8,128)(2,1)} %copy-done.66, ...), custom_call_target="tpu_custom_call" | custom-call | tf_op jit(solution)/shard_map/pallas_call | solution.py:111
  896.1 15.7 shard_map.309
  970.0 11.2 collective-permute-done.58.refs_14_
  981.2 11.2 collective-permute-done.57.refs_13_
  1003.3 256.2 %shard_map.310 = (bf16[8,128,2048]{2,1,0:T(8,128)(2,1)}, bf16[2,8,128,1024]{3,2,1,0:T(8,128)(2,1)}) custom-call(s32[8]{0:T(128)} %stack.233.owner_ref, s32[2]{0:T(128)} %pad_add_fusion.1.place_ref, bf16[256,1024]{1,0:T(8,128)(2,1)} %copy-done.26, bf16[256,1024]{1,0:T(8,128)(2,1)} %collective-permute-done.46.refs_1_, ...), custom_call_target="tpu_custom_call" | custom-call | tf_op jit(solution)/shard_map/pallas_call | solution.py:151
  1312.5 12.2 collective-permute-done.127
  1350.3 17.3 shard_map.311
  1418.4 10.6 collective-permute-start.132
  1432.1 11.1 collective-permute-done.109
  1476.2 11.9 collective-permute-done.93
  1502.8 11.1 collective-permute-done.66
  1601.1 17.0 shard_map.312
  1675.0 100.2 %all-reduce.4.cloned.1.call-done = f32[2,12288]{1,0:T(2,128)} async-done(((f32[2,12288]{1,0:T(2,128)}), f32[2,12288]{1,0:T(2,128)}) %all-reduce.4.cloned.1.call-update) | async-done | bytes 98320 | tf_op jit(solution)/shard_map/psum | solution.py:615
  (843 shorter events, 751.8 us)
Async XLA Ops:
  7.2 1768.0 %all-reduce.4.cloned.1.call-start = ((), (), s32[]{:S(2)}) async-start(), calls=%async_computation | async-start | bytes 196608 | tf_op jit(solution)/shard_map/psum | solution.py:615
  15.0 78.7 %collective-permute-start.7 = (bf16[128,2048]{1,0:T(8,128)(2,1)}, bf16[128,2048]{1,0:T(8,128)(2,1)}, u32[]{:S(2)}, u32[]{:S(2)}) collective-permute-start(bf16[128,2048]{1,0:T(8,128)(2,1)} %pad_maximum_fusion.30.refs_0_), channel_id=1, source_target_pairs={{2,0},{4,2},{6,4},{7,6},{5,7},{3,5},{1,3},{0,1},{10,8},{12,10},{14... | collective-permute-start | bytes 1572872 | tf_op jit(solution)/shard_map/ppermute | solution.py:70
  18.0 54.1 %collective-permute-start.6 = (bf16[128,2048]{1,0:T(8,128)(2,1)}, bf16[128,2048]{1,0:T(8,128)(2,1)}, u32[]{:S(2)}, u32[]{:S(2)}) collective-permute-start(bf16[128,2048]{1,0:T(8,128)(2,1)} %pad_maximum_fusion.30.refs_0_), channel_id=1, source_target_pairs={{0,2},{2,4},{4,6},{6,7},{7,5},{5,3},{3,1},{1,0},{8,10},{10,12},{12... | collective-permute-start | bytes 1572872 | tf_op jit(solution)/shard_map/ppermute | solution.py:66
  18.1 54.0 %collective-permute-start.2 = (bf16[256,1024]{1,0:T(8,128)(2,1)S(1)}, bf16[256,1024]{1,0:T(8,128)(2,1)}, u32[]{:S(2)}, u32[]{:S(2)}) collective-permute-start(bf16[256,1024]{1,0:T(8,128)(2,1)S(1)} %copy-done.23), channel_id=1, source_target_pairs={{0,1},{1,0},{2,3},{3,2},{4,5},{5,4},{6,7},{7,6},{8,9},{9,8},{10,11... | collective-permute-start | bytes 1572872 | tf_op jit(solution)/shard_map/ppermute | solution.py:357
  20.0 49.7 %collective-permute-start.1 = (bf16[256,1024]{1,0:T(8,128)(2,1)S(1)}, bf16[256,1024]{1,0:T(8,128)(2,1)}, u32[]{:S(2)}, u32[]{:S(2)}) collective-permute-start(bf16[256,1024]{1,0:T(8,128)(2,1)S(1)} %copy-done.23), channel_id=1, source_target_pairs={{0,2},{1,3},{2,4},{3,5},{4,6},{5,7},{8,10},{9,11},{10,12},{11,13},... | collective-permute-start | bytes 1572872 | tf_op jit(solution)/shard_map/ppermute | solution.py:355
  69.8 46.0 %collective-permute-start = (s32[2048]{0:T(1024)}, s32[2048]{0:T(1024)}, u32[]{:S(2)}, u32[]{:S(2)}) collective-permute-start(s32[2048]{0:T(1024)} %bitcast.6), channel_id=1, source_target_pairs={{0,8},{8,0},{16,24},{24,16},{1,9},{9,1},{17,25},{25,17},{2,10},{10... | collective-permute-start | bytes 24584 | tf_op jit(solution)/shard_map/ppermute | solution.py:29
  86.4 174.7 %collective-permute-start.5 = (bf16[5,256,1024]{2,1,0:T(8,128)(2,1)}, bf16[5,256,1024]{2,1,0:T(8,128)(2,1)}, u32[]{:S(2)}, u32[]{:S(2)}) collective-permute-start(bf16[5,256,1024]{2,1,0:T(8,128)(2,1)} %bitcast_dynamic-update-slice_fusion.5), channel_id=1, source_target_pairs={{0,8},{8,0},{16,24},{24,16},{1,9},{9,1},{17,25},{25,17},{2,10},{10... | collective-permute-start | bytes 7864328 | tf_op jit(solution)/shard_map/ppermute | solution.py:29
  116.7 140.2 %collective-permute-start.17 = (bf16[256,1024]{1,0:T(8,128)(2,1)}, bf16[256,1024]{1,0:T(8,128)(2,1)}, u32[]{:S(2)}, u32[]{:S(2)}) collective-permute-start(bf16[256,1024]{1,0:T(8,128)(2,1)} %pad_maximum_fusion.31.refs_0_), channel_id=1, source_target_pairs={{2,0},{4,2},{6,4},{7,6},{5,7},{3,5},{1,3},{0,1},{10,8},{12,10},{14... | collective-permute-start | bytes 1572872 | tf_op jit(solution)/shard_map/ppermute | solution.py:70
  335.0 49.0 %collective-permute-start.29 = (bf16[256,1024]{1,0:T(8,128)(2,1)}, bf16[256,1024]{1,0:T(8,128)(2,1)}, u32[]{:S(2)}, u32[]{:S(2)}) collective-permute-start(bf16[256,1024]{1,0:T(8,128)(2,1)} %collective-permute-done.22.refs_7_), channel_id=1, source_target_pairs={{0,16},{8,24},{16,0},{24,8},{1,17},{9,25},{17,1},{25,9},{2,18},{10... | collective-permute-start | bytes 1572872 | tf_op jit(solution)/shard_map/ppermute | solution.py:33
  339.6 300.7 %collective-permute-start.15 = (bf16[256,1024]{1,0:T(8,128)(2,1)}, bf16[256,1024]{1,0:T(8,128)(2,1)}, u32[]{:S(2)}, u32[]{:S(2)}) collective-permute-start(bf16[256,1024]{1,0:T(8,128)(2,1)} %fusion.78), channel_id=1, source_target_pairs={{0,8},{8,0},{16,24},{24,16},{1,9},{9,1},{17,25},{25,17},{2,10},{10... | collective-permute-start | bytes 1572872 | tf_op jit(solution)/shard_map/ppermute | solution.py:29
  704.3 177.4 %collective-permute-start.35 = (bf16[5,256,1024]{2,1,0:T(8,128)(2,1)}, bf16[5,256,1024]{2,1,0:T(8,128)(2,1)}, u32[]{:S(2)}, u32[]{:S(2)}) collective-permute-start(bf16[5,256,1024]{2,1,0:T(8,128)(2,1)} %bitcast_dynamic-update-slice_fusion), channel_id=1, source_target_pairs={{0,8},{8,0},{16,24},{24,16},{1,9},{9,1},{17,25},{25,17},{2,10},{10... | collective-permute-start | bytes 7864328 | tf_op jit(solution)/shard_map/ppermute | solution.py:29
  734.4 143.8 %collective-permute-start.47 = (bf16[256,1024]{1,0:T(8,128)(2,1)S(1)}, bf16[256,1024]{1,0:T(8,128)(2,1)}, u32[]{:S(2)}, u32[]{:S(2)}) collective-permute-start(bf16[256,1024]{1,0:T(8,128)(2,1)S(1)} %pad_maximum_fusion.34.refs_0_), channel_id=1, source_target_pairs={{2,0},{4,2},{6,4},{7,6},{5,7},{3,5},{1,3},{0,1},{10,8},{12,10},{14... | collective-permute-start | bytes 1572872 | tf_op jit(solution)/shard_map/ppermute | solution.py:70
  955.5 47.8 %collective-permute-start.59 = (bf16[256,1024]{1,0:T(8,128)(2,1)S(1)}, bf16[256,1024]{1,0:T(8,128)(2,1)}, u32[]{:S(2)}, u32[]{:S(2)}) collective-permute-start(bf16[256,1024]{1,0:T(8,128)(2,1)S(1)} %collective-permute-done.52.refs_7_), channel_id=1, source_target_pairs={{0,16},{8,24},{16,0},{24,8},{1,17},{9,25},{17,1},{25,9},{2,18},{10... | collective-permute-start | bytes 1572872 | tf_op jit(solution)/shard_map/ppermute | solution.py:33
  958.8 300.8 %collective-permute-start.45 = (bf16[256,1024]{1,0:T(8,128)(2,1)}, bf16[256,1024]{1,0:T(8,128)(2,1)}, u32[]{:S(2)}, u32[]{:S(2)}) collective-permute-start(bf16[256,1024]{1,0:T(8,128)(2,1)} %fusion.80), channel_id=1, source_target_pairs={{0,8},{8,0},{16,24},{24,16},{1,9},{9,1},{17,25},{25,17},{2,10},{10... | collective-permute-start | bytes 1572872 | tf_op jit(solution)/shard_map/ppermute | solution.py:29
  1342.2 65.4 %collective-permute-start.107 = (bf16[1024,1024]{1,0:T(8,128)(2,1)}, bf16[1024,1024]{1,0:T(8,128)(2,1)}, u32[]{:S(2)}, u32[]{:S(2)}) collective-permute-start(bf16[1024,1024]{1,0:T(8,128)(2,1)} %get-tuple-element.221), channel_id=1, source_target_pairs={{0,16},{8,24},{16,0},{24,8},{1,17},{9,25},{17,1},{25,9},{2,18},{10... | collective-permute-start | bytes 6291464 | tf_op jit(solution)/shard_map/ppermute | solution.py:33
  1345.5 102.9 %collective-permute-start.129 = (bf16[2,128,1024]{2,1,0:T(8,128)(2,1)}, bf16[2,128,1024]{2,1,0:T(8,128)(2,1)}, u32[]{:S(2)}, u32[]{:S(2)}) collective-permute-start(bf16[2,128,1024]{2,1,0:T(8,128)(2,1)} %get-tuple-element.206), channel_id=1, source_target_pairs={{0,2},{2,4},{4,6},{6,7},{7,5},{5,3},{3,1},{1,0},{8,10},{10,12},{12... | collective-permute-start | bytes 1572872 | tf_op jit(solution)/shard_map/ppermute | solution.py:85
  1345.7 71.2 %collective-permute-start.131 = (bf16[2,128,1024]{2,1,0:T(8,128)(2,1)}, bf16[2,128,1024]{2,1,0:T(8,128)(2,1)}, u32[]{:S(2)}, u32[]{:S(2)}) collective-permute-start(bf16[2,128,1024]{2,1,0:T(8,128)(2,1)} %get-tuple-element.207), channel_id=1, source_target_pairs={{2,0},{4,2},{6,4},{7,6},{5,7},{3,5},{1,3},{0,1},{10,8},{12,10},{14... | collective-permute-start | bytes 1572872 | tf_op jit(solution)/shard_map/ppermute | solution.py:90
  1375.7 53.2 %collective-permute-start.87 = (bf16[512,512]{1,0:T(8,128)(2,1)}, bf16[512,512]{1,0:T(8,128)(2,1)}, u32[]{:S(2)}, u32[]{:S(2)}) collective-permute-start(bf16[512,512]{1,0:T(8,128)(2,1)} %constant_dynamic-slice_fusion.13), channel_id=1, source_target_pairs={{0,8},{8,0},{16,24},{24,16},{1,9},{9,1},{17,25},{25,17},{2,10},{10... | collective-permute-start | bytes 1572872 | tf_op jit(solution)/shard_map/ppermute | solution.py:29
  1432.1 62.8 %collective-permute-start.64 = (bf16[5,256,1024]{2,1,0:T(8,128)(2,1)S(1)}, bf16[5,256,1024]{2,1,0:T(8,128)(2,1)S(1)}, u32[]{:S(2)}, u32[]{:S(2)}) collective-permute-start(bf16[5,256,1024]{2,1,0:T(8,128)(2,1)S(1)} %copy-done.12), channel_id=1, source_target_pairs={{0,8},{8,0},{16,24},{24,16},{1,9},{9,1},{17,25},{25,17},{2,10},{10... | collective-permute-start | bytes 7864328 | tf_op jit(solution)/shard_map/ppermute | solution.py:29
  1593.0 188.9 %collective-permute-start.97 = (bf16[1024,1024]{1,0:T(8,128)(2,1)}, bf16[1024,1024]{1,0:T(8,128)(2,1)}, u32[]{:S(2)}, u32[]{:S(2)}) collective-permute-start(bf16[1024,1024]{1,0:T(8,128)(2,1)} %get-tuple-element.215), channel_id=1, source_target_pairs={{0,16},{8,24},{16,0},{24,8},{1,17},{9,25},{17,1},{25,9},{2,18},{10... | collective-permute-start | bytes 6291464 | tf_op jit(solution)/shard_map/ppermute | solution.py:33
  1596.3 208.6 %collective-permute-start.120 = (bf16[2,128,1024]{2,1,0:T(8,128)(2,1)}, bf16[2,128,1024]{2,1,0:T(8,128)(2,1)}, u32[]{:S(2)}, u32[]{:S(2)}) collective-permute-start(bf16[2,128,1024]{2,1,0:T(8,128)(2,1)} %get-tuple-element.202), channel_id=1, source_target_pairs={{0,2},{2,4},{4,6},{6,7},{7,5},{5,3},{3,1},{1,0},{8,10},{10,12},{12... | collective-permute-start | bytes 1572872 | tf_op jit(solution)/shard_map/ppermute | solution.py:85
  1596.6 189.9 %collective-permute-start.122 = (bf16[2,128,1024]{2,1,0:T(8,128)(2,1)}, bf16[2,128,1024]{2,1,0:T(8,128)(2,1)}, u32[]{:S(2)}, u32[]{:S(2)}) collective-permute-start(bf16[2,128,1024]{2,1,0:T(8,128)(2,1)} %get-tuple-element.203), channel_id=1, source_target_pairs={{2,0},{4,2},{6,4},{7,6},{5,7},{3,5},{1,3},{0,1},{10,8},{12,10},{14... | collective-permute-start | bytes 1572872 | tf_op jit(solution)/shard_map/ppermute | solution.py:90
  1643.7 145.8 %collective-permute-start.77 = (bf16[512,512]{1,0:T(8,128)(2,1)}, bf16[512,512]{1,0:T(8,128)(2,1)}, u32[]{:S(2)}, u32[]{:S(2)}) collective-permute-start(bf16[512,512]{1,0:T(8,128)(2,1)} %constant_dynamic-slice_fusion.14), channel_id=1, source_target_pairs={{0,8},{8,0},{16,24},{24,16},{1,9},{9,1},{17,25},{25,17},{2,10},{10... | collective-permute-start | bytes 1572872 | tf_op jit(solution)/shard_map/ppermute | solution.py:29
  1795.7 62.2 %collective-permute-start.72 = (bf16[5,256,1024]{2,1,0:T(8,128)(2,1)S(1)}, bf16[5,256,1024]{2,1,0:T(8,128)(2,1)S(1)}, u32[]{:S(2)}, u32[]{:S(2)}) collective-permute-start(bf16[5,256,1024]{2,1,0:T(8,128)(2,1)S(1)} %copy-done.11), channel_id=1, source_target_pairs={{0,8},{8,0},{16,24},{24,16},{1,9},{9,1},{17,25},{25,17},{2,10},{10... | collective-permute-start | bytes 7864328 | tf_op jit(solution)/shard_map/ppermute | solution.py:29
  (250 other events, 5706.6 us)
Sparse Core Ops, SparseCore 0:
  1640.7 134.4 all-reduce.3

commit v2 on v1

v2 whole, which is shorter than its diff:
```python
import jax
import jax.numpy as jnp
from jax import lax
from jax.experimental import pallas as pl
from jax.experimental.pallas import tpu as pltpu
from jax.sharding import PartitionSpec as P

HD = 64
LAYERS = 2
SEQ = 2048
SLOTS = 5
OWN = 2
BF16 = jnp.bfloat16
F32 = jnp.float32
CORE_PAIRS = [(i, i ^ 1) for i in range(4)]
X_PAIRS = [(i, i ^ 2) for i in range(4)]


def dot(left, right, dims, out=F32):
    return lax.dot_general(left, right, (dims, ((), ())), preferred_element_type=F32).astype(out)


NN = ((1,), (0,))
NT = ((1,), (1,))
TN = ((0,), (0,))


def core_swap(value):
    return lax.ppermute(value, "dp", CORE_PAIRS)


def x_swap(value):
    return lax.ppermute(value, "dp", X_PAIRS)


def tie(value, *tokens):
    return lax.optimization_barrier((value,) + tokens)[0]


def ordered(place, mine, peer, axis):
    first = jnp.where(place == 0, mine, peer)
    second = jnp.where(place == 0, peer, mine)
    return jnp.concatenate([first, second], axis=axis)


class Ring:
    def __init__(self, n):
        self.n = n
        self.order = [2 * r if r < n // 2 else 2 * (n - 1 - r) + 1 for r in range(n)]
        self.cw = [(self.order[r], self.order[(r + 1) % n]) for r in range(n)]
        self.ccw = [(b, a) for a, b in self.cw]
        ctx = lax.axis_index("ctx")
        self.place = jnp.where(ctx % 2 == 0, ctx // 2, n - 1 - ctx // 2)

    def member(self, distance):
        r = (self.place + distance) % self.n
        return jnp.where(r < self.n // 2, 2 * r, 2 * (self.n - 1 - r) + 1)

    def send(self, value, sign):
        return lax.ppermute(value, "ctx", self.cw if sign > 0 else self.ccw)

    def steps(self, sign, long_sign):
        return self.n // 2 if sign == long_sign else self.n - 1 - self.n // 2


class Beats:
    def __init__(self):
        self.streams = []

    def start(self, stream):
        self.streams.append([stream, next(stream)])

    def beat(self, *state):
        flights = [s[1] for s in self.streams]
        flights, state = lax.optimization_barrier((flights, state))
        alive = []
        for (stream, _), flight in zip(self.streams, flights):
            try:
                alive.append([stream, stream.send(flight)])
            except StopIteration:
                pass
        self.streams = alive
        return state

    def until(self, ready, *state):
        while not ready():
            state = self.beat(*state)
        return state


def once(sent, sink, beats=1):
    for _ in range(beats - 1):
        yield None
    sink.append((yield sent))


class Gather:
    def __init__(self, ring, pack, long_sign):
        self.ring, self.pack, self.long_sign = ring, pack, long_sign
        self.own = None
        self.got = {}

    def value(self):
        if self.own is None:
            self.own = self.pack()
        return self.own

    def stream(self, sign):
        value = self.value()
        for step in range(1, self.ring.steps(sign, self.long_sign) + 1):
            value = yield self.ring.send(value, sign)
            self.got[-sign * step] = value

    def ready(self):
        return len(self.got) == self.ring.n - 1

    def chunks(self):
        distances = sorted(self.got)
        chunks = [self.own] + [self.got[d] for d in distances]
        owners = [self.ring.member(d) for d in [0] + distances]
        return chunks, jnp.stack(owners).astype(jnp.int32)


def gather_stream(gathers, sign):
    for g in gathers:
        yield from g.stream(sign)


class Scatter:
    def __init__(self, ring, part_of, long_sign):
        self.ring, self.part_of, self.long_sign = ring, part_of, long_sign
        self.got = {}

    def stream(self, sign):
        got = None
        for step in range(self.ring.steps(sign, self.long_sign), 0, -1):
            part = self.part_of(self.ring.member(sign * step))
            if got is not None:
                part = part + got.astype(F32)
            got = yield self.ring.send(part.astype(BF16), sign)
        self.got[sign] = got

    def ready(self):
        return len(self.got) == 2

    def total(self):
        return self.part_of(lax.axis_index("ctx")) + self.got[1].astype(F32) + self.got[-1].astype(F32)


def scatter_stream(queue, sign):
    i = 0
    while True:
        while i == len(queue):
            yield None
        if queue[i] is None:
            return
        yield from queue[i].stream(sign)
        i += 1


def assemble(chunks, owners, pieces):
    n = len(chunks)

    def kernel(owner_ref, *refs):
        ins, outs = refs[:n], refs[n:]
        for i in range(n):
            for (r0, r1, c0, c1), out in zip(pieces, outs):
                out[owner_ref[i]] = ins[i][r0:r1, c0:c1]

    return pl.pallas_call(
        kernel,
        out_shape=tuple(jax.ShapeDtypeStruct((n, r1 - r0, c1 - c0), BF16) for r0, r1, c0, c1 in pieces),
        in_specs=[pl.BlockSpec(memory_space=pltpu.SMEM)] + [pl.BlockSpec(memory_space=pltpu.VMEM)] * n,
        out_specs=tuple(pl.BlockSpec(memory_space=pltpu.VMEM) for _ in pieces),
    )(owners, *chunks)


SLOT_ORDER = (2, 1, 3, 0, 4)


def head_parts(value):
    lane = lax.broadcasted_iota(jnp.int32, value.shape, 1)
    zero = jnp.zeros_like(value)
    return jnp.where(lane < HD, value, zero), jnp.where(lane < HD, zero, value)


def attend(queries, keys_values, query_ids, key_ids, need, seq):
    _, tokens, width = queries.shape
    pairs = width // 128

    def kernel(need_ref, q_ref, k_ref, v_ref, qseg_ref, kseg_ref, mixed_ref, lse_ref, top, total, acc):
        heads = head_parts(q_ref[0])
        qseg = qseg_ref[0]

        def one_slot(slot, first):
            keys = k_ref[0, slot]
            values = v_ref[0, slot]
            mask = kseg_ref[0, slot * tokens : (slot + 1) * tokens] == qseg
            for h in range(2):
                scores = jnp.where(mask, dot(keys, heads[h], NT), -1e30)
                best = jnp.max(scores, axis=0, keepdims=True)
                if not first:
                    old = top[h]
                    best = jnp.maximum(best, old)
                expo = jnp.exp(scores - best)
                sums = jnp.sum(expo, axis=0, keepdims=True)
                part = dot(values, expo.astype(BF16), TN)
                if not first:
                    shrink = jnp.exp(old - best)
                    sums = sums + total[h] * shrink
                    part = part + acc[h] * shrink
                top[h] = best
                total[h] = sums
                acc[h] = part

        one_slot(OWN, True)
        for slot in SLOT_ORDER[1:]:

            @pl.when(need_ref[seq * SLOTS + slot] > 0)
            def _(slot=slot):
                one_slot(slot, False)

        halves = [acc[h][HD * h : HD * (h + 1)] / total[h] for h in range(2)]
        mixed_ref[0] = jnp.concatenate(halves, axis=0).T.astype(BF16)
        lse_ref[0] = jnp.concatenate([top[h] + jnp.log(total[h]) for h in range(2)], axis=0)

    return pl.pallas_call(
        kernel,
        grid_spec=pltpu.PrefetchScalarGridSpec(
            num_scalar_prefetch=1,
            grid=(pairs,),
            in_specs=[
                pl.BlockSpec((1, tokens, 128), lambda p, n: (seq, 0, p)),
                pl.BlockSpec((1, SLOTS, tokens, 128), lambda p, n: (seq, 0, 0, p)),
                pl.BlockSpec((1, SLOTS, tokens, 128), lambda p, n: (seq, 0, 0, pairs + p)),
                pl.BlockSpec((1, 1, tokens), lambda p, n: (seq, 0, 0)),
                pl.BlockSpec((1, SLOTS * tokens, 1), lambda p, n: (seq, 0, 0)),
            ],
            out_specs=[
                pl.BlockSpec((1, tokens, 128), lambda p, n: (0, 0, p)),
                pl.BlockSpec((1, 2, tokens), lambda p, n: (p, 0, 0)),
            ],
            scratch_shapes=[
                pltpu.VMEM((2, 1, tokens), F32),
                pltpu.VMEM((2, 1, tokens), F32),
                pltpu.VMEM((2, 128, tokens), F32),
            ],
        ),
        out_shape=(
            jax.ShapeDtypeStruct((1, tokens, width), BF16),
            jax.ShapeDtypeStruct((pairs, 2, tokens), F32),
        ),
    )(need, queries, keys_values, keys_values, query_ids, key_ids)


def attend_back(queries, keys_values, grad_mixed, lse, query_ids, key_ids, need, seq):
    _, tokens, width = queries.shape
    pairs = width // 128

    def kernel(
        need_ref, q_ref, k_ref, v_ref, g_ref, lse_ref, qseg_ref, kseg_ref,
        gq_ref, gk_ref, gv_ref, probs_ref, grads_ref, inner_ref, acc,
    ):
        heads = head_parts(q_ref[0])
        grads = head_parts(g_ref[0])
        qseg = qseg_ref[0]

        def when(slot, body):
            if slot == OWN:
                body()
            else:
                pl.when(need_ref[seq * SLOTS + slot] > 0)(body)

        def probabilities(slot):
            mask = kseg_ref[0, slot * tokens : (slot + 1) * tokens] == qseg
            for h in range(2):
                scores = jnp.where(mask, dot(k_ref[0, slot], heads[h], NT), -1e30)
                probs = jnp.exp(scores - lse_ref[0, h : h + 1])
                grad_probs = dot(v_ref[0, slot], grads[h], NT)
                part = jnp.sum(probs * grad_probs, axis=0, keepdims=True)
                probs_ref[h, slot] = probs
                grads_ref[h, slot] = grad_probs
                inner_ref[h] = part if slot == OWN else inner_ref[h] + part

        def gradients(slot):
            key_grad = value_grad = None
            for h in range(2):
                probs = probs_ref[h, slot]
                grad_scores = (probs * (grads_ref[h, slot] - inner_ref[h])).astype(BF16)
                part = dot(k_ref[0, slot], grad_scores, TN)
                acc[h] = part if slot == OWN else acc[h] + part
                key_part = dot(grad_scores, heads[h], NN)
                value_part = dot(probs.astype(BF16), grads[h], NN)
                key_grad = key_part if h == 0 else key_grad + key_part
                value_grad = value_part if h == 0 else value_grad + value_part
            gk_ref[0, slot] = key_grad.astype(BF16)
            gv_ref[0, slot] = value_grad.astype(BF16)

        for slot in SLOT_ORDER:
            when(slot, lambda slot=slot: probabilities(slot))
        for slot in SLOT_ORDER:
            when(slot, lambda slot=slot: gradients(slot))
            if slot != OWN:

                @pl.when(need_ref[seq * SLOTS + slot] == 0)
                def _(slot=slot):
                    gk_ref[0, slot] = jnp.zeros((tokens, 128), BF16)
                    gv_ref[0, slot] = jnp.zeros((tokens, 128), BF16)

        joined = jnp.concatenate([acc[h][HD * h : HD * (h + 1)] for h in range(2)], axis=0)
        gq_ref[0] = joined.T.astype(BF16) * (HD**-0.5)

    row_spec = pl.BlockSpec((1, tokens, 128), lambda p, n: (seq, 0, p))
    out_rows = pl.BlockSpec((1, tokens, 128), lambda p, n: (0, 0, p))
    out_slots = pl.BlockSpec((1, SLOTS, tokens, 128), lambda p, n: (0, 0, 0, p))
    return pl.pallas_call(
        kernel,
        grid_spec=pltpu.PrefetchScalarGridSpec(
            num_scalar_prefetch=1,
            grid=(pairs,),
            in_specs=[
                row_spec,
                pl.BlockSpec((1, SLOTS, tokens, 128), lambda p, n: (seq, 0, 0, p)),
                pl.BlockSpec((1, SLOTS, tokens, 128), lambda p, n: (seq, 0, 0, pairs + p)),
                row_spec,
                pl.BlockSpec((1, 2, tokens), lambda p, n: (p, 0, 0)),
                pl.BlockSpec((1, 1, tokens), lambda p, n: (seq, 0, 0)),
                pl.BlockSpec((1, SLOTS * tokens, 1), lambda p, n: (seq, 0, 0)),
            ],
            out_specs=[out_rows, out_slots, out_slots],
            scratch_shapes=[
                pltpu.VMEM((2, SLOTS, tokens, tokens), F32),
                pltpu.VMEM((2, SLOTS, tokens, tokens), F32),
                pltpu.VMEM((2, 1, tokens), F32),
                pltpu.VMEM((2, 128, tokens), F32),
            ],
        ),
        out_shape=(
            jax.ShapeDtypeStruct((1, tokens, width), BF16),
            jax.ShapeDtypeStruct((1, SLOTS, tokens, width), BF16),
            jax.ShapeDtypeStruct((1, SLOTS, tokens, width), BF16),
        ),
    )(need, queries, keys_values, keys_values, grad_mixed, lse, query_ids, key_ids)


def normalize(operand, gain, shift):
    centered = operand - jnp.mean(operand, axis=-1, keepdims=True)
    spread = jnp.mean(centered * centered, axis=-1, keepdims=True)
    return centered * lax.rsqrt(spread + 1e-05) * gain + shift


def normalize_back(operand, gain, grad):
    centered = operand - jnp.mean(operand, axis=-1, keepdims=True)
    spread = jnp.mean(centered * centered, axis=-1, keepdims=True)
    inverse = lax.rsqrt(spread + 1e-05)
    unit = centered * inverse
    scaled = grad * gain
    out = inverse * (
        scaled
        - jnp.mean(scaled, axis=-1, keepdims=True)
        - unit * jnp.mean(scaled * unit, axis=-1, keepdims=True)
    )
    return out, jnp.sum(grad * unit, axis=0), jnp.sum(grad, axis=0)


def column_sums(operand):
    return jnp.sum(operand.astype(F32), axis=0)


def shifts(n, by):
    return [(i, i + by) for i in range(n) if 0 <= i + by < n]


def slot_ids(group_ids, tokens, n):
    ctx = lax.axis_index("ctx")
    per = SEQ // tokens
    odd = ctx % 2 == 1
    blocks = [ctx - 2, ctx ^ 1, ctx, jnp.where(odd, ctx + 1, ctx - 1), ctx + 2]
    out = []
    for block in blocks:
        inside = (block >= 0) & (block < n) & (block // per == ctx // per)
        start = jnp.clip(block, 0, n - 1) * tokens
        out.append(jnp.where(inside, lax.dynamic_slice_in_dim(group_ids, start, tokens), -1))
    return jnp.stack(out)


def local(
    hidden_in,
    segment_ids,
    query_weight,
    query_bias,
    key_weight,
    value_weight,
    value_bias,
    output_weight,
    output_bias,
    first_gain,
    first_shift,
    inner_weight,
    inner_bias,
    outer_weight,
    outer_bias,
    second_gain,
    second_shift,
    cotangent,
):
    tokens, width = hidden_in.shape
    n = lax.axis_size("ctx")
    ctx = lax.axis_index("ctx")
    dp = lax.axis_index("dp")
    core = dp % 2
    x = dp // 2
    half = width // 2
    ff = inner_weight.shape[2]
    per = width // n
    quarter = ff // (4 * n)
    wide = ff // 4
    scale = HD**-0.5
    ring = Ring(n)
    beats = Beats()
    odd = ctx % 2 == 1
    beside_pairs = [(i, i ^ 1) for i in range(n)]

    vectors = [
        query_bias, value_bias, output_bias, first_gain, first_shift,
        outer_bias, second_gain, second_shift, inner_bias,
    ]
    vector_size = LAYERS * (8 * per + ff // n)
    vector_rows = -(-vector_size // (4 * half * 16)) * 16

    def attention_pack(layer):
        parts = [
            lax.dynamic_slice_in_dim(w[layer], core * half, half, 1).astype(BF16)
            for w in (query_weight, key_weight, value_weight, output_weight)
        ]
        pack = jnp.concatenate(parts, axis=1)
        if layer == 0:
            flat = jnp.concatenate([v.astype(BF16) for v in vectors], axis=1).reshape(-1)
            flat = jnp.pad(flat, (0, vector_rows * 4 * half - vector_size))
            pack = jnp.concatenate([pack, flat.reshape(vector_rows, 4 * half)], axis=0)
        return pack

    def inner_pack(layer):
        block = inner_weight[layer].reshape(per, n, 4, quarter)
        block = lax.dynamic_index_in_dim(block, core * 2 + x, 2, keepdims=False)
        return block.astype(BF16).reshape(per, wide)

    def outer_pack(layer, place):
        block = outer_weight[layer].reshape(4, quarter, width)
        return lax.dynamic_index_in_dim(block, core * 2 + place, 0, keepdims=False).astype(BF16)

    attn = [Gather(ring, lambda l=l: attention_pack(l), 1) for l in range(LAYERS)]
    inner_w = [Gather(ring, lambda l=l: inner_pack(l), -1) for l in range(LAYERS)]
    outer_w = [
        Gather(ring, lambda: outer_pack(0, x), 1),
        Gather(ring, lambda: jnp.concatenate([outer_pack(1, x), outer_pack(1, 1 - x)], axis=0), -1),
    ]
    order = [attn[0], inner_w[0], outer_w[0], inner_w[1], attn[1], outer_w[1]]
    beats.start(gather_stream(order, 1))
    beats.start(gather_stream(order, -1))

    swapped = {}

    def pass_on(gather, name, parts):
        chunks, owners = gather.chunks()
        (whole,) = assemble(chunks, owners, [(0, per if name[0] == "i" else quarter, 0, width)])
        whole = whole.reshape(-1, width)
        swapped[name] = [whole, []]
        rows = whole.shape[0] // parts
        for i in range(parts):
            beats.start(later(whole[i * rows : (i + 1) * rows], swapped[name][1], i))

    def later(value, sink, wait):
        for _ in range(wait):
            yield None
        sink.append((yield x_swap(value)))

    def has(name, parts):
        return name in swapped and len(swapped[name][1]) == parts

    def watch(*state):
        state = beats.beat(*state)
        for gather, name in ((inner_w[0], "i0"), (outer_w[0], "o0"), (inner_w[1], "i1")):
            if gather.ready() and name not in swapped:
                pass_on(gather, name, 4)
        return state

    def watch_until(ready, *state):
        while not ready():
            state = watch(*state)
        return state

    own_ids = segment_ids.reshape(-1)
    key_ids = jnp.stack([slot_ids(own_ids, tokens, n), slot_ids(core_swap(own_ids), tokens, n)])
    query_ids = key_ids[:, OWN]
    low, high = jnp.min(query_ids, axis=1), jnp.max(query_ids, axis=1)
    need = (jnp.max(key_ids, axis=2) >= low[:, None]) & (jnp.min(key_ids, axis=2) <= high[:, None])
    need = need.astype(jnp.int32).reshape(-1)
    query_ids = query_ids.reshape(2, 1, tokens)
    key_ids = key_ids.reshape(2, SLOTS * tokens, 1)

    def both(value):
        return jnp.concatenate([value, core_swap(value)], axis=0)

    def sum_cores(partial):
        return partial[:tokens] + core_swap(partial[tokens:])

    def window_streams(own, sink):
        def ends():
            behind = yield lax.ppermute(own, "ctx", shifts(n, 2))
            sink["behind"] = behind

        def front():
            ahead = yield lax.ppermute(own, "ctx", shifts(n, -2))
            sink["ahead"] = ahead

        def side():
            beside = yield lax.ppermute(own, "ctx", beside_pairs)
            sink["beside"] = beside
            send = jnp.where(odd, sink["behind"], sink["ahead"])
            sink["across"] = yield lax.ppermute(send, "ctx", beside_pairs)

        for stream in (ends(), front(), side()):
            beats.start(stream)

    def window_of(own, sink):
        blocks = [sink["behind"], sink["beside"], own, sink["across"], sink["ahead"]]
        mine = jnp.stack(blocks)
        return jnp.stack([mine, core_swap(mine)])

    hidden = hidden_in.astype(F32)
    rounded = hidden_in
    sink = {}
    window_streams(rounded, sink)
    saved = []
    gathered_vectors = None
    weights = []
    for layer in range(LAYERS):
        hidden, rounded = watch_until(
            lambda layer=layer, sink=sink: attn[layer].ready() and "across" in sink, hidden, rounded
        )
        window = window_of(rounded, sink)
        chunks, owners = attn[layer].chunks()
        pieces = [(0, per, 0, 3 * half), (0, per, 3 * half, 4 * half)]
        if layer == 0:
            pieces.append((per, per + vector_rows, 0, 4 * half))
            qkv, out_half, vector_block = assemble(chunks, owners, pieces)
            gathered_vectors = vector_block.reshape(n, -1)[:, :vector_size].reshape(n, LAYERS, -1)
        else:
            qkv, out_half = assemble(chunks, owners, pieces)
        qkv = qkv.reshape(width, 3 * half)
        out_half = out_half.reshape(width, half)
        theirs = core_swap(lax.dynamic_slice_in_dim(out_half, (1 - core) * half, half, 0))
        wo = ordered(core, lax.dynamic_slice_in_dim(out_half, core * half, half, 0), theirs, 1)
        wq, wkv = qkv[:, :half], qkv[:, half:]

        block = gathered_vectors[:, layer].astype(F32)
        flat_vectors = [block[:, i * per : (i + 1) * per].reshape(-1) for i in range(8)]
        b1 = lax.dynamic_index_in_dim(block[:, 8 * per :].reshape(n, 2, 2, quarter), core, 1, keepdims=False)
        b1_mine = lax.dynamic_index_in_dim(b1, x, 1, keepdims=False).reshape(-1)
        b1_other = lax.dynamic_index_in_dim(b1, 1 - x, 1, keepdims=False).reshape(-1)
        bq, bv = [lax.dynamic_slice_in_dim(v, core * half, half) for v in flat_vectors[:2]]
        bo, g1, c1, b2, g2, c2 = flat_vectors[2:]

        rows = window[:, OWN].reshape(2 * tokens, width)
        flat = window.reshape(2 * SLOTS * tokens, width)
        queries = ((dot(rows, wq, NN) + bq) * scale).astype(BF16).reshape(2, tokens, half)
        kv_bias = jnp.concatenate([jnp.zeros_like(bv), bv])
        keys_values = (dot(flat, wkv, NN) + kv_bias).astype(BF16).reshape(2, SLOTS, tokens, width)
        hidden, queries, keys_values = watch(hidden, queries, keys_values)
        mixed0, lse0 = attend(queries, keys_values, query_ids, key_ids, need, 0)
        hidden, mixed0, queries, keys_values = watch(hidden, mixed0, queries, keys_values)
        mixed1, lse1 = attend(queries, keys_values, query_ids, key_ids, need, 1)
        hidden, mixed0, mixed1 = watch(hidden, mixed0, mixed1)
        mixed = jnp.concatenate([mixed0, mixed1], axis=0).reshape(2 * tokens, half)
        first_sum = hidden + (sum_cores(dot(mixed, wo, NN)) + bo)
        settled = normalize(first_sum, g1, c1)
        settled_rows = both(settled.astype(BF16))
        name = str(layer)
        settled, settled_rows = watch_until(lambda: has("i" + name, 4), settled, settled_rows)
        w1_mine, w1_other = swapped["i" + name][0], jnp.concatenate(swapped["i" + name][1], axis=0)

        def feed(weight, bias, settled_rows=settled_rows):
            inner = dot(settled_rows, weight, NN) + bias
            cdf = (1.0 + lax.erf(inner * (0.5**0.5))) * 0.5
            slope = cdf + inner * jnp.exp(-0.5 * inner * inner) * (0.5 / jnp.pi) ** 0.5
            return (inner * cdf).astype(BF16), slope

        act_mine, slope_mine = feed(w1_mine, b1_mine)
        act_other, slope_other = feed(w1_other, b1_other)
        if layer == 0:
            settled, act_mine, act_other = watch_until(lambda: has("o0", 4), settled, act_mine, act_other)
            w2_mine, w2_other = swapped["o0"][0], jnp.concatenate(swapped["o0"][1], axis=0)
        else:
            settled, act_mine, act_other = watch_until(outer_w[1].ready, settled, act_mine, act_other)
            chunks, owners = outer_w[1].chunks()
            w2_mine, w2_other = assemble(
                chunks, owners, [(0, quarter, 0, width), (quarter, 2 * quarter, 0, width)]
            )
            w2_mine, w2_other = w2_mine.reshape(-1, width), w2_other.reshape(-1, width)
        outer = dot(act_mine, w2_mine, NN) + dot(act_other, w2_other, NN)
        second_sum = settled + (sum_cores(outer) + b2)
        hidden = normalize(second_sum, g2, c2)
        weights.append((wq, wkv, wo, w1_mine, w1_other, w2_mine, w2_other, g1, g2))
        saved.append(
            (
                flat, rows, queries, keys_values, lse0, lse1, mixed, first_sum, settled_rows,
                slope_mine, slope_other, act_mine, act_other, second_sum,
            )
        )
        if layer + 1 < LAYERS:
            rounded = hidden.astype(BF16)
            sink = {}
            window_streams(rounded, sink)
    output = hidden.astype(BF16)

    queue = []
    beats.start(scatter_stream(queue, 1))
    beats.start(scatter_stream(queue, -1))
    finished = []

    def owned(grad, joined):
        low_sum = grad.astype(BF16)
        return low_sum.astype(F32) + joined(x_swap(low_sum)).astype(F32)

    def turn(value):
        return jnp.concatenate([value[quarter:], value[:quarter]], axis=0)

    jobs = []

    def settle():
        for job in list(jobs):
            if job[0].ready():
                job[1](job[0].total())
                jobs.remove(job)

    def step(*state):
        state = beats.beat(*state)
        settle()
        return state

    outputs = [dict() for _ in range(LAYERS)]
    vector_grads = [None] * LAYERS
    grad = cotangent.astype(F32)
    for layer in reversed(range(LAYERS)):
        wq, wkv, wo, w1_mine, w1_other, w2_mine, w2_other, g1, g2 = weights[layer]
        (
            flat, rows, queries, keys_values, lse0, lse1, mixed, first_sum, settled_rows,
            slope_mine, slope_other, act_mine, act_other, second_sum,
        ) = saved[layer]
        out = outputs[layer]
        grad_second, d_g2, d_c2 = normalize_back(second_sum, g2, grad)
        go = grad_second.astype(BF16)
        go_rows = both(go)
        d_b2 = column_sums(go)
        dw2_mine = dot(act_mine, go_rows, TN, BF16).reshape(n, quarter, width)
        dw2_other = dot(act_other, go_rows, TN, BF16).reshape(n, quarter, width)

        def outer_part(t, parts=(dw2_mine, dw2_other)):
            return jnp.concatenate(
                [lax.dynamic_index_in_dim(p, t, 0, keepdims=False) for p in parts], axis=0
            ).astype(F32)

        def outer_done(total, out=out):
            low_sum = total.astype(BF16)

            def finish():
                came = yield x_swap(low_sum)
                whole = low_sum.astype(F32) + turn(came).astype(F32)
                whole = jnp.where(x == 0, whole, turn(whole))
                out["outer"] = ordered(core, whole, core_swap(whole), 0)

            beats.start(finish())

        queue.append(Scatter(ring, outer_part, 1))
        jobs.append((queue[-1], outer_done))
        grad_second, go_rows = step(grad_second, go_rows)
        gi_other = (slope_other * dot(go_rows, w2_other, NT)).astype(BF16)
        give = dot(settled_rows, gi_other, TN, BF16)
        gi_mine = (slope_mine * dot(go_rows, w2_mine, NT)).astype(BF16)
        came = []
        for i in range(4):
            rows_i = width // 4
            beats.start(later(give[i * rows_i : (i + 1) * rows_i], came, i))
        grad_second, gi_mine, gi_other = step(grad_second, gi_mine, gi_other)
        keep = dot(settled_rows, gi_mine, TN, BF16).reshape(n, per, wide)
        d_b1 = [column_sums(g).reshape(n, 1, 1, quarter) for g in (gi_mine, gi_other)]
        gset = grad_second + sum_cores(dot(gi_mine, w1_mine, NT) + dot(gi_other, w1_other, NT))
        grad_first, d_g1, d_c1 = normalize_back(first_sum, g1, gset)
        gb = grad_first.astype(BF16)
        gb_rows = both(gb)
        d_bo = column_sums(gb)
        grad_first, gb_rows, keep = step(grad_first, gb_rows, keep)
        d_wo = dot(mixed, gb_rows, TN, BF16)
        gm = dot(gb_rows, wo, NT, BF16).reshape(2, tokens, half)
        give = lax.dynamic_slice_in_dim(d_wo, (1 - core) * half, half, 1)
        d_wo = ordered(core, lax.dynamic_slice_in_dim(d_wo, core * half, half, 1), core_swap(give), 0)
        grad_first, gm, d_wo = step(grad_first, gm, d_wo)
        gq0, gk0, gv0 = attend_back(queries, keys_values, gm, lse0, query_ids, key_ids, need, 0)
        grad_first, gm, gq0, gk0, gv0 = step(grad_first, gm, gq0, gk0, gv0)

        def inner_part(t, keep=keep, came=came):
            other = jnp.concatenate(came, axis=0).reshape(n, per, wide)
            mine = lax.dynamic_index_in_dim(keep, t, 0, keepdims=False).astype(F32)
            return mine + lax.dynamic_index_in_dim(other, t, 0, keepdims=False).astype(F32)

        def inner_done(total, out=out):
            low_sum = total.astype(BF16)

            def finish():
                came = yield x_swap(low_sum)
                pair = ordered(x, low_sum.reshape(per, n, 1, quarter), came.reshape(per, n, 1, quarter), 2)
                pair = pair.reshape(per, n, 1, 2 * quarter)
                out["inner"] = ordered(core, pair, core_swap(pair), 2).reshape(per, ff).astype(F32)

            beats.start(finish())

        gq1, gk1, gv1 = attend_back(queries, keys_values, gm, lse1, query_ids, key_ids, need, 1)
        while len(came) < 4:
            grad_first, gq0, gk0, gv0, gq1, gk1, gv1 = step(grad_first, gq0, gk0, gv0, gq1, gk1, gv1)
        queue.append(Scatter(ring, inner_part, -1))
        jobs.append((queue[-1], inner_done))

        gq = jnp.concatenate([gq0, gq1], axis=0).reshape(2 * tokens, half)
        gk = jnp.concatenate([gk0, gk1], axis=0).reshape(2 * SLOTS * tokens, half)
        gv = jnp.concatenate([gv0, gv1], axis=0).reshape(2 * SLOTS * tokens, half)
        pieces = [d.reshape(n, per, half) for d in (
            dot(rows, gq, TN, BF16), dot(flat, gk, TN, BF16), dot(flat, gv, TN, BF16), d_wo)]

        def spread(value):
            return lax.dynamic_update_slice_in_dim(jnp.zeros((width,), F32), value, core * half, 0)

        d_bq, d_bv = spread(column_sums(gq)), spread(column_sums(gv))
        b1_grad = ordered(x, d_b1[0], d_b1[1], 2).reshape(n, 1, 2 * quarter)
        b1_grad = lax.dynamic_update_slice_in_dim(jnp.zeros((n, 2, 2 * quarter), F32), b1_grad, core, 1)
        vector_grads[layer] = jnp.concatenate(
            [v.reshape(n, per) for v in (d_bq, d_bv, d_bo, d_g1, d_c1, d_b2, d_g2, d_c2)]
            + [b1_grad.reshape(n, ff // n)],
            axis=1,
        )
        if layer == 0:
            tail = jnp.concatenate(vector_grads, axis=1)
            tail = jnp.pad(tail, ((0, 0), (0, vector_rows * 4 * half - vector_size)))
            tail = tail.reshape(n, vector_rows, 4 * half)

        def attention_part(t, pieces=pieces, layer=layer):
            part = jnp.concatenate(
                [lax.dynamic_index_in_dim(p, t, 0, keepdims=False) for p in pieces], axis=1
            ).astype(F32)
            if layer == 0:
                part = jnp.concatenate([part, lax.dynamic_index_in_dim(tail, t, 0, keepdims=False)], axis=0)
            return part

        def attention_done(total, out=out, layer=layer):
            low_sum = total.astype(BF16)

            def finish():
                came = yield x_swap(low_sum)
                whole = low_sum.astype(F32) + came.astype(F32)
                peer = core_swap(whole)
                out["attn"] = [
                    ordered(core, whole[:per, i * half : (i + 1) * half], peer[:per, i * half : (i + 1) * half], 1)
                    for i in range(4)
                ]
                if layer == 0:
                    out["vectors"] = (whole[per:] + peer[per:]).reshape(-1)[:vector_size].reshape(LAYERS, -1)

            beats.start(finish())

        queue.append(Scatter(ring, attention_part, 1))
        jobs.append((queue[-1], attention_done))
        grad_first, gq, gk, gv = step(grad_first, gq, gk, gv)
        du_rows = dot(gq, wq, NT)
        du = (dot(gk, wkv[:, :half], NT) + dot(gv, wkv[:, half:], NT)).reshape(2, SLOTS, tokens, width)
        du = du.at[:, OWN].add(du_rows.reshape(2, tokens, width)).astype(BF16)
        parts = du[0].astype(F32) + core_swap(du[1]).astype(F32)
        grad_first, parts = step(grad_first, parts)
        back = {}

        def send(name, value, pairs):
            def stream():
                back[name] = (yield lax.ppermute(value.astype(BF16), "ctx", pairs)).astype(F32)

            beats.start(stream())

        send("across", parts[3], beside_pairs)
        send("beside", parts[1], beside_pairs)
        (own_part,) = step(grad_first + parts[2])
        behind = parts[0] + jnp.where(odd, back["across"], 0.0)
        ahead = parts[4] + jnp.where(odd, 0.0, back["across"])
        send("ahead", behind, shifts(n, -2))
        send("behind", ahead, shifts(n, 2))
        (own_part,) = step(own_part + back["beside"])
        grad = own_part + back["ahead"] + back["behind"]
    queue.append(None)
    while beats.streams or jobs:
        step()

    fields = outputs[0]["vectors"]
    own_vectors = [fields[:, i * per : (i + 1) * per] for i in range(8)] + [fields[:, 8 * per :]]
    d_bq, d_bv, d_bo, d_g1, d_c1, d_b2, d_g2, d_c2, d_b1 = own_vectors
    dq, dk, dv, do = [jnp.stack([o["attn"][i] for o in outputs]) for i in range(4)]
    d1 = jnp.stack([o["inner"] for o in outputs])
    d2 = jnp.stack([o["outer"] for o in outputs])
    return (
        output,
        grad.astype(BF16),
        dq, d_bq, dk, dv, d_bv, do, d_bo, d_g1, d_c1, d1, d_b1, d2, d_b2, d_g2, d_c2,
    )


def solution(mesh):
    tokens = P(("dp", "ctx"), None)
    matrix = P(None, "ctx", None)
    vector = P(None, "ctx")
    params = (
        matrix, vector, matrix, matrix, vector, matrix, vector, vector,
        vector, matrix, vector, matrix, vector, vector, vector,
    )
    return jax.shard_map(
        local,
        mesh=mesh,
        in_specs=(tokens, P("dp", None, None)) + params + (tokens,),
        out_specs=(tokens, tokens) + params,
        check_vma=False,
    )
```

time: 1920 us -> 1080 us (0.56)
  Pallas kernels: 836 us -> 84.8 us
  waiting for transfers between devices: 467 us -> 394 us
  local copies, waits for them, and re-layouts: 108 us -> 165 us
  blocking collectives: 39.8 us -> 0 us
    pallas_call x8 -> x12, Pallas kernels: 836 us -> 84.8 us  [the longest x4 43 us: attend(): pl.pallas_call(kernel, grid_spec=pltpu.PrefetchScalarGridSpec(num_scalar_...]
    psum x1 -> x0, waiting for transfers between devices: 100 us -> none  [local(): sums = lax.psum(jnp.stack(vector_grads), ('dp', 'ctx'))]
    all_gather x1 -> x0, blocking collectives: 39.8 us -> none  [local(): gathered_vectors = lax.all_gather(vector_pack, 'ctx', axis=0)]
    unnamed x312 -> x601, local copies, waits for them, and re-layouts: 32.4 us -> 68 us
    ppermute x86 -> x100, waiting for transfers between devices: 253 us -> 287 us  [the longest x84 211 us: send(): return lax.ppermute(value, 'ctx', self.cw if sign > 0 else self.ccw)]
    pallas_call x0 -> x2, local copies, waits for them, and re-layouts: none -> 23.7 us  [attend_back(): pl.pallas_call(kernel, grid_spec=pltpu.PrefetchScalarGridSpec(num_scalar_...]
    convert_element_type x47 -> x48, other arithmetic: 49.6 us -> 27.7 us  [the longest x28 18.9 us: stream(): got = (yield self.ring.send(part.astype(BF16), sign))]
    dot_general x34 -> x46, matrix products: 134 us -> 125 us  [dot(): lax.dot_general(left, right, (dims, ((), ())), preferred_element_type=F32)]
  transfers between devices with their start and end apart: 136 -> 153, of which waited for: 58 -> 70; matrix products, arithmetic and copies ran while one was open for 16% -> 27% of each run, Pallas kernels for 44% -> 8%
where the time goes in v2:
time: 1080 us; the launch traced here: 1070 us
  waiting for transfers between devices  394 us (36%)
  starting transfers between devices  176 us (16%)
  local copies, waits for them, and re-layouts  165 us (15%)
  matrix products  125 us (12%)
  other arithmetic  114 us (11%)
  Pallas kernels  84.8 us (8%)
    ppermute x84, waiting for transfers between devices, send(): return lax.ppermute(value, 'ctx', self.cw if sign > 0 else self.ccw)  211 us
    dot_general x46, matrix products, dot(): lax.dot_general(left, right, (dims, ((), ())), preferred_element_type=F32)  125 us
    ppermute x84, starting transfers between devices, send(): return lax.ppermute(value, 'ctx', self.cw if sign > 0 else self.ccw)  123 us
    ppermute x26, waiting for transfers between devices, x_swap(): return lax.ppermute(value, 'dp', X_PAIRS)  98.8 us
    unnamed x601, local copies, waits for them, and re-layouts  68 us
    pallas_call x4, Pallas kernels, attend(): pl.pallas_call(kernel, grid_spec=pltpu.PrefetchScalarGridSpec(num_scalar_...  43 us
    ppermute x2, waiting for transfers between devices, side(): sink['across'] = (yield lax.ppermute(send, 'ctx', beside_pairs))  28.4 us
    ppermute x2, waiting for transfers between devices, side(): beside = (yield lax.ppermute(own, 'ctx', beside_pairs))  25.8 us
  transfers between devices with their start and end apart: 153, of which 70 were waited for; matrix products, arithmetic and copies ran while one was open for 27% of the time, Pallas kernels for 8%

profile of v2, /device:TPU:0, one launch (start us, length us, event | category | flops | bytes accessed | tf_op | source)
XLA Modules:
  0.0 1065.6 jit_solution(9161115164616499125)
XLA Ops:
  24.6 17.4 %collective-permute-done.10 = bf16[256,1024]{1,0:T(8,128)(2,1)} collective-permute-done((bf16[256,1024]{1,0:T(8,128)(2,1)S(1)}, bf16[256,1024]{1,0:T(8,128)(2,1)}, u32[]{:S(2)}, u32[]{:S(2)}) %collective-permute-start.10) | collective-permute-done | bytes 524320 | tf_op jit(solution)/shard_map/ppermute | solution.py:518
  47.4 19.9 %collective-permute-done.13 = bf16[256,1024]{1,0:T(8,128)(2,1)S(1)} collective-permute-done((bf16[256,1024]{1,0:T(8,128)(2,1)}, bf16[256,1024]{1,0:T(8,128)(2,1)S(1)}, u32[]{:S(2)}, u32[]{:S(2)}) %collective-permute-start.13) | collective-permute-done | bytes 524320 | tf_op jit(solution)/shard_map/ppermute | solution.py:521
  130.3 9.2 shard_map.306
  148.7 12.3 %shard_map.307 = (bf16[1,256,512]{2,1,0:T(8,128)(2,1)}, f32[4,2,256]{2,1,0:T(2,128)}) custom-call(s32[10]{0:T(128)} %reshape.950.need_ref, bf16[2,256,512]{2,1,0:T(8,128)(2,1)} %bitcast.737, bf16[2,5,256,1024]{3,2,1,0:T(8,128)(2,1)} %bitcast.700, bf16[2,5,256,1024]{3,2,1,0:T(8,128)(2,1)} %bitcast.701, s32[2,1,256]{2,1,0:T(1,128)} %get-tuple-element.657.qseg_ref, ...), custom_call_target="tpu_custom_call" | custom-call | tf_op jit(solution)/shard_map/pallas_call | solution.py:227
  238.3 14.9 %collective-permute-done.41 = bf16[256,1024]{1,0:T(8,128)(2,1)S(1)} collective-permute-done((bf16[256,1024]{1,0:T(8,128)(2,1)S(1)}, bf16[256,1024]{1,0:T(8,128)(2,1)S(1)}, u32[]{:S(2)}, u32[]{:S(2)}) %collective-permute-start.41) | collective-permute-done | bytes 524320 | tf_op jit(solution)/shard_map/ppermute | solution.py:33
  340.5 9.4 collective-permute-done.56.refs_2_
  389.3 9.3 shard_map.312
  408.1 12.3 %shard_map.313 = (bf16[1,256,512]{2,1,0:T(8,128)(2,1)}, f32[4,2,256]{2,1,0:T(2,128)}) custom-call(s32[10]{0:T(128)} %reshape.950.need_ref, bf16[2,256,512]{2,1,0:T(8,128)(2,1)} %bitcast.741, bf16[2,5,256,1024]{3,2,1,0:T(8,128)(2,1)} %bitcast.707, bf16[2,5,256,1024]{3,2,1,0:T(8,128)(2,1)} %bitcast.708, s32[2,1,256]{2,1,0:T(1,128)} %get-tuple-element.657.qseg_ref, ...), custom_call_target="tpu_custom_call" | custom-call | tf_op jit(solution)/shard_map/pallas_call | solution.py:227
  512.7 11.3 %collective-permute-done.79 = bf16[256,1024]{1,0:T(8,128)(2,1)S(1)} collective-permute-done((bf16[256,1024]{1,0:T(8,128)(2,1)}, bf16[256,1024]{1,0:T(8,128)(2,1)S(1)}, u32[]{:S(2)}, u32[]{:S(2)}) %collective-permute-start.79) | collective-permute-done | bytes 524320 | tf_op jit(solution)/shard_map/ppermute | solution.py:33
  543.3 9.6 shard_map.315
  556.2 11.9 %shard_map.317 = (bf16[2,256,512]{2,1,0:T(8,128)(2,1)S(1)}, bf16[1,5,256,512]{3,2,1,0:T(8,128)(2,1)}, bf16[1,5,256,512]{3,2,1,0:T(8,128)(2,1)}) fusion(bf16[2,256,512]{2,1,0:T(8,128)(2,1)S(1)} %constant_dynamic-update-slice_fusion.24, s32[10]{0:T(128)S(1)} %copy-done.237, bf16[2,256,512]{2,1,0:T(8,128)(2,1)S(1)} %bitcast.743, ...), kind=kCustom, calls=%fused_computation.439 | custom fusion | bytes 10496512 | tf_op jit(solution)/shard_map/pallas_call | solution.py:316
  639.5 23.2 %collective-permute-done.94 = bf16[128,1024]{1,0:T(8,128)(2,1)S(1)} collective-permute-done((bf16[128,1024]{1,0:T(8,128)(2,1)S(1)}, bf16[128,1024]{1,0:T(8,128)(2,1)S(1)}, u32[]{:S(2)}, u32[]{:S(2)}) %collective-permute-start.94) | collective-permute-done | bytes 262176 | tf_op jit(solution)/shard_map/ppermute | solution.py:60
  671.0 16.2 %collective-permute-done.98 = bf16[128,1024]{1,0:T(8,128)(2,1)S(1)} collective-permute-done((bf16[128,1024]{1,0:T(8,128)(2,1)S(1)}, bf16[128,1024]{1,0:T(8,128)(2,1)S(1)}, u32[]{:S(2)}, u32[]{:S(2)}) %collective-permute-start.98) | collective-permute-done | bytes 262176 | tf_op jit(solution)/shard_map/ppermute | solution.py:60
  692.2 13.0 %collective-permute-done.101 = bf16[128,1024]{1,0:T(8,128)(2,1)S(1)} collective-permute-done((bf16[128,1024]{1,0:T(8,128)(2,1)S(1)}, bf16[128,1024]{1,0:T(8,128)(2,1)S(1)}, u32[]{:S(2)}, u32[]{:S(2)}) %collective-permute-start.101) | collective-permute-done | bytes 262176 | tf_op jit(solution)/shard_map/ppermute | solution.py:60
  769.3 9.6 shard_map.316
  795.2 11.8 %shard_map.318 = (bf16[2,256,512]{2,1,0:T(8,128)(2,1)S(1)}, bf16[1,5,256,512]{3,2,1,0:T(8,128)(2,1)}, bf16[1,5,256,512]{3,2,1,0:T(8,128)(2,1)}) fusion(bf16[2,256,512]{2,1,0:T(8,128)(2,1)S(1)} %constant_dynamic-update-slice_fusion.30, s32[10]{0:T(128)S(1)} %copy-done.238, bf16[2,256,512]{2,1,0:T(8,128)(2,1)S(1)} %bitcast.739, ...), kind=kCustom, calls=%fused_computation.445 | custom fusion | bytes 10496512 | tf_op jit(solution)/shard_map/pallas_call | solution.py:316
  902.6 9.9 collective-permute-done.126
  912.5 11.2 %collective-permute-done.129 = bf16[256,1024]{1,0:T(8,128)(2,1)S(1)} collective-permute-done((bf16[256,1024]{1,0:T(8,128)(2,1)S(1)}, bf16[256,1024]{1,0:T(8,128)(2,1)S(1)}, u32[]{:S(2)}, u32[]{:S(2)}) %collective-permute-start.129) | collective-permute-done | bytes 524320 | tf_op jit(solution)/shard_map/ppermute | solution.py:782
  923.8 9.0 collective-permute-done.128
  938.7 16.8 %collective-permute-done.130 = bf16[128,1024]{1,0:T(8,128)(2,1)S(1)} collective-permute-done((bf16[128,1024]{1,0:T(8,128)(2,1)S(1)}, bf16[128,1024]{1,0:T(8,128)(2,1)S(1)}, u32[]{:S(2)}, u32[]{:S(2)}) %collective-permute-start.130) | collective-permute-done | bytes 262176 | tf_op jit(solution)/shard_map/ppermute | solution.py:60
  961.1 13.2 %collective-permute-done.137 = bf16[128,1024]{1,0:T(8,128)(2,1)S(1)} collective-permute-done((bf16[128,1024]{1,0:T(8,128)(2,1)S(1)}, bf16[128,1024]{1,0:T(8,128)(2,1)S(1)}, u32[]{:S(2)}, u32[]{:S(2)}) %collective-permute-start.137) | collective-permute-done | bytes 262176 | tf_op jit(solution)/shard_map/ppermute | solution.py:60
  994.8 10.6 collective-permute-done.141
  1009.3 12.4 %collective-permute-done.143 = bf16[144,2048]{1,0:T(8,128)(2,1)S(1)} collective-permute-done((bf16[144,2048]{1,0:T(8,128)(2,1)S(1)}, bf16[144,2048]{1,0:T(8,128)(2,1)S(1)}, u32[]{:S(2)}, u32[]{:S(2)}) %collective-permute-start.143) | collective-permute-done | bytes 589856 | tf_op jit(solution)/shard_map/ppermute | solution.py:60
  1033.1 8.9 collective-permute-done.146
  (1234 shorter events, 756.8 us)
Async XLA Ops:
  12.8 29.2 %collective-permute-start.7 = (bf16[144,2048]{1,0:T(8,128)(2,1)S(1)}, bf16[144,2048]{1,0:T(8,128)(2,1)}, u32[]{:S(2)}, u32[]{:S(2)}) collective-permute-start(bf16[144,2048]{1,0:T(8,128)(2,1)S(1)} %pad_maximum_fusion.25.refs_0_), channel_id=1, source_target_pairs={{2,0},{4,2},{6,4},{7,6},{5,7},{3,5},{1,3},{0,1},{10,8},{12,10},{14... | collective-permute-start | bytes 1769480 | tf_op jit(solution)/shard_map/ppermute | solution.py:60
  96.8 28.7 %collective-permute-start.5 = (bf16[128,1024]{1,0:T(8,128)(2,1)S(1)}, bf16[128,1024]{1,0:T(8,128)(2,1)}, u32[]{:S(2)}, u32[]{:S(2)}) collective-permute-start(bf16[128,1024]{1,0:T(8,128)(2,1)S(1)} %bitcast.804), channel_id=1, source_target_pairs={{0,2},{2,4},{4,6},{6,7},{7,5},{5,3},{3,1},{1,0},{8,10},{10,12},{12... | collective-permute-start | bytes 786440 | tf_op jit(solution)/shard_map/ppermute | solution.py:60
  111.5 34.8 %collective-permute-start.26 = (bf16[512,512]{1,0:T(8,128)(2,1)}, bf16[512,512]{1,0:T(8,128)(2,1)}, u32[]{:S(2)}, u32[]{:S(2)}) collective-permute-start(bf16[512,512]{1,0:T(8,128)(2,1)} %constant_dynamic-slice_fusion.8), channel_id=1, source_target_pairs={{0,8},{8,0},{16,24},{24,16},{1,9},{9,1},{17,25},{25,17},{2,10},{10... | collective-permute-start | bytes 1572872 | tf_op jit(solution)/shard_map/ppermute | solution.py:29
  203.6 34.7 %collective-permute-start.39 = (bf16[128,1024]{1,0:T(8,128)(2,1)S(1)}, bf16[128,1024]{1,0:T(8,128)(2,1)S(1)}, u32[]{:S(2)}, u32[]{:S(2)}) collective-permute-start(bf16[128,1024]{1,0:T(8,128)(2,1)S(1)} %bitcast.806), channel_id=1, source_target_pairs={{0,2},{2,4},{4,6},{6,7},{7,5},{5,3},{3,1},{1,0},{8,10},{10,12},{12... | collective-permute-start | bytes 786440 | tf_op jit(solution)/shard_map/ppermute | solution.py:60
  229.0 29.1 %collective-permute-start.44 = (bf16[256,1024]{1,0:T(8,128)(2,1)S(1)}, bf16[256,1024]{1,0:T(8,128)(2,1)S(1)}, u32[]{:S(2)}, u32[]{:S(2)}) collective-permute-start(bf16[256,1024]{1,0:T(8,128)(2,1)S(1)} %bitcast.832), channel_id=1, source_target_pairs={{0,16},{8,24},{16,0},{24,8},{1,17},{9,25},{17,1},{25,9},{2,18},{10... | collective-permute-start | bytes 1572872 | tf_op jit(solution)/shard_map/ppermute | solution.py:33
  330.0 30.2 %collective-permute-start.61 = (bf16[256,1024]{1,0:T(8,128)(2,1)S(1)}, bf16[256,1024]{1,0:T(8,128)(2,1)}, u32[]{:S(2)}, u32[]{:S(2)}) collective-permute-start(bf16[256,1024]{1,0:T(8,128)(2,1)S(1)} %pad_maximum_fusion.28.refs_0_), channel_id=1, source_target_pairs={{2,0},{4,2},{6,4},{7,6},{5,7},{3,5},{1,3},{0,1},{10,8},{12,10},{14... | collective-permute-start | bytes 1572872 | tf_op jit(solution)/shard_map/ppermute | solution.py:60
  330.9 29.4 %collective-permute-start.62 = (bf16[256,1024]{1,0:T(8,128)(2,1)S(1)}, bf16[256,1024]{1,0:T(8,128)(2,1)S(1)}, u32[]{:S(2)}, u32[]{:S(2)}) collective-permute-start(bf16[256,1024]{1,0:T(8,128)(2,1)S(1)} %bitcast.827), channel_id=1, source_target_pairs={{0,16},{8,24},{16,0},{24,8},{1,17},{9,25},{17,1},{25,9},{2,18},{10... | collective-permute-start | bytes 1572872 | tf_op jit(solution)/shard_map/ppermute | solution.py:33
  497.8 57.6 %collective-permute-start.87 = (bf16[256,1024]{1,0:T(8,128)(2,1)}, bf16[256,1024]{1,0:T(8,128)(2,1)}, u32[]{:S(2)}, u32[]{:S(2)}) collective-permute-start(bf16[256,1024]{1,0:T(8,128)(2,1)} %get-tuple-element.738), channel_id=1, source_target_pairs={{0,16},{8,24},{16,0},{24,8},{1,17},{9,25},{17,1},{25,9},{2,18},{10... | collective-permute-start | bytes 1572872 | tf_op jit(solution)/shard_map/ppermute | solution.py:33
  574.4 58.9 %collective-permute-start.90 = (bf16[128,1024]{1,0:T(8,128)(2,1)}, bf16[128,1024]{1,0:T(8,128)(2,1)}, u32[]{:S(2)}, u32[]{:S(2)}) collective-permute-start(bf16[128,1024]{1,0:T(8,128)(2,1)} %get-tuple-element.672), channel_id=1, source_target_pairs={{2,0},{4,2},{6,4},{7,6},{5,7},{3,5},{1,3},{0,1},{10,8},{12,10},{14... | collective-permute-start | bytes 786440 | tf_op jit(solution)/shard_map/ppermute | solution.py:60
  580.6 52.7 %collective-permute-start.89 = (bf16[128,1024]{1,0:T(8,128)(2,1)}, bf16[128,1024]{1,0:T(8,128)(2,1)}, u32[]{:S(2)}, u32[]{:S(2)}) collective-permute-start(bf16[128,1024]{1,0:T(8,128)(2,1)} %get-tuple-element.673), channel_id=1, source_target_pairs={{0,2},{2,4},{4,6},{6,7},{7,5},{5,3},{3,1},{1,0},{8,10},{10,12},{12... | collective-permute-start | bytes 786440 | tf_op jit(solution)/shard_map/ppermute | solution.py:60
  621.2 71.0 %collective-permute-start.88 = (bf16[128,2048]{1,0:T(8,128)(2,1)S(1)}, bf16[128,2048]{1,0:T(8,128)(2,1)S(1)}, u32[]{:S(2)}, u32[]{:S(2)}) collective-permute-start(bf16[128,2048]{1,0:T(8,128)(2,1)S(1)} %pad_maximum_fusion.34), channel_id=1, source_target_pairs={{0,2},{2,4},{4,6},{6,7},{7,5},{5,3},{3,1},{1,0},{8,10},{10,12},{12... | collective-permute-start | bytes 1572872 | tf_op jit(solution)/shard_map/ppermute | solution.py:60
  633.8 31.0 %collective-permute-start.96 = (bf16[256,1024]{1,0:T(8,128)(2,1)S(1)}, bf16[256,1024]{1,0:T(8,128)(2,1)S(1)}, u32[]{:S(2)}, u32[]{:S(2)}) collective-permute-start(bf16[256,1024]{1,0:T(8,128)(2,1)S(1)} %get-tuple-element.680), channel_id=1, source_target_pairs={{0,1},{1,0},{2,3},{3,2},{4,5},{5,4},{6,7},{7,6},{8,9},{9,8},{10,11... | collective-permute-start | bytes 1572872 | tf_op jit(solution)/shard_map/ppermute | solution.py:782
  634.2 30.6 %collective-permute-start.95 = (bf16[256,1024]{1,0:T(8,128)(2,1)S(1)}, bf16[256,1024]{1,0:T(8,128)(2,1)S(1)}, u32[]{:S(2)}, u32[]{:S(2)}) collective-permute-start(bf16[256,1024]{1,0:T(8,128)(2,1)S(1)} %get-tuple-element.681), channel_id=1, source_target_pairs={{0,1},{1,0},{2,3},{3,2},{4,5},{5,4},{6,7},{7,6},{8,9},{9,8},{10,11... | collective-permute-start | bytes 1572872 | tf_op jit(solution)/shard_map/ppermute | solution.py:782
  637.6 27.2 %collective-permute-start.93 = (bf16[128,1024]{1,0:T(8,128)(2,1)S(1)}, bf16[128,1024]{1,0:T(8,128)(2,1)S(1)}, u32[]{:S(2)}, u32[]{:S(2)}) collective-permute-start(bf16[128,1024]{1,0:T(8,128)(2,1)S(1)} %get-tuple-element.671), channel_id=1, source_target_pairs={{0,2},{2,4},{4,6},{6,7},{7,5},{5,3},{3,1},{1,0},{8,10},{10,12},{12... | collective-permute-start | bytes 786440 | tf_op jit(solution)/shard_map/ppermute | solution.py:60
  687.2 36.4 %collective-permute-start.104 = (bf16[128,2048]{1,0:T(8,128)(2,1)S(1)}, bf16[128,2048]{1,0:T(8,128)(2,1)S(1)}, u32[]{:S(2)}, u32[]{:S(2)}) collective-permute-start(bf16[128,2048]{1,0:T(8,128)(2,1)S(1)} %pad_maximum_fusion.35), channel_id=1, source_target_pairs={{2,0},{4,2},{6,4},{7,6},{5,7},{3,5},{1,3},{0,1},{10,8},{12,10},{14... | collective-permute-start | bytes 1572872 | tf_op jit(solution)/shard_map/ppermute | solution.py:60
  721.3 58.5 %collective-permute-start.116 = (bf16[256,1024]{1,0:T(8,128)(2,1)}, bf16[256,1024]{1,0:T(8,128)(2,1)S(1)}, u32[]{:S(2)}, u32[]{:S(2)}) collective-permute-start(bf16[256,1024]{1,0:T(8,128)(2,1)} %pad_maximum_fusion.36), channel_id=1, source_target_pairs={{0,2},{2,4},{4,6},{6,7},{7,5},{5,3},{3,1},{1,0},{8,10},{10,12},{12... | collective-permute-start | bytes 1572872 | tf_op jit(solution)/shard_map/ppermute | solution.py:60
  793.0 109.6 %collective-permute-start.127 = (bf16[128,1024]{1,0:T(8,128)(2,1)}, bf16[128,1024]{1,0:T(8,128)(2,1)}, u32[]{:S(2)}, u32[]{:S(2)}) collective-permute-start(bf16[128,1024]{1,0:T(8,128)(2,1)} %get-tuple-element.666), channel_id=1, source_target_pairs={{2,0},{4,2},{6,4},{7,6},{5,7},{3,5},{1,3},{0,1},{10,8},{12,10},{14... | collective-permute-start | bytes 786440 | tf_op jit(solution)/shard_map/ppermute | solution.py:60
  793.3 145.3 %collective-permute-start.120 = (bf16[128,1024]{1,0:T(8,128)(2,1)}, bf16[128,1024]{1,0:T(8,128)(2,1)}, u32[]{:S(2)}, u32[]{:S(2)}) collective-permute-start(bf16[128,1024]{1,0:T(8,128)(2,1)} %get-tuple-element.667), channel_id=1, source_target_pairs={{0,2},{2,4},{4,6},{6,7},{7,5},{5,3},{3,1},{1,0},{8,10},{10,12},{12... | collective-permute-start | bytes 786440 | tf_op jit(solution)/shard_map/ppermute | solution.py:60
  812.0 42.5 %collective-permute-start.121 = (bf16[256,1024]{1,0:T(8,128)(2,1)}, bf16[256,1024]{1,0:T(8,128)(2,1)}, u32[]{:S(2)}, u32[]{:S(2)}) collective-permute-start(bf16[256,1024]{1,0:T(8,128)(2,1)} %add_convert_fusion.8), channel_id=1, source_target_pairs={{0,2},{2,4},{4,6},{6,7},{7,5},{5,3},{3,1},{1,0},{8,10},{10,12},{12... | collective-permute-start | bytes 1572872 | tf_op jit(solution)/shard_map/ppermute | solution.py:60
  821.2 33.4 %collective-permute-start.122 = (bf16[256,1024]{1,0:T(8,128)(2,1)}, bf16[256,1024]{1,0:T(8,128)(2,1)}, u32[]{:S(2)}, u32[]{:S(2)}) collective-permute-start(bf16[256,1024]{1,0:T(8,128)(2,1)} %add_convert_fusion.7), channel_id=1, source_target_pairs={{2,0},{4,2},{6,4},{7,6},{5,7},{3,5},{1,3},{0,1},{10,8},{12,10},{14... | collective-permute-start | bytes 1572872 | tf_op jit(solution)/shard_map/ppermute | solution.py:60
  900.3 32.4 %collective-permute-start.128 = (bf16[256,1024]{1,0:T(8,128)(2,1)S(1)}, bf16[256,1024]{1,0:T(8,128)(2,1)S(1)}, u32[]{:S(2)}, u32[]{:S(2)}) collective-permute-start(bf16[256,1024]{1,0:T(8,128)(2,1)S(1)} %get-tuple-element.679), channel_id=1, source_target_pairs={{0,1},{1,0},{2,3},{3,2},{4,5},{5,4},{6,7},{7,6},{8,9},{9,8},{10,11... | collective-permute-start | bytes 1572872 | tf_op jit(solution)/shard_map/ppermute | solution.py:782
  938.6 53.4 %collective-permute-start.148 = (f32[128,2048]{1,0:T(8,128)S(1)}, f32[128,2048]{1,0:T(8,128)S(1)}, u32[]{:S(2)}, u32[]{:S(2)}) collective-permute-start(f32[128,2048]{1,0:T(8,128)S(1)} %convert_add_fusion.5), channel_id=1, source_target_pairs={{0,8},{8,0},{16,24},{24,16},{1,9},{9,1},{17,25},{25,17},{2,10},{10... | collective-permute-start | bytes 3145736 | tf_op jit(solution)/shard_map/ppermute | solution.py:29
  955.5 28.3 %collective-permute-start.134 = (bf16[144,2048]{1,0:T(8,128)(2,1)S(1)}, bf16[144,2048]{1,0:T(8,128)(2,1)S(1)}, u32[]{:S(2)}, u32[]{:S(2)}) collective-permute-start(bf16[144,2048]{1,0:T(8,128)(2,1)S(1)} %pad_maximum_fusion.26), channel_id=1, source_target_pairs={{0,2},{2,4},{4,6},{6,7},{7,5},{5,3},{3,1},{1,0},{8,10},{10,12},{12... | collective-permute-start | bytes 1769480 | tf_op jit(solution)/shard_map/ppermute | solution.py:60
  955.5 28.3 %collective-permute-start.135 = (bf16[144,2048]{1,0:T(8,128)(2,1)S(1)}, bf16[144,2048]{1,0:T(8,128)(2,1)S(1)}, u32[]{:S(2)}, u32[]{:S(2)}) collective-permute-start(bf16[144,2048]{1,0:T(8,128)(2,1)S(1)} %pad_maximum_fusion.27), channel_id=1, source_target_pairs={{2,0},{4,2},{6,4},{7,6},{5,7},{3,5},{1,3},{0,1},{10,8},{12,10},{14... | collective-permute-start | bytes 1769480 | tf_op jit(solution)/shard_map/ppermute | solution.py:60
  (404 other events, 4243.4 us)

commit v3 on v2

v3 whole, which is shorter than its diff:
```python
import jax
import jax.numpy as jnp
from jax import lax
from jax.experimental import pallas as pl
from jax.experimental.pallas import tpu as pltpu
from jax.sharding import PartitionSpec as P

HD = 64
LAYERS = 2
SEQ = 2048
SLOTS = 5
OWN = 2
BF16 = jnp.bfloat16
F32 = jnp.float32
CORE_PAIRS = [(i, i ^ 1) for i in range(4)]
X_PAIRS = [(i, i ^ 2) for i in range(4)]


def dot(left, right, dims, out=F32):
    return lax.dot_general(left, right, (dims, ((), ())), preferred_element_type=F32).astype(out)


NN = ((1,), (0,))
NT = ((1,), (1,))
TN = ((0,), (0,))


def core_swap(value):
    return lax.ppermute(value, "dp", CORE_PAIRS)


def x_swap(value):
    return lax.ppermute(value, "dp", X_PAIRS)


def tie(value, *tokens):
    return lax.optimization_barrier((value,) + tokens)[0]


def ordered(place, mine, peer, axis):
    first = jnp.where(place == 0, mine, peer)
    second = jnp.where(place == 0, peer, mine)
    return jnp.concatenate([first, second], axis=axis)


class Ring:
    def __init__(self, n):
        self.n = n
        self.order = [2 * r if r < n // 2 else 2 * (n - 1 - r) + 1 for r in range(n)]
        self.cw = [(self.order[r], self.order[(r + 1) % n]) for r in range(n)]
        self.ccw = [(b, a) for a, b in self.cw]
        ctx = lax.axis_index("ctx")
        self.place = jnp.where(ctx % 2 == 0, ctx // 2, n - 1 - ctx // 2)

    def member(self, distance):
        r = (self.place + distance) % self.n
        return jnp.where(r < self.n // 2, 2 * r, 2 * (self.n - 1 - r) + 1)

    def send(self, value, sign):
        return lax.ppermute(value, "ctx", self.cw if sign > 0 else self.ccw)

    def steps(self, sign, long_sign):
        return self.n // 2 if sign == long_sign else self.n - 1 - self.n // 2


class Hold:
    def __init__(self, value, beats):
        self.value, self.beats = value, beats


class Beats:
    def __init__(self):
        self.streams = []
        self.kept = []

    def start(self, stream):
        self.streams.append([stream, self.flight(next(stream))])

    def flight(self, sent):
        return sent if isinstance(sent, Hold) else Hold(sent, 1)

    def keep(self, place, name):
        self.kept.append((place, name))

    def beat(self, *state):
        for _, flight in self.streams:
            flight.beats -= 1
        if self.streams and not self.kept and not state and all(f.beats > 0 for _, f in self.streams):
            least = min(f.beats for _, f in self.streams)
            for _, flight in self.streams:
                flight.beats -= least
        due = [s for s in self.streams if s[1].beats == 0]
        kept, self.kept = self.kept, []
        values = ([s[1].value for s in due], [place[name] for place, name in kept], state)
        flights, places, state = lax.optimization_barrier(values)
        for (place, name), value in zip(kept, places):
            place[name] = value
        for entry, flight in zip(due, flights):
            try:
                entry[1] = self.flight(entry[0].send(flight))
            except StopIteration:
                self.streams.remove(entry)
        return state

    def until(self, ready, *state):
        while not ready():
            state = self.beat(*state)
        return state


class Gather:
    def __init__(self, ring, pack, long_sign):
        self.ring, self.pack, self.long_sign = ring, pack, long_sign
        self.own = None
        self.got = {}

    def value(self):
        if self.own is None:
            self.own = self.pack()
        return self.own

    def stream(self, sign):
        value = self.value()
        for step in range(1, self.ring.steps(sign, self.long_sign) + 1):
            value = yield self.ring.send(value, sign)
            self.got[-sign * step] = value

    def ready(self):
        return len(self.got) == self.ring.n - 1

    def chunks(self):
        distances = sorted(self.got)
        chunks = [self.own] + [self.got[d] for d in distances]
        owners = [self.ring.member(d) for d in [0] + distances]
        return chunks, jnp.stack(owners).astype(jnp.int32)


def gather_stream(gathers, sign):
    for g in gathers:
        yield from g.stream(sign)


class Scatter:
    def __init__(self, ring, part_of, long_sign):
        self.ring, self.part_of, self.long_sign = ring, part_of, long_sign
        self.got = {}

    def stream(self, sign):
        got = None
        for step in range(self.ring.steps(sign, self.long_sign), 0, -1):
            part = self.part_of(self.ring.member(sign * step))
            if got is not None:
                part = part + got.astype(F32)
            got = yield self.ring.send(part.astype(BF16), sign)
        self.got[sign] = got

    def ready(self):
        return len(self.got) == 2

    def total(self):
        return self.part_of(lax.axis_index("ctx")) + self.got[1].astype(F32) + self.got[-1].astype(F32)


def busy(us):
    return pl.CostEstimate(flops=int(us * 1.1e9), bytes_accessed=int(us * 3e6), transcendentals=0)


def whole(space=pltpu.VMEM):
    return pl.BlockSpec(memory_space=space)


def pack_layer(weights, inner_weight, outer_weight, layer, core, x, extra):
    query, key, value, out = weights
    _, per, width = query.shape
    half = width // 2
    ff = inner_weight.shape[2]
    n = ff // outer_weight.shape[1]
    quarter = ff // (4 * n)
    more = 0 if extra is None else extra.shape[0]
    picks = [core * 2 + x]

    def kernel(sel_ref, q_ref, k_ref, v_ref, o_ref, *refs):
        pack_ref = refs[-1]
        for p in range(half // 128):
            cols = slice(128 * p, 128 * p + 128)
            pack_ref[:per, 256 * p : 256 * p + 128] = k_ref[0, :, cols].astype(BF16)
            pack_ref[:per, 256 * p + 128 : 256 * p + 256] = v_ref[0, :, cols].astype(BF16)
        pack_ref[:per, 2 * half : 3 * half] = q_ref[0].astype(BF16)
        pack_ref[:per, 3 * half :] = o_ref[0].astype(BF16)
        if more:
            pack_ref[per:] = refs[0][...]

    attention = pl.pallas_call(
        kernel,
        cost_estimate=busy(2),
        grid_spec=pltpu.PrefetchScalarGridSpec(
            num_scalar_prefetch=1,
            grid=(1,),
            in_specs=[pl.BlockSpec((1, per, half), lambda i, c: (layer, 0, c[0]))] * 4 + [whole()] * (more > 0),
            out_specs=pl.BlockSpec((per + more, 4 * half), lambda i, c: (0, 0)),
        ),
        out_shape=jax.ShapeDtypeStruct((per + more, 4 * half), BF16),
    )(core.reshape(1).astype(jnp.int32), query, key, value, out, *([extra] if more else []))

    if quarter % 128:
        feeds = []
        for pick in picks:
            first = inner_weight[layer].reshape(per, n, 4, quarter)
            first = lax.dynamic_index_in_dim(first, pick, 2, keepdims=False).reshape(per, width)
            second = outer_weight[layer].reshape(4, quarter, width)
            second = lax.dynamic_index_in_dim(second, pick, 0, keepdims=False)
            feeds.append(jnp.concatenate([first, second], axis=1).astype(BF16))
        return attention, *feeds

    def feed_kernel(sel_ref, *refs):
        for i, dest in enumerate(refs[-1:]):
            for j in range(n):
                dest[:, j * quarter : (j + 1) * quarter] = refs[i * (n + 1) + j][0].astype(BF16)
            dest[:, width:] = refs[i * (n + 1) + n][0].astype(BF16)

    blocks, args = [], []
    for i in range(1):
        for j in range(n):
            blocks.append(pl.BlockSpec((1, per, quarter), lambda _, c, i=i, j=j: (layer, 0, 4 * j + c[i])))
            args.append(inner_weight)
        blocks.append(pl.BlockSpec((1, quarter, width), lambda _, c, i=i: (layer, c[i], 0)))
        args.append(outer_weight)
    feeds = pl.pallas_call(
        feed_kernel,
        cost_estimate=busy(3),
        grid_spec=pltpu.PrefetchScalarGridSpec(
            num_scalar_prefetch=1,
            grid=(1,),
            in_specs=blocks,
            out_specs=[pl.BlockSpec((per, 4 * half), lambda i, c: (0, 0))],
        ),
        out_shape=[jax.ShapeDtypeStruct((per, 4 * half), BF16)],
    )(jnp.stack(picks).astype(jnp.int32), *args)
    return attention, *feeds


def vector_rows(vectors):
    rows = 16
    total = sum(v.shape[1] for v in vectors)
    if any(v.shape[1] % 128 for v in vectors):
        flat = jnp.concatenate([v.astype(BF16) for v in vectors], axis=1)
        return jnp.pad(flat, ((0, rows - LAYERS), (0, 2048 - total)))

    def kernel(*refs):
        out = refs[-1]
        row = lax.broadcasted_iota(jnp.int32, (rows, 1), 0)
        at = 0
        for ref in refs[:-1]:
            k = ref.shape[1]
            value = jnp.zeros((rows, k), F32)
            for l in range(LAYERS):
                value = jnp.where(row == l, ref[l : l + 1, :], value)
            out[:, at : at + k] = value.astype(BF16)
            at += k
        if at < 2048:
            out[:, at:] = jnp.zeros((rows, 2048 - at), BF16)

    return pl.pallas_call(
        kernel,
        cost_estimate=busy(1),
        in_specs=[whole()] * len(vectors),
        out_specs=whole(),
        out_shape=jax.ShapeDtypeStruct((rows, 2048), BF16),
    )(*vectors)


def assemble(chunks, owners, pieces):
    n = len(chunks)
    wide = chunks[0].shape[1]
    kinds = sorted(set((rows, at) for rows, at, _, _ in pieces))

    def kernel(owner_ref, *refs):
        ins, outs = refs[: n * len(kinds)], refs[n * len(kinds) :]
        for i in range(n):
            for (rows, at, first, size), out in zip(pieces, outs):
                out[owner_ref[i]] = ins[n * kinds.index((rows, at)) + i][:, first : first + size]

    blocks = [pl.BlockSpec((rows, wide), lambda _, o, at=at: (at, 0)) for rows, at in kinds for _ in range(n)]
    return pl.pallas_call(
        kernel,
        cost_estimate=busy(5),
        grid_spec=pltpu.PrefetchScalarGridSpec(
            num_scalar_prefetch=1, grid=(1,), in_specs=blocks, out_specs=[whole() for _ in pieces]
        ),
        out_shape=tuple(jax.ShapeDtypeStruct((n, rows, size), BF16) for rows, _, _, size in pieces),
    )(owners, *(chunks * len(kinds)))


SLOT_ORDER = (2, 1, 3, 0, 4)


def two_heads(value):
    lane = lax.broadcasted_iota(jnp.int32, value.shape, 1)
    zero = jnp.zeros_like(value)
    return jnp.concatenate([jnp.where(lane < HD, value, zero), jnp.where(lane < HD, zero, value)], axis=0)


def own_lanes(value, tokens):
    return jnp.concatenate([value[:HD, :tokens], value[HD:, tokens:]], axis=0).T


def attend(window, weights, query_bias, value_bias, query_ids, key_ids, need, seq):
    tokens, width = window[0].shape
    half = width // 2
    pairs = half // 128

    def kernel(need_ref, *refs):
        u = refs[:SLOTS]
        (wkv_ref, wq_ref, bq_ref, bv_ref, qseg_ref, kseg_ref, q_ref, kv_ref, mixed_ref, lse_ref, top, total, acc) = refs[SLOTS:]
        value_lane = lax.broadcasted_iota(jnp.int32, (1, 256), 1) >= 128
        bias = jnp.where(value_lane, jnp.concatenate([bv_ref[...], bv_ref[...]], axis=1), 0.0)
        q = ((dot(u[OWN][...], wq_ref[...], NN) + bq_ref[...]) * (HD**-0.5)).astype(BF16)
        q_ref[...] = q
        heads = two_heads(q)
        qseg = jnp.concatenate([qseg_ref[seq], qseg_ref[seq]], axis=1)

        def one_slot(slot):
            kv = (dot(u[slot][...], wkv_ref[...], NN) + bias).astype(BF16)
            kv_ref[slot] = kv
            mask = kseg_ref[seq, slot * tokens : (slot + 1) * tokens] == qseg
            scores = jnp.where(mask, dot(kv[:, :128], heads, NT), -1e30)
            best = jnp.max(scores, axis=0, keepdims=True)
            if slot != OWN:
                old = top[...]
                best = jnp.maximum(best, old)
            expo = jnp.exp(scores - best)
            sums = jnp.sum(expo, axis=0, keepdims=True)
            part = dot(kv[:, 128:], expo.astype(BF16), TN)
            if slot != OWN:
                shrink = jnp.exp(old - best)
                sums = sums + total[...] * shrink
                part = part + acc[...] * shrink
            top[...] = best
            total[...] = sums
            acc[...] = part

        one_slot(OWN)
        for slot in SLOT_ORDER[1:]:
            pl.when(need_ref[seq * SLOTS + slot] > 0)(lambda slot=slot: one_slot(slot))
        mixed_ref[...] = own_lanes(acc[...] / total[...], tokens).astype(BF16)
        lse_ref[0] = top[...] + jnp.log(total[...])

    return pl.pallas_call(
        kernel,
        cost_estimate=busy(16),
        grid_spec=pltpu.PrefetchScalarGridSpec(
            num_scalar_prefetch=1,
            grid=(pairs,),
            in_specs=[whole()] * SLOTS
            + [
                pl.BlockSpec((width, 256), lambda p, n: (0, p)),
                pl.BlockSpec((width, 128), lambda p, n: (0, 2 * pairs + p)),
                pl.BlockSpec((1, 128), lambda p, n: (0, p)),
                pl.BlockSpec((1, 128), lambda p, n: (0, p)),
                whole(),
                whole(),
            ],
            out_specs=[
                pl.BlockSpec((tokens, 128), lambda p, n: (0, p)),
                pl.BlockSpec((SLOTS, tokens, 256), lambda p, n: (0, 0, p)),
                pl.BlockSpec((tokens, 128), lambda p, n: (0, p)),
                pl.BlockSpec((1, 1, 2 * tokens), lambda p, n: (p, 0, 0)),
            ],
            scratch_shapes=[
                pltpu.VMEM((1, 2 * tokens), F32),
                pltpu.VMEM((1, 2 * tokens), F32),
                pltpu.VMEM((128, 2 * tokens), F32),
            ],
        ),
        out_shape=(
            jax.ShapeDtypeStruct((tokens, half), BF16),
            jax.ShapeDtypeStruct((SLOTS, tokens, width), BF16),
            jax.ShapeDtypeStruct((tokens, half), BF16),
            jax.ShapeDtypeStruct((pairs, 1, 2 * tokens), F32),
        ),
    )(need, *window, weights, weights, query_bias, value_bias, query_ids, key_ids)


def attend_back(window, weights, out_rows, kept, grad_rows, query_ids, key_ids, need):
    tokens, width = window[0].shape
    half = width // 2
    pairs = half // 128
    blocks = 2 * SLOTS

    def kernel(need_ref, *refs):
        u = refs[:blocks]
        wkv_ref, wq_ref, wo_ref, *rest = refs[blocks:]
        saved_refs = (rest[:4], rest[4:8])
        (
            g_ref, qseg_ref, kseg_ref,
            dw_ref, dwo_ref, dbq_ref, dbv_ref, own_ref, peer_ref,
            probs_ref, grads_ref, inner_ref, acc, gkv, gq, u_all, sems,
        ) = rest[8:]
        pair = pl.program_id(0)
        copies = [
            pltpu.make_async_copy(u[i], u_all.at[pl.ds(i * tokens, tokens)], sems.at[i]) for i in range(blocks)
        ]

        @pl.when(pair == 0)
        def _():
            for c in copies:
                c.start()

        mixed = [refs_of[2][...] for refs_of in saved_refs]
        dwo_ref[...] = (dot(mixed[0], g_ref[:tokens], TN) + dot(mixed[1], g_ref[tokens:], TN)).astype(BF16)
        kv_cols = pl.ds(pl.multiple_of(pair * 256, 256), 256)
        q_cols = pl.ds(pl.multiple_of(pair * 128, 128), 128)
        for seq in range(2):
            q_ref, kv_ref, _, lse_ref = saved_refs[seq]
            gm = dot(g_ref[seq * tokens : (seq + 1) * tokens], wo_ref[...], NT, BF16)
            heads = two_heads(q_ref[...])
            grads = two_heads(gm)
            qseg = jnp.concatenate([qseg_ref[seq], qseg_ref[seq]], axis=1)

            def when(slot, body, seq=seq):
                if slot == OWN:
                    body()
                else:
                    pl.when(need_ref[seq * SLOTS + slot] > 0)(body)

            def probabilities(slot, seq=seq, heads=heads, grads=grads, qseg=qseg, kv_ref=kv_ref, lse_ref=lse_ref):
                mask = kseg_ref[seq, slot * tokens : (slot + 1) * tokens] == qseg
                scores = jnp.where(mask, dot(kv_ref[slot, :, :128], heads, NT), -1e30)
                probs = jnp.exp(scores - lse_ref[0])
                grad_probs = dot(kv_ref[slot, :, 128:], grads, NT)
                part = jnp.sum(probs * grad_probs, axis=0, keepdims=True)
                probs_ref[slot] = probs
                grads_ref[slot] = grad_probs
                inner_ref[...] = part if slot == OWN else inner_ref[...] + part

            def gradients(slot, seq=seq, heads=heads, grads=grads, kv_ref=kv_ref):
                probs = probs_ref[slot]
                grad_scores = (probs * (grads_ref[slot] - inner_ref[...])).astype(BF16)
                part = dot(kv_ref[slot, :, :128], grad_scores, TN)
                acc[...] = part if slot == OWN else acc[...] + part
                gk = dot(grad_scores, heads, NN, BF16)
                gv = dot(probs.astype(BF16), grads, NN, BF16)
                at = (seq * SLOTS + slot) * tokens
                gkv[at : at + tokens, kv_cols] = jnp.concatenate([gk, gv], axis=1)

            for slot in SLOT_ORDER:
                when(slot, lambda slot=slot: probabilities(slot))
            for slot in SLOT_ORDER:
                when(slot, lambda slot=slot: gradients(slot))
                if slot != OWN:

                    @pl.when(need_ref[seq * SLOTS + slot] == 0)
                    def _(at=(seq * SLOTS + slot) * tokens):
                        gkv[at : at + tokens, kv_cols] = jnp.zeros((tokens, 256), BF16)

            gq[seq * tokens : (seq + 1) * tokens, q_cols] = own_lanes(acc[...], tokens).astype(BF16) * (HD**-0.5)

        @pl.when(pair == pairs - 1)
        def _():
            for c in copies:
                c.wait()
            dw_ref[:, :width] = dot(u_all[...], gkv[...], TN, BF16)
            dw_ref[:, width:] = (
                dot(u_all[OWN * tokens : (OWN + 1) * tokens], gq[:tokens], TN)
                + dot(u_all[(SLOTS + OWN) * tokens : (SLOTS + OWN + 1) * tokens], gq[tokens:], TN)
            ).astype(BF16)
            dbq_ref[...] = jnp.sum(gq[...].astype(F32), axis=0, keepdims=True)
            for p in range(pairs):
                values = gkv[:, 256 * p + 128 : 256 * p + 256].astype(F32)
                dbv_ref[:, 128 * p : 128 * p + 128] = jnp.sum(values, axis=0, keepdims=True)
            for seq, out in ((0, own_ref), (1, peer_ref)):
                for slot in range(SLOTS):
                    at = (seq * SLOTS + slot) * tokens

                    def part(at=at):
                        return dot(gkv[at : at + tokens], wkv_ref[...], NT)

                    if slot == OWN:
                        own = dot(gq[seq * tokens : (seq + 1) * tokens], wq_ref[...], NT)
                        out[slot] = (part() + own).astype(BF16)
                        continue
                    wanted = need_ref[seq * SLOTS + slot] > 0

                    @pl.when(wanted)
                    def _(slot=slot, out=out, part=part):
                        out[slot] = part().astype(BF16)

                    @pl.when(jnp.logical_not(wanted))
                    def _(slot=slot, out=out):
                        out[slot] = jnp.zeros((tokens, width), BF16)

    saved_specs = [
        pl.BlockSpec((tokens, 128), lambda p, n: (0, p)),
        pl.BlockSpec((SLOTS, tokens, 256), lambda p, n: (0, 0, p)),
        pl.BlockSpec((tokens, 128), lambda p, n: (0, p)),
        pl.BlockSpec((1, 1, 2 * tokens), lambda p, n: (p, 0, 0)),
    ]
    full = lambda *shape: pl.BlockSpec(shape, lambda p, n: (0,) * len(shape))
    return pl.pallas_call(
        kernel,
        cost_estimate=busy(40),
        grid_spec=pltpu.PrefetchScalarGridSpec(
            num_scalar_prefetch=1,
            grid=(pairs,),
            in_specs=[whole(pl.ANY)] * blocks
            + [full(width, width), pl.BlockSpec((width, half), lambda p, n: (0, 2)), pl.BlockSpec((128, width), lambda p, n: (p, 0))]
            + saved_specs * 2
            + [whole(), whole(), whole()],
            out_specs=[
                full(width, width + half),
                pl.BlockSpec((128, width), lambda p, n: (p, 0)),
                full(1, half),
                full(1, half),
                full(SLOTS, tokens, width),
                full(SLOTS, tokens, width),
            ],
            scratch_shapes=[
                pltpu.VMEM((SLOTS, tokens, 2 * tokens), F32),
                pltpu.VMEM((SLOTS, tokens, 2 * tokens), F32),
                pltpu.VMEM((1, 2 * tokens), F32),
                pltpu.VMEM((128, 2 * tokens), F32),
                pltpu.VMEM((blocks * tokens, width), BF16),
                pltpu.VMEM((2 * tokens, half), BF16),
                pltpu.VMEM((blocks * tokens, width), BF16),
                pltpu.SemaphoreType.DMA((blocks,)),
            ],
        ),
        out_shape=(
            jax.ShapeDtypeStruct((width, width + 2 * half), BF16),
            jax.ShapeDtypeStruct((half, width), BF16),
            jax.ShapeDtypeStruct((1, half), F32),
            jax.ShapeDtypeStruct((1, half), F32),
            jax.ShapeDtypeStruct((SLOTS, tokens, width), BF16),
            jax.ShapeDtypeStruct((SLOTS, tokens, width), BF16),
        ),
    )(need, *window, weights, weights, out_rows, *kept[0], *kept[1], grad_rows, query_ids, key_ids)


def with_output_gradient(grads, mine, theirs, core):
    width, columns = grads.shape
    half = width // 2

    def kernel(core_ref, _, mine_ref, theirs_ref, out_ref):
        at = pl.multiple_of(core_ref[0] * half, 128)
        out_ref[pl.ds(at, half)] = mine_ref[...]
        out_ref[pl.ds(pl.multiple_of((1 - core_ref[0]) * half, 128), half)] = theirs_ref[...]

    return pl.pallas_call(
        kernel,
        cost_estimate=busy(2),
        grid_spec=pltpu.PrefetchScalarGridSpec(
            num_scalar_prefetch=1,
            grid=(1,),
            in_specs=[
                whole(pl.ANY),
                pl.BlockSpec((half, half), lambda i, c: (0, c[0])),
                pl.BlockSpec((half, half), lambda i, c: (0, 0)),
            ],
            out_specs=pl.BlockSpec((width, half), lambda i, c: (0, 3)),
        ),
        out_shape=jax.ShapeDtypeStruct((width, columns), BF16),
        input_output_aliases={1: 0},
    )(core.reshape(1).astype(jnp.int32), grads, mine, theirs)


def feed_gradient(settled, grad_inner, activated, grad_outer):
    rows, width = settled[0].shape
    wide = activated[0].shape[1]

    def kernel(*refs):
        (a0, a1, gi0, gi1, b0, b1, go0, go1, out_ref, sum_ref) = refs
        i = pl.program_id(0)

        @pl.when(i == 0)
        def _():
            out_ref[...] = (dot(a0[...], gi0[...], TN) + dot(a1[...], gi1[...], TN)).astype(BF16)
            total = jnp.sum(gi0[...].astype(F32), axis=0, keepdims=True)
            sum_ref[...] = total + jnp.sum(gi1[...].astype(F32), axis=0, keepdims=True)

        @pl.when(i == 1)
        def _():
            out_ref[...] = (dot(b0[...], go0[...], TN) + dot(b1[...], go1[...], TN)).astype(BF16)

    return pl.pallas_call(
        kernel,
        cost_estimate=busy(6),
        grid=(2,),
        in_specs=[whole()] * 8,
        out_specs=[pl.BlockSpec((width, wide), lambda i: (0, i)), pl.BlockSpec((1, wide), lambda i: (0, 0))],
        out_shape=[jax.ShapeDtypeStruct((width, 2 * wide), BF16), jax.ShapeDtypeStruct((1, wide), F32)],
    )(*settled, *grad_inner, *activated, *grad_outer)


def vector_grad_rows(grads, core, x, n):
    width = grads[0][2].shape[1]
    half = width // 2
    per = width // n
    wide = grads[0][8].shape[1]
    quarter = wide // n
    if per % 128 or quarter % 128:
        rows = []
        for g in grads:
            halves = [lax.dynamic_update_slice(jnp.zeros((1, width), F32), v, (0, core * half)) for v in g[:2]]
            b1 = jnp.zeros((n, 4, quarter), F32)
            b1 = lax.dynamic_update_slice(b1, g[8].reshape(n, 1, quarter), (0, core * 2 + x, 0))
            rows.append(
                jnp.concatenate([v.reshape(n, per) for v in halves + list(g[2:8])] + [b1.reshape(n, -1)], axis=1)
            )
        block = jnp.stack(rows, axis=1)
        return jnp.pad(block, ((0, 0), (0, 16 - LAYERS), (0, 2048 - block.shape[2])))

    def kernel(sel_ref, *refs):
        out = refs[-1]
        out[...] = jnp.zeros_like(out)
        core_at = sel_ref[0] * (n // 2)
        for l in range(LAYERS):
            mine = refs[9 * l : 9 * l + 9]
            for i in range(2):
                for t in range(n // 2):
                    out[core_at + t, l : l + 1, i * per : (i + 1) * per] = mine[i][:, t * per : (t + 1) * per]
            for i in range(2, 8):
                for t in range(n):
                    out[t, l : l + 1, i * per : (i + 1) * per] = mine[i][:, t * per : (t + 1) * per]
            at = pl.multiple_of(8 * per + sel_ref[1] * quarter, 128)
            for t in range(n):
                out[t, l : l + 1, pl.ds(at, quarter)] = mine[8][:, t * quarter : (t + 1) * quarter]

    return pl.pallas_call(
        kernel,
        cost_estimate=busy(2),
        in_specs=[whole(pltpu.SMEM)] + [whole()] * (9 * LAYERS),
        out_specs=whole(),
        out_shape=jax.ShapeDtypeStruct((n, 16, 2048), F32),
    )(jnp.stack([core, core * 2 + x]).astype(jnp.int32), *[v for g in grads for v in g])


def into_layer(kernel, name, layer, before, shapes, blocks, sel, inputs, in_specs, grid):
    held = [] if before is None else list(before)

    def body(sel_ref, *refs):
        kernel(sel_ref, *refs[len(held) :])

    return pl.pallas_call(
        body,
        cost_estimate=busy(4),
        name=name,
        grid_spec=pltpu.PrefetchScalarGridSpec(
            num_scalar_prefetch=1,
            grid=grid,
            in_specs=[whole(pl.ANY)] * len(held) + in_specs,
            out_specs=blocks,
        ),
        out_shape=shapes,
        input_output_aliases={1 + i: i for i in range(len(held))},
    )(sel, *held, *inputs)


def finish_feed(layer, before, pieces, core, x):
    per = pieces[0].shape[0]
    wide = width = pieces[0].shape[1] // 2
    n = lax.axis_size("ctx")
    quarter = wide // n
    places = jnp.stack([core * 2 + x, core * 2 + 1 - x, (1 - core) * 2 + x, (1 - core) * 2 + 1 - x]).astype(jnp.int32)
    shapes = (
        jax.ShapeDtypeStruct((LAYERS, per, 4 * wide), F32),
        jax.ShapeDtypeStruct((LAYERS, 4 * per, width), F32),
    )
    if quarter % 128:
        first = jnp.zeros((4, per, n, quarter), F32)
        second = jnp.zeros((4, per, width), F32)
        for i, piece in enumerate(pieces):
            piece = piece.astype(F32)
            first = lax.dynamic_update_index_in_dim(first, piece[:, :wide].reshape(per, n, quarter), places[i], 0)
            second = lax.dynamic_update_index_in_dim(second, piece[:, wide:], places[i], 0)
        first = jnp.transpose(first, (1, 2, 0, 3)).reshape(1, per, 4 * wide)
        second = second.reshape(1, 4 * per, width)
        base = [jnp.zeros(s.shape, F32) for s in shapes] if before is None else before
        return tuple(lax.dynamic_update_slice(b, v, (layer, 0, 0)) for b, v in zip(base, (first, second)))

    def kernel(sel_ref, a, b, c, d, first, second):
        for i, ref in enumerate((a, b, c, d)):
            at = pl.multiple_of(sel_ref[i] * quarter, 128)
            for j in range(n):
                cols = pl.ds(4 * j * quarter + at, quarter)
                first[0, :, cols] = ref[:, j * quarter : (j + 1) * quarter].astype(F32)
            second[0, pl.ds(pl.multiple_of(sel_ref[i] * per, 8), per), :] = ref[:, wide:].astype(F32)

    return into_layer(
        kernel, "finish_feed", layer, before, shapes,
        tuple(pl.BlockSpec((1,) + s.shape[1:], lambda i, s: (layer, 0, 0)) for s in shapes),
        places, pieces, [whole()] * 4, (1,),
    )


def finish_attention(layer, before, sums, core, per):
    rows, columns = sums[0].shape
    half = columns // 4
    pairs = half // 128
    shape = jax.ShapeDtypeStruct((LAYERS, per, 2 * half), F32)
    more = rows > per

    def kernel(sel_ref, a, b, c, d, q_out, k_out, v_out, o_out, *extra):
        for i, (low, came) in enumerate(((a, b), (c, d))):
            at = pl.multiple_of((sel_ref[0] if i == 0 else 1 - sel_ref[0]) * half, 128)

            def part(start, size, low=low, came=came):
                cols = slice(start, start + size)
                return low[:per, cols].astype(F32) + came[:per, cols].astype(F32)

            for p in range(pairs):
                k_out[0, :, pl.ds(at + 128 * p, 128)] = part(256 * p, 128)
                v_out[0, :, pl.ds(at + 128 * p, 128)] = part(256 * p + 128, 128)
            q_out[0, :, pl.ds(at, half)] = part(2 * half, half)
            o_out[0, :, pl.ds(at, half)] = part(3 * half, half)
        if more:
            first = a[per:].astype(F32) + b[per:].astype(F32)
            extra[0][...] = first + (c[per:].astype(F32) + d[per:].astype(F32))

    block = pl.BlockSpec((1, per, 2 * half), lambda i, s: (layer, 0, 0))
    shapes, blocks = (shape,) * 4, (block,) * 4
    if more:
        shapes += (jax.ShapeDtypeStruct((rows - per, columns), F32),)
        blocks += (pl.BlockSpec((rows - per, columns), lambda i, s: (0, 0)),)
    return into_layer(
        kernel, "finish_attention", layer, before, shapes, blocks,
        core.reshape(1).astype(jnp.int32), sums, [whole()] * 4, (1,),
    )


def normalize(operand, gain, shift):
    centered = operand - jnp.mean(operand, axis=-1, keepdims=True)
    spread = jnp.mean(centered * centered, axis=-1, keepdims=True)
    return centered * lax.rsqrt(spread + 1e-05) * gain + shift


def normalize_back(operand, gain, grad):
    centered = operand - jnp.mean(operand, axis=-1, keepdims=True)
    spread = jnp.mean(centered * centered, axis=-1, keepdims=True)
    inverse = lax.rsqrt(spread + 1e-05)
    unit = centered * inverse
    scaled = grad * gain
    out = inverse * (
        scaled
        - jnp.mean(scaled, axis=-1, keepdims=True)
        - unit * jnp.mean(scaled * unit, axis=-1, keepdims=True)
    )
    return out, jnp.sum(grad * unit, axis=0), jnp.sum(grad, axis=0)


def column_sums(operand):
    return jnp.sum(operand.astype(F32), axis=0)


def shifts(n, by):
    return [(i, i + by) for i in range(n) if 0 <= i + by < n]


def slot_ids(group_ids, tokens, n):
    ctx = lax.axis_index("ctx")
    per = SEQ // tokens
    odd = ctx % 2 == 1
    blocks = [ctx - 2, ctx ^ 1, ctx, jnp.where(odd, ctx + 1, ctx - 1), ctx + 2]
    out = []
    for block in blocks:
        inside = (block >= 0) & (block < n) & (block // per == ctx // per)
        start = jnp.clip(block, 0, n - 1) * tokens
        out.append(jnp.where(inside, lax.dynamic_slice_in_dim(group_ids, start, tokens), -1))
    return jnp.stack(out)


def local(
    hidden_in,
    segment_ids,
    query_weight,
    query_bias,
    key_weight,
    value_weight,
    value_bias,
    output_weight,
    output_bias,
    first_gain,
    first_shift,
    inner_weight,
    inner_bias,
    outer_weight,
    outer_bias,
    second_gain,
    second_shift,
    cotangent,
):
    tokens, width = hidden_in.shape
    n = lax.axis_size("ctx")
    ctx = lax.axis_index("ctx")
    dp = lax.axis_index("dp")
    core = dp % 2
    x = dp // 2
    half = width // 2
    ff = inner_weight.shape[2]
    per = width // n
    quarter = ff // (4 * n)
    wide = ff // 4
    ring = Ring(n)
    beats = Beats()
    odd = ctx % 2 == 1
    beside_pairs = [(i, i ^ 1) for i in range(n)]
    core_index = core.reshape(1).astype(jnp.int32)

    vectors = [
        query_bias, value_bias, output_bias, first_gain, first_shift,
        outer_bias, second_gain, second_shift, inner_bias,
    ]
    vector_size = 8 * per + ff // n
    matrices = (query_weight, key_weight, value_weight, output_weight)

    extra = vector_rows(vectors)
    packs = [
        pack_layer(matrices, inner_weight, outer_weight, layer, core, x, extra if layer == 0 else None)
        for layer in range(LAYERS)
    ]
    attn_in = Gather(ring, lambda: packs[0][0], 1)
    for sign in (1, -1):
        beats.start(attn_in.stream(sign))

    arrived = {}

    def native_gathers():
        feed = yield packs[0][1]
        feed = yield feed
        for name, pack, held_beats in (("f0", feed, 3), ("a1", packs[1][0], 2), ("f1", packs[1][1], 3)):
            arrived[name] = yield Hold(lax.all_gather(pack, "ctx", axis=0, tiled=True), held_beats)

    beats.start(native_gathers())

    watch, watch_until = beats.beat, beats.until

    own_ids = segment_ids.reshape(-1)
    key_ids = jnp.stack([slot_ids(own_ids, tokens, n), slot_ids(core_swap(own_ids), tokens, n)])
    query_ids = key_ids[:, OWN]
    low, high = jnp.min(query_ids, axis=1), jnp.max(query_ids, axis=1)
    need = (jnp.max(key_ids, axis=2) >= low[:, None]) & (jnp.min(key_ids, axis=2) <= high[:, None])
    need = need.astype(jnp.int32).reshape(-1)
    query_ids = query_ids.reshape(2, 1, tokens)
    key_ids = key_ids.reshape(2, SLOTS * tokens, 1)

    def both(value):
        return jnp.concatenate([value, core_swap(value)], axis=0)

    def far(value):
        beyond = x_swap(value)
        return jnp.concatenate([beyond, core_swap(beyond)], axis=0)

    def pair_sum(partial):
        return partial[:tokens] + core_swap(partial[tokens:].astype(BF16)).astype(F32)

    def sum_group(partial_near, partial_far):
        beyond = x_swap(pair_sum(partial_far).astype(BF16)).astype(F32)
        return pair_sum(partial_near) + beyond

    def sum_cores(partial):
        return partial[:tokens] + core_swap(partial[tokens:])

    def window_streams(own, sink):
        def behind():
            sink["behind"] = yield lax.ppermute(own, "ctx", shifts(n, 2))

        def ahead():
            sink["ahead"] = yield lax.ppermute(own, "ctx", shifts(n, -2))

        def side():
            sink["beside"] = yield lax.ppermute(own, "ctx", beside_pairs)
            send = jnp.where(odd, sink["behind"], sink["ahead"])
            sink["across"] = yield lax.ppermute(send, "ctx", beside_pairs)

        for stream in (behind(), ahead(), side()):
            beats.start(stream)

    def window_of(own, sink):
        mine = [sink["behind"], sink["beside"], own, sink["across"], sink["ahead"]]
        return mine + [core_swap(block) for block in mine]

    hidden = hidden_in.astype(F32)
    rounded = hidden_in
    sink = {}
    window_streams(rounded, sink)
    saved = []
    weights = []
    vector_block = None
    for layer in range(LAYERS):
        hidden, rounded = watch_until(
            lambda sink=sink, layer=layer: attn_in.ready() and "across" in sink and (layer == 0 or "a1" in arrived),
            hidden, rounded,
        )
        if layer == 0:
            chunks, owners = attn_in.chunks()
            w_attn, vector_block = assemble(chunks, owners, [(per, 0, 0, 4 * half), (16, per // 16, 0, 4 * half)])
            w_attn = w_attn.reshape(width, 4 * half)
        else:
            w_attn = arrived["a1"]
        window = window_of(rounded, sink)
        out_half = w_attn[:, 3 * half :]
        theirs = core_swap(lax.dynamic_slice_in_dim(out_half, (1 - core) * half, half, 0))
        wo = ordered(core, lax.dynamic_slice_in_dim(out_half, core * half, half, 0), theirs, 1)

        block = vector_block[:, layer, :vector_size].astype(F32)
        flat_vectors = [block[:, i * per : (i + 1) * per].reshape(1, -1) for i in range(8)]
        b1 = lax.dynamic_index_in_dim(block[:, 8 * per :].reshape(n, 2, 2, quarter), core, 1, keepdims=False)
        b1 = lax.dynamic_index_in_dim(b1, x, 1, keepdims=False).reshape(1, -1)
        bq, bv = [lax.dynamic_slice_in_dim(v, core * half, half, 1) for v in flat_vectors[:2]]
        bo, g1, c1, b2, g2, c2 = flat_vectors[2:]

        first = attend(window[:SLOTS], w_attn, bq, bv, query_ids, key_ids, need, 0)
        (hidden, w_attn, *first) = watch(hidden, w_attn, *first)
        second = attend(window[SLOTS:], w_attn, bq, bv, query_ids, key_ids, need, 1)
        (hidden, *second) = watch(hidden, *second)
        mixed = jnp.concatenate([first[2], second[2]], axis=0)
        first_sum = hidden + (sum_cores(dot(mixed, wo, NN)) + bo)
        settled = normalize(first_sum, g1, c1)
        settled_low = settled.astype(BF16)
        settled_rows = (both(settled_low), far(settled_low))
        name = "f" + str(layer)
        settled, settled_low = watch_until(lambda name=name: name in arrived, settled, settled_low)
        w_feed = arrived[name]

        def feed_in(rows, w_feed=w_feed, b1=b1):
            inner = dot(rows, w_feed[:, :wide], NN) + b1
            cdf = (1.0 + lax.erf(inner * (0.5**0.5))) * 0.5
            slope = cdf + inner * jnp.exp(-0.5 * inner * inner) * (0.5 / jnp.pi) ** 0.5
            return (inner * cdf).astype(BF16), slope

        act_near, slope_near = feed_in(settled_rows[0])
        act_far, slope_far = feed_in(settled_rows[1])
        partial_far = dot(act_far, w_feed[:, wide:], NN)
        partial_near = dot(act_near, w_feed[:, wide:], NN)
        second_sum = settled + (sum_group(partial_near, partial_far) + b2)
        slope = (slope_near, slope_far)
        activated = (act_near, act_far)
        hidden = normalize(second_sum, g2, c2)
        weights.append((w_attn, wo, w_feed, g1, g2))
        saved.append((window, (first, second), first_sum, settled_rows, slope, activated, second_sum))
        if layer + 1 < LAYERS:
            rounded = hidden.astype(BF16)
            sink = {}
            window_streams(rounded, sink)
    output = hidden.astype(BF16)

    jobs = []

    def step(*state):
        state = beats.beat(*state)
        for job in list(jobs):
            if job[0].ready():
                job[1](job[0].total())
                jobs.remove(job)
        return state

    held = {"feed": None, "attn": None}
    tail_vectors = []

    def shared(low_sum, done):
        mirror = core_swap(low_sum)

        def stream():
            came = yield x_swap(low_sum)
            done([low_sum, came, mirror, core_swap(came)])

        beats.start(stream())

    def feed_done(low_sum, layer):
        def stream():
            mirror = core_swap(low_sum)
            other = yield x_swap(low_sum)
            held["feed"] = finish_feed(layer, held["feed"], [low_sum, other, mirror, core_swap(other)], core, x)
            beats.keep(held, "feed")

        beats.start(stream())

    def attention_done(sums, layer):
        parts = finish_attention(layer, held["attn"], sums, core, per)
        held["attn"] = parts[:4]
        beats.keep(held, "attn")
        tail_vectors.extend(parts[4:])

    vector_grads = [None] * LAYERS
    grad = cotangent.astype(F32)

    def native(value, held_beats, done):
        def stream():
            done((yield Hold(lax.psum_scatter(value, "ctx", scatter_dimension=0, tiled=True), held_beats)))

        beats.start(stream())

    for layer in reversed(range(LAYERS)):
        w_attn, wo, w_feed, g1, g2 = weights[layer]
        window, kept, first_sum, settled_rows, slope, activated, second_sum = saved[layer]
        last = layer == 0
        grad_second, d_g2, d_c2 = normalize_back(second_sum, g2, grad)
        go = grad_second.astype(BF16)
        go_rows = (both(go), far(go))
        d_b2 = column_sums(go)
        gi = [(s * dot(rows, w_feed[:, wide:], NT)).astype(BF16) for s, rows in zip(slope, go_rows)]
        partial_far = dot(gi[1], w_feed[:, :wide], NT)
        partial_near = dot(gi[0], w_feed[:, :wide], NT)
        gset = grad_second + sum_group(partial_near, partial_far)
        d_feed, d_b1 = feed_gradient(settled_rows, gi, activated, go_rows)
        gset, d_feed = step(gset, d_feed)
        native(d_feed, 3 if not last else 5, lambda total, layer=layer: feed_done(total, layer))
        grad_first, d_g1, d_c1 = normalize_back(first_sum, g1, gset)
        gb = grad_first.astype(BF16)
        gb_rows = both(gb)
        d_bo = column_sums(gb)
        grad_first, gb_rows = step(grad_first, gb_rows)
        d_attn, d_wo, d_bq, d_bv, du_own, du_peer = attend_back(
            window, w_attn, wo, kept, gb_rows, query_ids, key_ids, need
        )
        give = lax.dynamic_slice_in_dim(d_wo, (1 - core) * half, half, 1)
        d_attn = with_output_gradient(d_attn, d_wo, core_swap(give), core)
        parts = du_own.astype(F32) + core_swap(du_peer).astype(F32)
        grad_first, d_attn, parts = step(grad_first, d_attn, parts)
        back = {}

        def send(name, value, pairs, back=back):
            def stream():
                back[name] = (yield lax.ppermute(value.astype(BF16), "ctx", pairs)).astype(F32)

            beats.start(stream())

        send("across", parts[3], beside_pairs)
        send("beside", parts[1], beside_pairs)
        vector_grads[layer] = (
            d_bq, d_bv, d_bo[None], d_g1[None], d_c1[None], d_b2[None], d_g2[None], d_c2[None],
            d_b1,
        )
        if last:
            tail = vector_grad_rows(vector_grads, core, x, n)

            def attention_part(t, d_attn=d_attn.reshape(n, per, -1)):
                part = lax.dynamic_index_in_dim(d_attn, t, 0, keepdims=False).astype(F32)
                below = lax.dynamic_index_in_dim(tail, t, 0, keepdims=False)
                return jnp.concatenate([part, below], axis=0)

            def attention_ring_done(total):
                shared(total.astype(BF16), lambda sums: attention_done(sums, 0))

            attention_ring = Scatter(ring, attention_part, 1)
            jobs.append((attention_ring, attention_ring_done))
            beats.start(attention_ring.stream(1))
            beats.start(attention_ring.stream(-1))
        while "across" not in back:
            grad_first, parts, d_attn = step(grad_first, parts, d_attn)
        send("ahead", parts[0] + jnp.where(odd, back["across"], 0.0), shifts(n, -2))
        send("behind", parts[4] + jnp.where(odd, 0.0, back["across"]), shifts(n, 2))
        own_part, d_attn = step(grad_first + parts[2] + back["beside"], d_attn)
        grad = own_part + back["ahead"] + back["behind"]
        if not last:
            native(d_attn, 3, lambda total: shared(total, lambda sums: attention_done(sums, 1)))
    while beats.streams or jobs:
        step()

    fields = tail_vectors[0][:LAYERS, :vector_size]
    own_vectors = [fields[:, i * per : (i + 1) * per] for i in range(8)] + [fields[:, 8 * per :]]
    d_bq, d_bv, d_bo, d_g1, d_c1, d_b2, d_g2, d_c2, d_b1 = own_vectors
    dq, dk, dv, do = held["attn"]
    return (
        output,
        grad.astype(BF16),
        dq, d_bq, dk, dv, d_bv, do, d_bo, d_g1, d_c1, held["feed"][0], d_b1, held["feed"][1], d_b2, d_g2, d_c2,
    )


def solution(mesh):
    tokens = P(("dp", "ctx"), None)
    matrix = P(None, "ctx", None)
    vector = P(None, "ctx")
    params = (
        matrix, vector, matrix, matrix, vector, matrix, vector, vector,
        vector, matrix, vector, matrix, vector, vector, vector,
    )
    return jax.shard_map(
        local,
        mesh=mesh,
        in_specs=(tokens, P("dp", None, None)) + params + (tokens,),
        out_specs=(tokens, tokens) + params,
        check_vma=False,
    )
```

time: 1080 us -> 827 us (0.77)
  local copies, waits for them, and re-layouts: 165 us -> 35.9 us
  Pallas kernels: 84.8 us -> 187 us
  matrix products: 125 us -> 35.4 us
  starting transfers between devices: 176 us -> 87.1 us
  other arithmetic: 114 us -> 76.3 us
    ppermute x84 -> x14, waiting for transfers between devices: 211 us -> 42.6 us  [send(): return lax.ppermute(value, 'ctx', self.cw if sign > 0 else self.ccw)]
    pallas_call x12 -> x21, Pallas kernels: 84.8 us -> 187 us  [the longest x2 75.2 us: attend_back(): pl.pallas_call(kernel, cost_estimate=busy(40), grid_spec=pltpu.PrefetchSc...]
    ppermute x8, waiting for transfers between devices: 20.2 us -> 120 us  [stream(): lax.ppermute(value.astype(BF16), 'ctx', pairs)]
    ppermute x84 -> x14, starting transfers between devices: 123 us -> 27.3 us  [send(): return lax.ppermute(value, 'ctx', self.cw if sign > 0 else self.ccw)]
    dot_general x46 -> x18, matrix products: 125 us -> 35.4 us  [dot(): lax.dot_general(left, right, (dims, ((), ())), preferred_element_type=F32)]
    unnamed x601 -> x166, local copies, waits for them, and re-layouts: 68 us -> 18.6 us
    all_gather x0 -> x3, waiting for transfers between devices: none -> 42.2 us  [native_gathers(): lax.all_gather(pack, 'ctx', axis=0, tiled=True)]
    pallas_call x2 -> x0, local copies, waits for them, and re-layouts: 23.7 us -> none  [attend_back(): pl.pallas_call(kernel, grid_spec=pltpu.PrefetchScalarGridSpec(num_scalar_...]
  transfers between devices with their start and end apart: 153 -> 93, of which waited for: 70 -> 42; matrix products, arithmetic and copies ran while one was open for 27% -> 13% of each run, Pallas kernels for 8% -> 22%
where the time goes in v3:
time: 827 us; the launch traced here: 822 us
  waiting for transfers between devices  384 us (46%)
  Pallas kernels  187 us (23%)
  starting transfers between devices  87.1 us (11%)
  other arithmetic  76.3 us (9%)
  local copies, waits for them, and re-layouts  35.9 us (4%)
  matrix products  35.4 us (4%)
  between operations  16.2 us (2%)
    ppermute x8, waiting for transfers between devices, stream(): lax.ppermute(value.astype(BF16), 'ctx', pairs)  120 us
    ppermute x12, waiting for transfers between devices, x_swap(): return lax.ppermute(value, 'dp', X_PAIRS)  98.8 us
    pallas_call x2, Pallas kernels, attend_back(): pl.pallas_call(kernel, cost_estimate=busy(40), grid_spec=pltpu.PrefetchSc...  75.2 us
    pallas_call x4, Pallas kernels, attend(): pl.pallas_call(kernel, cost_estimate=busy(16), grid_spec=pltpu.PrefetchSc...  54.2 us
    ppermute x14, waiting for transfers between devices, send(): return lax.ppermute(value, 'ctx', self.cw if sign > 0 else self.ccw)  42.6 us
    all_gather x3, waiting for transfers between devices, native_gathers(): lax.all_gather(pack, 'ctx', axis=0, tiled=True)  42.2 us
    dot_general x18, matrix products, dot(): lax.dot_general(left, right, (dims, ((), ())), preferred_element_type=F32)  35.4 us
    ppermute x14, starting transfers between devices, send(): return lax.ppermute(value, 'ctx', self.cw if sign > 0 else self.ccw)  27.3 us
  transfers between devices with their start and end apart: 93, of which 42 were waited for; matrix products, arithmetic and copies ran while one was open for 13% of the time, Pallas kernels for 22%

profile of v3, /device:TPU:0, one launch (start us, length us, event | category | flops | bytes accessed | tf_op | source)
XLA Modules:
  0.0 821.9 jit_solution(18349565510286520187)
XLA Ops:
  25.8 14.2 %collective-permute-done.4.refs_1_ = bf16[256,1024]{1,0:T(8,128)(2,1)S(1)} collective-permute-done((bf16[256,1024]{1,0:T(8,128)(2,1)}, bf16[256,1024]{1,0:T(8,128)(2,1)S(1)}, u32[]{:S(2)}, u32[]{:S(2)}) %collective-permute-start.4) | collective-permute-done | bytes 524320 | tf_op jit(solution)/shard_map/ppermute | solution.py:870
  45.0 20.4 %collective-permute-done.7.refs_3_ = bf16[256,1024]{1,0:T(8,128)(2,1)S(1)} collective-permute-done((bf16[256,1024]{1,0:T(8,128)(2,1)S(1)}, bf16[256,1024]{1,0:T(8,128)(2,1)S(1)}, u32[]{:S(2)}, u32[]{:S(2)}) %collective-permute-start.7) | collective-permute-done | bytes 524320 | tf_op jit(solution)/shard_map/ppermute | solution.py:872
  72.0 12.5 %collective-permute-done.8.refs_2_.refs_10_ = bf16[144,2048]{1,0:T(8,128)(2,1)} collective-permute-done((bf16[144,2048]{1,0:T(8,128)(2,1)}, bf16[144,2048]{1,0:T(8,128)(2,1)}, u32[]{:S(2)}, u32[]{:S(2)}) %collective-permute-start.8) | collective-permute-done | bytes 589856 | tf_op jit(solution)/shard_map/ppermute | solution.py:60
  94.9 12.0 %collective-permute-done.10.refs_1_.refs_9_ = bf16[144,2048]{1,0:T(8,128)(2,1)} collective-permute-done((bf16[144,2048]{1,0:T(8,128)(2,1)}, bf16[144,2048]{1,0:T(8,128)(2,1)}, u32[]{:S(2)}, u32[]{:S(2)}) %collective-permute-start.10) | collective-permute-done | bytes 589856 | tf_op jit(solution)/shard_map/ppermute | solution.py:60
  117.8 11.9 %shard_map.311 = (bf16[256,512]{1,0:T(8,128)(2,1)}, bf16[5,256,1024]{2,1,0:T(8,128)(2,1)}, bf16[256,512]{1,0:T(8,128)(2,1)}, f32[4,1,512]{2,1,0:T(1,128)}) custom-call(s32[10]{0:T(128)} %reshape.304.need_ref, bf16[256,1024]{1,0:T(8,128)(2,1)} %collective-permute-done.2.refs_0_, bf16[256,1024]{1,0:T(8,128)(2,1)} %copy-done.58, bf16[256,1024]{1,0:T(8,128)(2,1)} %refs_2_.7, ...), custom_call_target="tpu_custom_call" | custom-call | flops 17600000000 | bytes 48000000 | tf_op jit(solution)/shard_map/pallas_call | solution.py:348
  131.0 20.8 %all-gather.8.cloned.1.call-done = bf16[1024,2048]{1,0:T(8,128)(2,1)} async-done(((bf16[128,2048]{1,0:T(8,128)(2,1)}), bf16[1024,2048]{1,0:T(8,128)(2,1)}) %all-gather.8.cloned.1.call-update) | async-done | bytes 4194320 | tf_op jit(solution)/shard_map/all_gather | solution.py:830
  151.8 15.1 %shard_map.312 = (bf16[256,512]{1,0:T(8,128)(2,1)}, bf16[5,256,1024]{2,1,0:T(8,128)(2,1)}, bf16[256,512]{1,0:T(8,128)(2,1)}, f32[4,1,512]{2,1,0:T(1,128)}) custom-call(s32[10]{0:T(128)} %reshape.304.need_ref, bf16[256,1024]{1,0:T(8,128)(2,1)} %collective-permute-done.12.refs_0_.refs_5_, bf16[256,1024]{1,0:T(8,128)(2,1)} %collective-permute-done.13.refs_1_.refs_6_, ...), custom_call_target="tpu_custom_call" | custom-call | flops 17600000000 | bytes 48000000 | tf_op jit(solution)/shard_map/pallas_call | solution.py:348
  173.8 12.5 %collective-permute-done.21 = bf16[256,1024]{1,0:T(8,128)(2,1)S(1)} collective-permute-done((bf16[256,1024]{1,0:T(8,128)(2,1)S(1)}, bf16[256,1024]{1,0:T(8,128)(2,1)S(1)}, u32[]{:S(2)}, u32[]{:S(2)}) %collective-permute-start.21) | collective-permute-done | bytes 524320 | tf_op jit(solution)/shard_map/ppermute | solution.py:33
  206.0 12.5 %collective-permute-done.24 = bf16[256,1024]{1,0:T(8,128)(2,1)S(1)} collective-permute-done((bf16[256,1024]{1,0:T(8,128)(2,1)S(1)}, bf16[256,1024]{1,0:T(8,128)(2,1)S(1)}, u32[]{:S(2)}, u32[]{:S(2)}) %collective-permute-start.24) | collective-permute-done | bytes 524320 | tf_op jit(solution)/shard_map/ppermute | solution.py:33
  256.6 11.8 %shard_map.313 = (bf16[256,512]{1,0:T(8,128)(2,1)}, bf16[5,256,1024]{2,1,0:T(8,128)(2,1)}, bf16[256,512]{1,0:T(8,128)(2,1)}, f32[4,1,512]{2,1,0:T(1,128)}) custom-call(s32[10]{0:T(128)} %reshape.304.need_ref, bf16[256,1024]{1,0:T(8,128)(2,1)} %collective-permute-done.25.refs_0_, bf16[256,1024]{1,0:T(8,128)(2,1)} %collective-permute-done.27.refs_1_, ...), custom_call_target="tpu_custom_call" | custom-call | flops 17600000000 | bytes 48000000 | tf_op jit(solution)/shard_map/pallas_call | solution.py:348
  270.6 15.4 %shard_map.314 = (bf16[256,512]{1,0:T(8,128)(2,1)}, bf16[5,256,1024]{2,1,0:T(8,128)(2,1)}, bf16[256,512]{1,0:T(8,128)(2,1)}, f32[4,1,512]{2,1,0:T(1,128)}) custom-call(s32[10]{0:T(128)} %reshape.304.need_ref, bf16[256,1024]{1,0:T(8,128)(2,1)} %collective-permute-done.29.refs_0_.refs_5_, bf16[256,1024]{1,0:T(8,128)(2,1)} %collective-permute-done.30.refs_1_.refs_6_, ...), custom_call_target="tpu_custom_call" | custom-call | flops 17600000000 | bytes 48000000 | tf_op jit(solution)/shard_map/pallas_call | solution.py:348
  286.1 21.4 %all-gather.4.cloned.1.call-done = bf16[1024,2048]{1,0:T(8,128)(2,1)} async-done(((bf16[128,2048]{1,0:T(8,128)(2,1)}), bf16[1024,2048]{1,0:T(8,128)(2,1)}) %all-gather.4.cloned.1.call-update) | async-done | bytes 4194320 | tf_op jit(solution)/shard_map/all_gather | solution.py:830
  314.4 12.5 %collective-permute-done.38 = bf16[256,1024]{1,0:T(8,128)(2,1)S(1)} collective-permute-done((bf16[256,1024]{1,0:T(8,128)(2,1)S(1)}, bf16[256,1024]{1,0:T(8,128)(2,1)S(1)}, u32[]{:S(2)}, u32[]{:S(2)}) %collective-permute-start.38) | collective-permute-done | bytes 524320 | tf_op jit(solution)/shard_map/ppermute | solution.py:33
  337.1 12.5 %collective-permute-done.41 = bf16[256,1024]{1,0:T(8,128)(2,1)S(1)} collective-permute-done((bf16[256,1024]{1,0:T(8,128)(2,1)S(1)}, bf16[256,1024]{1,0:T(8,128)(2,1)S(1)}, u32[]{:S(2)}, u32[]{:S(2)}) %collective-permute-start.41) | collective-permute-done | bytes 524320 | tf_op jit(solution)/shard_map/ppermute | solution.py:33
  354.1 11.7 %collective-permute-done.44 = bf16[256,1024]{1,0:T(8,128)(2,1)S(1)} collective-permute-done((bf16[256,1024]{1,0:T(8,128)(2,1)S(1)}, bf16[256,1024]{1,0:T(8,128)(2,1)S(1)}, u32[]{:S(2)}, u32[]{:S(2)}) %collective-permute-start.44) | collective-permute-done | bytes 524320 | tf_op jit(solution)/shard_map/ppermute | solution.py:33
  405.7 37.4 %shard_map.316 = (bf16[1024,2048]{1,0:T(8,128)(2,1)}, bf16[512,1024]{1,0:T(8,128)(2,1)}, f32[1,512]{1,0:T(1,128)}, f32[1,512]{1,0:T(1,128)}, bf16[5,256,1024]{2,...) custom-call(s32[10]{0:T(128)} %reshape.304.need_ref, bf16[256,1024]{1,0:T(8,128)(2,1)} %collective-permute-done.25.refs_0_, ...), custom_call_target="tpu_custom_call" | custom-call | flops 44000002048 | bytes 120000000 | tf_op jit(solution)/shard_map/pallas_call | solution.py:499
  461.7 18.2 %collective-permute-done.52 = bf16[256,1024]{1,0:T(8,128)(2,1)S(1)} collective-permute-done((bf16[256,1024]{1,0:T(8,128)(2,1)S(1)}, bf16[256,1024]{1,0:T(8,128)(2,1)S(1)}, u32[]{:S(2)}, u32[]{:S(2)}) %collective-permute-start.52) | collective-permute-done | bytes 524320 | tf_op jit(solution)/shard_map/ppermute | solution.py:1023
  480.8 14.8 %collective-permute-done.51 = bf16[256,1024]{1,0:T(8,128)(2,1)} collective-permute-done((bf16[256,1024]{1,0:T(8,128)(2,1)S(1)}, bf16[256,1024]{1,0:T(8,128)(2,1)}, u32[]{:S(2)}, u32[]{:S(2)}) %collective-permute-start.51) | collective-permute-done | bytes 524320 | tf_op jit(solution)/shard_map/ppermute | solution.py:1023
  495.6 12.0 %reduce-scatter.4.cloned.1.call-done.refs_0_ = bf16[128,2048]{1,0:T(8,128)(2,1)} async-done(((bf16[1024,2048]{1,0:T(8,128)(2,1)}), bf16[128,2048]{1,0:T(8,128)(2,1)}) %reduce-scatter.4.cloned.1.call-update) | async-done | bytes 524304 | tf_op jit(solution)/shard_map/reduce_scatter | solution.py:988
  598.9 37.7 %shard_map.319 = (bf16[1024,2048]{1,0:T(8,128)(2,1)}, bf16[512,1024]{1,0:T(8,128)(2,1)}, f32[1,512]{1,0:T(1,128)}, f32[1,512]{1,0:T(1,128)}, bf16[5,256,1024]{2,...) custom-call(s32[10]{0:T(128)} %reshape.304.need_ref, bf16[256,1024]{1,0:T(8,128)(2,1)} %collective-permute-done.2.refs_0_, ...), custom_call_target="tpu_custom_call" | custom-call | flops 44000002048 | bytes 120000000 | tf_op jit(solution)/shard_map/pallas_call | solution.py:499
  669.4 31.5 %collective-permute-done.69 = bf16[256,1024]{1,0:T(8,128)(2,1)S(1)} collective-permute-done((bf16[256,1024]{1,0:T(8,128)(2,1)S(1)}, bf16[256,1024]{1,0:T(8,128)(2,1)S(1)}, u32[]{:S(2)}, u32[]{:S(2)}) %collective-permute-start.69) | collective-permute-done | bytes 524320 | tf_op jit(solution)/shard_map/ppermute | solution.py:1023
  700.9 15.4 %collective-permute-done.68 = bf16[256,1024]{1,0:T(8,128)(2,1)S(1)} collective-permute-done((bf16[256,1024]{1,0:T(8,128)(2,1)S(1)}, bf16[256,1024]{1,0:T(8,128)(2,1)S(1)}, u32[]{:S(2)}, u32[]{:S(2)}) %collective-permute-start.68) | collective-permute-done | bytes 524320 | tf_op jit(solution)/shard_map/ppermute | solution.py:1023
  729.9 21.2 %collective-permute-done.75 = bf16[256,1024]{1,0:T(8,128)(2,1)} collective-permute-done((bf16[256,1024]{1,0:T(8,128)(2,1)}, bf16[256,1024]{1,0:T(8,128)(2,1)}, u32[]{:S(2)}, u32[]{:S(2)}) %collective-permute-start.75) | collective-permute-done | bytes 524320 | tf_op jit(solution)/shard_map/ppermute | solution.py:1023
  756.8 11.9 %collective-permute-done.78 = bf16[144,2048]{1,0:T(8,128)(2,1)} collective-permute-done((bf16[144,2048]{1,0:T(8,128)(2,1)S(1)}, bf16[144,2048]{1,0:T(8,128)(2,1)}, u32[]{:S(2)}, u32[]{:S(2)}) %collective-permute-start.78) | collective-permute-done | bytes 589856 | tf_op jit(solution)/shard_map/ppermute | solution.py:60
  (495 shorter events, 388.1 us)
Async XLA Ops:
  7.2 144.6 %all-gather.8.cloned.1.call-start = ((), (), s32[]{:S(2)}) async-start(), calls=%async_computation.5 | async-start | bytes 4718592 | tf_op jit(solution)/shard_map/all_gather | solution.py:830
  10.8 29.2 %collective-permute-start.1 = (bf16[144,2048]{1,0:T(8,128)(2,1)}, bf16[144,2048]{1,0:T(8,128)(2,1)S(1)}, u32[]{:S(2)}, u32[]{:S(2)}) collective-permute-start(bf16[144,2048]{1,0:T(8,128)(2,1)} %shard_map.308.refs_0_.refs_8_), channel_id=1, source_target_pairs={{2,0},{4,2},{6,4},{7,6},{5,7},{3,5},{1,3},{0,1},{10,8},{12,10},{14... | collective-permute-start | bytes 1769480 | tf_op jit(solution)/shard_map/ppermute | solution.py:60
  13.8 26.3 %collective-permute-start = (bf16[144,2048]{1,0:T(8,128)(2,1)}, bf16[144,2048]{1,0:T(8,128)(2,1)S(1)}, u32[]{:S(2)}, u32[]{:S(2)}) collective-permute-start(bf16[144,2048]{1,0:T(8,128)(2,1)} %shard_map.308.refs_0_.refs_8_), channel_id=1, source_target_pairs={{0,2},{2,4},{4,6},{6,7},{7,5},{5,3},{3,1},{1,0},{8,10},{10,12},{12... | collective-permute-start | bytes 1769480 | tf_op jit(solution)/shard_map/ppermute | solution.py:60
  13.8 26.2 %collective-permute-start.4 = (bf16[256,1024]{1,0:T(8,128)(2,1)}, bf16[256,1024]{1,0:T(8,128)(2,1)S(1)}, u32[]{:S(2)}, u32[]{:S(2)}) collective-permute-start(bf16[256,1024]{1,0:T(8,128)(2,1)} %refs_2_.7), channel_id=1, source_target_pairs={{0,1},{1,0},{2,3},{3,2},{4,5},{5,4},{6,7},{7,6},{8,9},{9,8},{10,11... | collective-permute-start | bytes 1572872 | tf_op jit(solution)/shard_map/ppermute | solution.py:870
  66.1 163.5 %all-gather.6.cloned.1.call-start = ((), (), s32[]{:S(2)}) async-start(), calls=%async_computation.4 | async-start | bytes 4718592 | tf_op jit(solution)/shard_map/all_gather | solution.py:830
  70.4 237.2 %all-gather.4.cloned.1.call-start = ((), (), s32[]{:S(2)}) async-start(), calls=%async_computation.3 | async-start | bytes 4718592 | tf_op jit(solution)/shard_map/all_gather | solution.py:830
  93.8 58.0 %collective-permute-start.12 = (bf16[256,1024]{1,0:T(8,128)(2,1)}, bf16[256,1024]{1,0:T(8,128)(2,1)}, u32[]{:S(2)}, u32[]{:S(2)}) collective-permute-start(bf16[256,1024]{1,0:T(8,128)(2,1)} %collective-permute-done.2.refs_0_), channel_id=1, source_target_pairs={{0,8},{8,0},{16,24},{24,16},{1,9},{9,1},{17,25},{25,17},{2,10},{10... | collective-permute-start | bytes 1572872 | tf_op jit(solution)/shard_map/ppermute | solution.py:29
  93.9 57.9 %collective-permute-start.16 = (bf16[256,1024]{1,0:T(8,128)(2,1)}, bf16[256,1024]{1,0:T(8,128)(2,1)}, u32[]{:S(2)}, u32[]{:S(2)}) collective-permute-start(bf16[256,1024]{1,0:T(8,128)(2,1)} %collective-permute-done.3.refs_4_), channel_id=1, source_target_pairs={{0,8},{8,0},{16,24},{24,16},{1,9},{9,1},{17,25},{25,17},{2,10},{10... | collective-permute-start | bytes 1572872 | tf_op jit(solution)/shard_map/ppermute | solution.py:29
  94.4 57.4 %collective-permute-start.13 = (bf16[256,1024]{1,0:T(8,128)(2,1)}, bf16[256,1024]{1,0:T(8,128)(2,1)}, u32[]{:S(2)}, u32[]{:S(2)}) collective-permute-start(bf16[256,1024]{1,0:T(8,128)(2,1)} %copy-done.58), channel_id=1, source_target_pairs={{0,8},{8,0},{16,24},{24,16},{1,9},{9,1},{17,25},{25,17},{2,10},{10... | collective-permute-start | bytes 1572872 | tf_op jit(solution)/shard_map/ppermute | solution.py:29
  94.4 57.3 %collective-permute-start.15 = (bf16[256,1024]{1,0:T(8,128)(2,1)}, bf16[256,1024]{1,0:T(8,128)(2,1)}, u32[]{:S(2)}, u32[]{:S(2)}) collective-permute-start(bf16[256,1024]{1,0:T(8,128)(2,1)} %copy-done.59), channel_id=1, source_target_pairs={{0,8},{8,0},{16,24},{24,16},{1,9},{9,1},{17,25},{25,17},{2,10},{10... | collective-permute-start | bytes 1572872 | tf_op jit(solution)/shard_map/ppermute | solution.py:29
  117.7 34.1 %collective-permute-start.14 = (bf16[256,1024]{1,0:T(8,128)(2,1)}, bf16[256,1024]{1,0:T(8,128)(2,1)}, u32[]{:S(2)}, u32[]{:S(2)}) collective-permute-start(bf16[256,1024]{1,0:T(8,128)(2,1)} %refs_2_.7), channel_id=1, source_target_pairs={{0,8},{8,0},{16,24},{24,16},{1,9},{9,1},{17,25},{25,17},{2,10},{10... | collective-permute-start | bytes 1572872 | tf_op jit(solution)/shard_map/ppermute | solution.py:29
  200.2 307.4 %reduce-scatter.4.cloned.1.call-start = ((), (), s32[]{:S(2)}) async-start(), calls=%async_computation.6 | async-start | bytes 4718592 | tf_op jit(solution)/shard_map/reduce_scatter | solution.py:988
  401.4 249.6 %reduce-scatter.6.cloned.1.call-start = ((), (), s32[]{:S(2)}) async-start(), calls=%async_computation.7 | async-start | bytes 4718592 | tf_op jit(solution)/shard_map/reduce_scatter | solution.py:988
  461.7 34.0 %collective-permute-start.51 = (bf16[256,1024]{1,0:T(8,128)(2,1)S(1)}, bf16[256,1024]{1,0:T(8,128)(2,1)}, u32[]{:S(2)}, u32[]{:S(2)}) collective-permute-start(bf16[256,1024]{1,0:T(8,128)(2,1)S(1)} %get-tuple-element.383), channel_id=1, source_target_pairs={{0,1},{1,0},{2,3},{3,2},{4,5},{5,4},{6,7},{7,6},{8,9},{9,8},{10,11... | collective-permute-start | bytes 1572872 | tf_op jit(solution)/shard_map/ppermute | solution.py:1023
  536.6 236.6 %reduce-scatter.8.cloned.1.call-start = ((), (), s32[]{:S(2)}) async-start(), calls=%async_computation.8 | async-start | bytes 4718592 | tf_op jit(solution)/shard_map/reduce_scatter | solution.py:988
  656.8 59.5 %collective-permute-start.70 = (bf16[144,2048]{1,0:T(8,128)(2,1)S(1)}, bf16[144,2048]{1,0:T(8,128)(2,1)S(1)}, u32[]{:S(2)}, u32[]{:S(2)}) collective-permute-start(bf16[144,2048]{1,0:T(8,128)(2,1)S(1)} %pad_maximum_fusion.8), channel_id=1, source_target_pairs={{0,2},{2,4},{4,6},{6,7},{7,5},{5,3},{3,1},{1,0},{8,10},{10,12},{12... | collective-permute-start | bytes 1769480 | tf_op jit(solution)/shard_map/ppermute | solution.py:60
  664.7 51.6 %collective-permute-start.71 = (bf16[144,2048]{1,0:T(8,128)(2,1)S(1)}, bf16[144,2048]{1,0:T(8,128)(2,1)S(1)}, u32[]{:S(2)}, u32[]{:S(2)}) collective-permute-start(bf16[144,2048]{1,0:T(8,128)(2,1)S(1)} %pad_maximum_fusion.9), channel_id=1, source_target_pairs={{2,0},{4,2},{6,4},{7,6},{5,7},{3,5},{1,3},{0,1},{10,8},{12,10},{14... | collective-permute-start | bytes 1769480 | tf_op jit(solution)/shard_map/ppermute | solution.py:60
  664.8 36.1 %collective-permute-start.69 = (bf16[256,1024]{1,0:T(8,128)(2,1)S(1)}, bf16[256,1024]{1,0:T(8,128)(2,1)S(1)}, u32[]{:S(2)}, u32[]{:S(2)}) collective-permute-start(bf16[256,1024]{1,0:T(8,128)(2,1)S(1)} %get-tuple-element.380), channel_id=1, source_target_pairs={{0,1},{1,0},{2,3},{3,2},{4,5},{5,4},{6,7},{7,6},{8,9},{9,8},{10,11... | collective-permute-start | bytes 1572872 | tf_op jit(solution)/shard_map/ppermute | solution.py:1023
  668.5 47.7 %collective-permute-start.68 = (bf16[256,1024]{1,0:T(8,128)(2,1)S(1)}, bf16[256,1024]{1,0:T(8,128)(2,1)S(1)}, u32[]{:S(2)}, u32[]{:S(2)}) collective-permute-start(bf16[256,1024]{1,0:T(8,128)(2,1)S(1)} %get-tuple-element.381), channel_id=1, source_target_pairs={{0,1},{1,0},{2,3},{3,2},{4,5},{5,4},{6,7},{7,6},{8,9},{9,8},{10,11... | collective-permute-start | bytes 1572872 | tf_op jit(solution)/shard_map/ppermute | solution.py:1023
  669.3 55.5 %collective-permute-start.76 = (bf16[128,2048]{1,0:T(8,128)(2,1)S(1)}, bf16[128,2048]{1,0:T(8,128)(2,1)S(1)}, u32[]{:S(2)}, u32[]{:S(2)}) collective-permute-start(bf16[128,2048]{1,0:T(8,128)(2,1)S(1)} %copy-done.60), channel_id=1, source_target_pairs={{0,8},{8,0},{16,24},{24,16},{1,9},{9,1},{17,25},{25,17},{2,10},{10... | collective-permute-start | bytes 1572872 | tf_op jit(solution)/shard_map/ppermute | solution.py:29
  717.2 34.7 %collective-permute-start.73 = (bf16[144,2048]{1,0:T(8,128)(2,1)}, bf16[144,2048]{1,0:T(8,128)(2,1)}, u32[]{:S(2)}, u32[]{:S(2)}) collective-permute-start(bf16[144,2048]{1,0:T(8,128)(2,1)} %fusion.56), channel_id=1, source_target_pairs={{2,0},{4,2},{6,4},{7,6},{5,7},{3,5},{1,3},{0,1},{10,8},{12,10},{14... | collective-permute-start | bytes 1769480 | tf_op jit(solution)/shard_map/ppermute | solution.py:60
  720.6 31.3 %collective-permute-start.72 = (bf16[144,2048]{1,0:T(8,128)(2,1)}, bf16[144,2048]{1,0:T(8,128)(2,1)}, u32[]{:S(2)}, u32[]{:S(2)}) collective-permute-start(bf16[144,2048]{1,0:T(8,128)(2,1)} %fusion.55), channel_id=1, source_target_pairs={{0,2},{2,4},{4,6},{6,7},{7,5},{5,3},{3,1},{1,0},{8,10},{10,12},{12... | collective-permute-start | bytes 1769480 | tf_op jit(solution)/shard_map/ppermute | solution.py:60
  722.5 28.6 %collective-permute-start.75 = (bf16[256,1024]{1,0:T(8,128)(2,1)}, bf16[256,1024]{1,0:T(8,128)(2,1)}, u32[]{:S(2)}, u32[]{:S(2)}) collective-permute-start(bf16[256,1024]{1,0:T(8,128)(2,1)} %get-tuple-element.366), channel_id=1, source_target_pairs={{0,2},{1,3},{2,4},{3,5},{4,6},{5,7},{8,10},{9,11},{10,12},{11,13},... | collective-permute-start | bytes 1572872 | tf_op jit(solution)/shard_map/ppermute | solution.py:1023
  725.6 26.3 %collective-permute-start.74 = (bf16[256,1024]{1,0:T(8,128)(2,1)}, bf16[256,1024]{1,0:T(8,128)(2,1)}, u32[]{:S(2)}, u32[]{:S(2)}) collective-permute-start(bf16[256,1024]{1,0:T(8,128)(2,1)} %get-tuple-element.367), channel_id=1, source_target_pairs={{2,0},{3,1},{4,2},{5,3},{6,4},{7,5},{10,8},{11,9},{12,10},{13,11},... | collective-permute-start | bytes 1572872 | tf_op jit(solution)/shard_map/ppermute | solution.py:1023
  (149 other events, 1923.9 us)
Sparse Core Ops, SparseCore 0:
  66.3 85.4 all-gather.7
  154.4 71.6 all-gather.5
  228.8 78.6 all-gather.3
  401.5 106.1 reduce-scatter.3
  535.9 87.1 reduce-scatter.5
  626.6 109.4 reduce-scatter.7
